TPU v7x, 32 devices: a whole 2x2x4 slice. The times are simulated.
32 devices in a mesh: dp: 16 (over z, x, core), tensor: 2 (over y).
Axes of the slice: x: 2, y: 2, z: 4, core: 2. Of those that a mesh axis runs over, the one named last changes fastest.
Arguments:
- tokens: bfloat16 [16384, 1024], P(('dp', 'tensor')), may hold values from -6 to 6
- doc_ids: int32 [16, 1024], P('dp'), may hold values from 0 to 7, never falling along the last dimension, each value on 1 to 512 neighbouring positions
- gain_attn: float32 [1024], replicated, may hold values from 0.25 to 1.75
- w_q: bfloat16 [1024, 1024], P(None, 'tensor'), may hold values from -0.1875 to 0.1875
- w_kv: bfloat16 [1024, 2, 512], P(None, None, 'tensor'), may hold values from -0.1875 to 0.1875
- q_gain: float32 [64], replicated, may hold values from 0.25 to 1.75
- k_gain: float32 [64], replicated, may hold values from 0.25 to 1.75
- w_o: bfloat16 [1024, 1024], P('tensor'), may hold values from -1.5 to 1.5
- gain_ffn: float32 [1024], replicated, may hold values from 0.25 to 1.75
- w_gu: bfloat16 [1024, 2, 4608], P(None, None, 'tensor'), may hold values from -0.1875 to 0.1875
- w_down: bfloat16 [4608, 1024], P('tensor'), may hold values from -0.09375 to 0.09375
- cotangent: bfloat16 [16384, 1024], P(('dp', 'tensor')), may hold values from -6 to 6
Outputs:
- output: bfloat16 [16384, 1024], P(('dp', 'tensor'))
- grad_tokens: float32 [16384, 1024], P(('dp', 'tensor'))
- grad_gain_attn: float32 [1024], replicated
- grad_w_q: float32 [1024, 1024], P('dp', 'tensor')
- grad_w_kv: float32 [1024, 2, 512], P('dp', None, 'tensor')
- grad_q_gain: float32 [64], replicated
- grad_k_gain: float32 [64], replicated
- grad_w_o: float32 [1024, 1024], P('tensor', 'dp')
- grad_gain_ffn: float32 [1024], replicated
- grad_w_gu: float32 [1024, 2, 4608], P('dp', None, 'tensor')
- grad_w_down: float32 [4608, 1024], P('tensor', 'dp')
Inputs may be any that keep to these rules, and one draw needn't show every extreme that they name: In each row of doc_ids the document numbers never fall along the sequence; each document holds 1 to 512 tokens and one holds exactly 512.
All inputs are finite; a program needn't handle non-finite values.
Results may differ from a plain program's by a relative error of at most 0.019.
Values may be sent and summed in bfloat16 or wider, within the bound.
A program may use at most 192 MiB of HBM per device.

v0:
```python
import math

import jax
import jax.numpy as jnp
from jax import lax
from jax.sharding import PartitionSpec as P

EPS = 1e-06
THETA = 1000000.0


def normalize(values):
    inverse = lax.rsqrt(jnp.mean(values * values, axis=-1, keepdims=True) + EPS)
    return (values * inverse, inverse)


def norm_back(grad_normed, normed, inverse):
    return inverse * (grad_normed - normed * jnp.mean(grad_normed * normed, axis=-1, keepdims=True))


def rotate(values, cosine_table, sine_table):
    half_dim = values.shape[-1] // 2
    first_half = values[..., :half_dim]
    second_half = values[..., half_dim:]
    return jnp.concatenate(
        [
            first_half * cosine_table - second_half * sine_table,
            second_half * cosine_table + first_half * sine_table,
        ],
        -1,
    )


def shards(
    tokens, doc_ids, gain_attn, w_q, w_kv, q_gain, k_gain, w_o, gain_ffn, w_gu, w_down, cotangent
):
    f32 = jnp.float32
    bf16 = jnp.bfloat16
    rows_dev, model_width = tokens.shape
    head_dim = q_gain.shape[0]
    q_cols = w_q.shape[1]
    q_heads = q_cols // head_dim
    kv_cols = w_kv.shape[2]
    kv_heads = kv_cols // head_dim
    group_size = q_heads // kv_heads
    hidden = w_gu.shape[2]
    seq_len = doc_ids.shape[1]
    segment = doc_ids[0]
    block_rows = min(512, seq_len)
    blocks = seq_len // block_rows
    score_scale = head_dim ** (-0.5)
    w_kv_flat = w_kv.reshape(model_width, 2 * kv_cols)
    w_gu_flat = w_gu.reshape(model_width, 2 * hidden)
    half_dim = head_dim // 2
    frequency = jnp.exp(-math.log(THETA) * 2.0 * jnp.arange(half_dim, dtype=f32) / head_dim)
    angles = jnp.arange(seq_len, dtype=f32)[:, None] * frequency[None, :]
    cosine_table = jnp.cos(angles)[:, None, :]
    sine_table = jnp.sin(angles)[:, None, :]
    key_pos = jnp.arange(seq_len, dtype=jnp.int32)
    x_float = tokens.astype(f32)
    normed1, inverse1 = normalize(x_float)
    attn_in = (normed1 * gain_attn).astype(bf16)
    attn_all = lax.all_gather(attn_in, "tensor", axis=0, tiled=True)
    q_raw = jnp.dot(attn_all, w_q, preferred_element_type=f32).reshape(seq_len, q_heads, head_dim)
    kv_raw = jnp.dot(attn_all, w_kv_flat, preferred_element_type=f32).reshape(
        seq_len, 2, kv_heads, head_dim
    )
    q_normed, q_inverse = normalize(q_raw)
    k_normed, k_inverse = normalize(kv_raw[:, 0])
    queries = rotate(q_normed * q_gain, cosine_table, sine_table).astype(bf16)
    queries = queries.reshape(seq_len, kv_heads, group_size, head_dim)
    keys = rotate(k_normed * k_gain, cosine_table, sine_table).astype(bf16)
    values_low = kv_raw[:, 1].astype(bf16)

    def scores_of(first_row):
        q_block = lax.dynamic_slice_in_dim(queries, first_row, block_rows, 0)
        seg_block = lax.dynamic_slice_in_dim(segment, first_row, block_rows, 0)
        raw_scores = (
            jnp.einsum("qhgd,thd->hgqt", q_block, keys, preferred_element_type=f32) * score_scale
        )
        query_pos = first_row + jnp.arange(block_rows, dtype=jnp.int32)
        allowed = (key_pos[None, :] <= query_pos[:, None]) & (
            seg_block[:, None] == segment[None, :]
        )
        return (jnp.where(allowed, raw_scores, -1e30), q_block)

    def attend(first_row):
        masked, q_block = scores_of(first_row)
        row_max = jnp.max(masked, axis=-1, keepdims=True)
        exponent = jnp.exp(masked - row_max)
        denominator = jnp.sum(exponent, axis=-1, keepdims=True)
        probs = (exponent / denominator).astype(bf16)
        attended_block = jnp.einsum("hgqt,thd->qhgd", probs, values_low, preferred_element_type=f32)
        return (attended_block, (row_max + jnp.log(denominator))[..., 0])

    starts = jnp.arange(blocks, dtype=jnp.int32) * block_rows
    attended, log_sums = lax.map(attend, starts)
    attended_low = attended.reshape(seq_len, q_cols).astype(bf16)
    resid = x_float + lax.psum_scatter(
        jnp.dot(attended_low, w_o, preferred_element_type=f32),
        "tensor",
        scatter_dimension=0,
        tiled=True,
    )
    normed2, inverse2 = normalize(resid)
    ffn_in = (normed2 * gain_ffn).astype(bf16)
    ffn_all = lax.all_gather(ffn_in, "tensor", axis=0, tiled=True)
    gate_up = jnp.dot(ffn_all, w_gu_flat, preferred_element_type=f32)
    gate_part = gate_up[:, :hidden]
    up_part = gate_up[:, hidden:]
    sigmoid_gate = jax.nn.sigmoid(gate_part)
    silu_gate = gate_part * sigmoid_gate
    mixed = (silu_gate * up_part).astype(bf16)
    result = resid + lax.psum_scatter(
        jnp.dot(mixed, w_down, preferred_element_type=f32).astype(jnp.bfloat16),
        "tensor",
        scatter_dimension=0,
        tiled=True,
    ).astype(jnp.float32)
    output = result.astype(bf16)
    grad_all = lax.all_gather(cotangent, "tensor", axis=0, tiled=True)
    grad_down = jnp.einsum("sf,sd->fd", mixed, grad_all, preferred_element_type=f32)
    grad_mixed = jnp.einsum("sd,fd->sf", grad_all, w_down, preferred_element_type=f32)
    grad_gate = grad_mixed * up_part * sigmoid_gate * (1.0 + gate_part * (1.0 - sigmoid_gate))
    grad_up = grad_mixed * silu_gate
    grad_gu = jnp.concatenate([grad_gate, grad_up], 1).astype(bf16)
    grad_w_gu = jnp.einsum("sd,sf->df", ffn_all, grad_gu, preferred_element_type=f32).reshape(
        model_width, 2, hidden
    )
    grad_ffn_in = lax.psum_scatter(
        jnp.einsum("sf,df->sd", grad_gu, w_gu_flat, preferred_element_type=f32).astype(
            jnp.bfloat16
        ),
        "tensor",
        scatter_dimension=0,
        tiled=True,
    ).astype(jnp.float32)
    gain_ffn_part = jnp.sum(grad_ffn_in * normed2, axis=0)
    grad_resid = cotangent.astype(f32) + norm_back(grad_ffn_in * gain_ffn, normed2, inverse2)
    branch_all = lax.all_gather(grad_resid.astype(bf16), "tensor", axis=0, tiled=True)
    grad_w_o = jnp.einsum("sc,sd->cd", attended_low, branch_all, preferred_element_type=f32)
    grad_attended = jnp.einsum("sd,cd->sc", branch_all, w_o, preferred_element_type=f32).astype(
        bf16
    )
    grad_attended = grad_attended.reshape(seq_len, kv_heads, group_size, head_dim)

    def attend_back(carried, scanned):
        first_row, lse_block = scanned
        masked, q_block = scores_of(first_row)
        probs = jnp.exp(masked - lse_block[..., None])
        go_block = lax.dynamic_slice_in_dim(grad_attended, first_row, block_rows, 0)
        grad_probs = jnp.einsum("qhgd,thd->hgqt", go_block, values_low, preferred_element_type=f32)
        grad_scores = (
            probs * (grad_probs - jnp.sum(probs * grad_probs, axis=-1, keepdims=True))
        ).astype(bf16)
        keys_next = carried[0] + score_scale * jnp.einsum(
            "hgqt,qhgd->thd", grad_scores, q_block, preferred_element_type=f32
        )
        values_next = carried[1] + jnp.einsum(
            "hgqt,qhgd->thd", probs.astype(bf16), go_block, preferred_element_type=f32
        )
        grad_q_block = score_scale * jnp.einsum(
            "hgqt,thd->qhgd", grad_scores, keys, preferred_element_type=f32
        )
        return ((keys_next, values_next), grad_q_block)

    zero_kv = jnp.zeros((seq_len, kv_heads, head_dim), f32)
    (grad_keys, grad_values), grad_queries = lax.scan(
        attend_back, (zero_kv, zero_kv), (starts, log_sums)
    )
    grad_q_normed = rotate(
        grad_queries.reshape(seq_len, q_heads, head_dim), cosine_table, -sine_table
    )
    q_gain_part = jnp.sum(grad_q_normed * q_normed, axis=(0, 1))
    grad_q_raw = (
        norm_back(grad_q_normed * q_gain, q_normed, q_inverse).astype(bf16).reshape(seq_len, q_cols)
    )
    grad_k_normed = rotate(grad_keys, cosine_table, -sine_table)
    k_gain_part = jnp.sum(grad_k_normed * k_normed, axis=(0, 1))
    grad_k_raw = (
        norm_back(grad_k_normed * k_gain, k_normed, k_inverse)
        .astype(bf16)
        .reshape(seq_len, kv_cols)
    )
    grad_kv = jnp.concatenate([grad_k_raw, grad_values.astype(bf16).reshape(seq_len, kv_cols)], 1)
    grad_w_q = jnp.einsum("sd,sc->dc", attn_all, grad_q_raw, preferred_element_type=f32)
    grad_w_kv = jnp.einsum("sd,sc->dc", attn_all, grad_kv, preferred_element_type=f32).reshape(
        model_width, 2, kv_cols
    )
    grad_attn_in = lax.psum_scatter(
        (
            jnp.einsum("sc,dc->sd", grad_q_raw, w_q, preferred_element_type=f32)
            + jnp.einsum("sc,dc->sd", grad_kv, w_kv_flat, preferred_element_type=f32)
        ).astype(jnp.bfloat16),
        "tensor",
        scatter_dimension=0,
        tiled=True,
    ).astype(jnp.float32)
    gain_attn_part = jnp.sum(grad_attn_in * normed1, axis=0)
    grad_tokens = grad_resid + norm_back(grad_attn_in * gain_attn, normed1, inverse1)
    gain_sums = lax.psum(
        (gain_attn_part, gain_ffn_part, q_gain_part, k_gain_part), ("dp", "tensor")
    )
    shard_q, shard_kv, shard_o, shard_gu, shard_down = (
        lax.psum_scatter(
            grad_w_q.astype(jnp.bfloat16), "dp", scatter_dimension=0, tiled=True
        ).astype(jnp.float32),
        lax.psum_scatter(
            grad_w_kv.astype(jnp.bfloat16), "dp", scatter_dimension=0, tiled=True
        ).astype(jnp.float32),
        lax.psum_scatter(
            grad_w_o.astype(jnp.bfloat16), "dp", scatter_dimension=1, tiled=True
        ).astype(jnp.float32),
        lax.psum_scatter(
            grad_w_gu.astype(jnp.bfloat16), "dp", scatter_dimension=0, tiled=True
        ).astype(jnp.float32),
        lax.psum_scatter(
            grad_down.astype(jnp.bfloat16), "dp", scatter_dimension=1, tiled=True
        ).astype(jnp.float32),
    )
    return (
        output,
        grad_tokens,
        gain_sums[0],
        shard_q,
        shard_kv,
        gain_sums[2],
        gain_sums[3],
        shard_o,
        gain_sums[1],
        shard_gu,
        shard_down,
    )


def solution(mesh):
    in_specs = (
        P(("dp", "tensor"), None),
        P("dp", None),
        P(),
        P(None, "tensor"),
        P(None, None, "tensor"),
        P(),
        P(),
        P("tensor", None),
        P(),
        P(None, None, "tensor"),
        P("tensor", None),
        P(("dp", "tensor"), None),
    )
    out_specs = (
        P(("dp", "tensor"), None),
        P(("dp", "tensor"), None),
        P(),
        P("dp", "tensor"),
        P("dp", None, "tensor"),
        P(),
        P(),
        P("tensor", "dp"),
        P(),
        P("dp", None, "tensor"),
        P("tensor", "dp"),
    )
    return jax.shard_map(shards, mesh=mesh, in_specs=in_specs, out_specs=out_specs, check_vma=False)
```

profile of v0, /device:TPU:0, one launch (start us, length us, event | category | flops | bytes accessed | tf_op | source)
XLA Modules:
  0.0 830.4 jit_solution(4698267748066584381)
XLA Ops:
  14.1 33.9 %all-gather.5.cloned.1.call-done = bf16[1024,1024]{1,0:T(8,128)(2,1)} async-done(((bf16[512,1024]{1,0:T(8,128)(2,1)}), bf16[1024,1024]{1,0:T(8,128)(2,1)}) %all-gather.5.cloned.1.call-update) | async-done | bytes 2097168 | tf_op jit(solution)/shard_map/all_gather | solution.py:63
  48.0 2.9 fusion.66
  58.0 37.0 %while.28 = (s32[]{:T(128)}, bf16[2,512,4,2,64]{1,4,3,2,0:T(8,128)(2,1)S(1)}, f32[2,4,2,512]{3,2,1,0:T(2,128)S(1)}, s32[2]{0:T(128)S(1)}, s32[1024]{0:T(1024)S(1...) while((s32[]{:T(128)}, ...), condition=%wide.region_6.7_spmd.clone, body=%wide.region_3.6_spmd.clone.sunk | while | flops 1125642752 | bytes 55195840 | solution.py:97
  61.9 4.6 bitcast_reduce_fusion.2
  66.5 4.3 fusion.136
  70.7 5.8 fusion.137
  80.3 4.6 bitcast_reduce_fusion.2
  84.9 4.3 fusion.136
  89.2 5.8 fusion.137
  97.3 3.3 fusion.85
  100.7 54.4 %reduce-scatter.8.cloned.1.call-done = f32[512,1024]{1,0:T(8,128)} async-done(((f32[1024,1024]{1,0:T(8,128)}), f32[512,1024]{1,0:T(8,128)}) %reduce-scatter.8.cloned.1.call-update) | async-done | bytes 2097168 | tf_op jit(solution)/shard_map/reduce_scatter | solution.py:99
  159.4 9.3 %copy.61 = bf16[128,8,2,2304]{3,1,2,0:T(8,128)(2,1)} copy(bf16[128,8,2,2304]{3,2,1,0:T(2,128)(2,1)} %bitcast.248) | data formatting | bytes 18874368
  168.7 23.3 %all-gather.7.cloned.1.call-done = bf16[1024,1024]{1,0:T(8,128)(2,1)} async-done(((bf16[512,1024]{1,0:T(8,128)(2,1)}), bf16[1024,1024]{1,0:T(8,128)(2,1)}) %all-gather.7.cloned.1.call-update) | async-done | bytes 2097168 | tf_op jit(solution)/shard_map/all_gather | solution.py:107
  192.1 17.0 %fusion.86 = f32[1024,4608]{1,0:T(8,128)} fusion(bf16[1024,1024]{1,0:T(8,128)(2,1)} %all-gather.7.cloned.1.call-done, bf16[1024,4608]{1,0:T(8,128)(2,1)} %bitcast.249), kind=kOutput, calls=%fused_computation.159 | convolution fusion | flops 9663676416 | bytes 30408704 | tf_op jit(solution)/shard_map/dot_general | solution.py:108
  209.1 17.6 %all-gather.9.cloned.1.call-done = bf16[1024,1024]{1,0:T(8,128)(2,1)} async-done(((bf16[512,1024]{1,0:T(8,128)(2,1)}), bf16[1024,1024]{1,0:T(8,128)(2,1)}) %all-gather.9.cloned.1.call-update) | async-done | bytes 2097168 | tf_op jit(solution)/shard_map/all_gather | solution.py:121
  226.7 18.0 %multiply_convert_fusion.1 = (bf16[1024,2304]{1,0:T(8,128)(2,1)}, bf16[1024,2304]{1,0:T(8,128)(2,1)}, bf16[1024,2304]{1,0:T(8,128)(2,1)}) fusion(f32[1024,4608]{1,0:T(8,128)} %fusion.86, bf16[1024,1024]{1,0:T(8,128)(2,1)} %all-gather.9.cloned.1.call-done, bf16[2304,1024]{1,0:T(8,128)(2,1)} %param.26), kind=kOutput, calls=%fused_computation.58 | convolution fusion | flops 4867227648 | bytes 39845888 | tf_op jit(solution)/shard_map/sd,fd->sf/dot_general | solution.py:123
  244.7 16.2 %fusion.70 = bf16[1024,1024]{1,0:T(8,128)(2,1)} fusion(bf16[1024,4608]{1,0:T(8,128)(2,1)} %bitcast.250, bf16[1024,2304]{1,0:T(8,128)(2,1)} %get-tuple-element.260, bf16[1024,2304]{1,0:T(8,128)(2,1)} %get-tuple-element.259), kind=kOutput, calls=%fused_computation.105 | convolution fusion | flops 9683599360 | bytes 20971520 | tf_op jit(solution)/shard_map/sf,df->sd/dot_general | solution.py:131
  261.4 31.5 %reduce-scatter.12.cloned.1.call-done = bf16[512,1024]{1,0:T(8,128)(2,1)} async-done(((bf16[1024,1024]{1,0:T(8,128)(2,1)}), bf16[512,1024]{1,0:T(8,128)(2,1)}) %reduce-scatter.12.cloned.1.call-update) | async-done | bytes 1048592 | tf_op jit(solution)/shard_map/reduce_scatter | solution.py:130
  293.0 2.7 fusion.60
  297.4 9.4 %convolution_convert_fusion.1 = bf16[2304,1024]{0,1:T(8,128)(2,1)} fusion(bf16[1024,2304]{1,0:T(8,128)(2,1)} %get-tuple-element.261, bf16[1024,1024]{1,0:T(8,128)(2,1)} %all-gather.9.cloned.1.call-done), kind=kOutput, calls=%fused_computation.63 | convolution fusion | flops 4834197504 | bytes 11534336 | tf_op jit(solution)/shard_map/sf,sd->fd/dot_general | solution.py:122
  308.8 21.8 %all-gather.11.cloned.1.call-done = bf16[1024,1024]{1,0:T(8,128)(2,1)} async-done(((bf16[512,1024]{1,0:T(8,128)(2,1)}), bf16[1024,1024]{1,0:T(8,128)(2,1)}) %all-gather.11.cloned.1.call-update) | async-done | bytes 2097168 | tf_op jit(solution)/shard_map/all_gather | solution.py:140
  330.6 3.9 convolution_convert_fusion.4
  334.6 3.9 convolution_convert_fusion.6
  338.5 136.8 %while.29 = (s32[]{:T(128)}, f32[1024,4,64]{0,2,1:T(8,128)}, f32[1024,4,64]{0,2,1:T(8,128)}, f32[2,512,4,2,64]{1,0,4,3,2:T(2,128)}, s32[2]{0:T(128)S(1)}, /*inde...) while((s32[]{:T(128)}, f32[1024,4,64]{0,2,1:T(8,128)}, ...), condition=%wide.region_14.15_spmd.clone, body=%wide.region_12.14_spmd.clone.sunk | while | flops 2725245440 | bytes 178092400 | solution.py:168
  343.8 10.4 %fusion.146 = f32[4,512,2,1024]{3,1,2,0:T(8,128)} fusion(bf16[1024,4,64]{0,2,1:T(8,128)(2,1)} %get-tuple-element.495, bf16[1024,4,2,64]{0,3,2,1:T(8,128)(2,1)} %get-tuple-element.494, s32[]{:T(128)S(6)} %select_n.52), kind=kOutput, calls=%fused_computation.41.clone.1 | convolution fusion | flops 536870912 | bytes 17825796 | tf_op jit(solution)/shard_map/while/body/eval_jaxpr/qhgd,thd->hgqt/dot_general | solution.py:152
  354.2 10.8 %fusion.148 = (f32[4,2,512]{2,1,0:T(2,128)}, f32[4,2,512,1024]{3,2,1,0:T(8,128)S(1)}) fusion(f32[4,512,2,1024]{3,1,2,0:T(8,128)} %fusion.146, f32[4,2,512]{2,1,0:T(2,128)} %dynamic-slice_bitcast_fusion.2, bf16[1024,4,64]{0,2,1:T(8,128)(2,1)} %get-tuple-element.492, bf16[1024,4,2,64]{0,3,2,1:T(8,128)(2,1)} %get-tuple-element.489, s32[]{:T(128)S(6)} %select_n.52, ...), kind=kOutput, calls=%fused_computation.24.clone.1 | convolution fusion | flops 557838336 | bytes 35160068 | tf_op jit(solution)/shard_map/while/body/eval_jaxpr/qhgd,thd->hgqt/dot_general | solution.py:79
  365.0 7.4 fusion.149
  372.4 4.3 fusion.151
  379.4 6.3 fusion.152
  386.8 19.5 %dynamic_update_slice.21 = f32[2,512,4,2,64]{1,0,4,3,2:T(2,128)} dynamic-update-slice(f32[2,512,4,2,64]{1,0,4,3,2:T(2,128)} %get-tuple-element.472, f32[1,512,4,2,64]{1,0,4,3,2:T(1,128)S(1)} %copy.63, s32[]{:T(128)S(6)} %copy.80, s32[]{:T(128)} %constant.39.clone.1..sunk.1, s32[]{:T(128)} %constant.39.clone.1..sunk.1, s32[]{:T(128)} %constant.39.clone.1..sunk.1, s32[]{:T(128)} %constant.39.clone.1..sunk.1) | dynamic-update-slice | bytes 2097156 | tf_op jit(solution)/shard_map/while/body/jit(dynamic_update_index_in_dim)/dynamic_update_slice | solution.py:97
  411.5 9.4 %fusion.146 = f32[4,512,2,1024]{3,1,2,0:T(8,128)} fusion(bf16[1024,4,64]{0,2,1:T(8,128)(2,1)} %get-tuple-element.495, bf16[1024,4,2,64]{0,3,2,1:T(8,128)(2,1)} %get-tuple-element.494, s32[]{:T(128)S(6)} %select_n.52), kind=kOutput, calls=%fused_computation.41.clone.1 | convolution fusion | flops 536870912 | bytes 17825796 | tf_op jit(solution)/shard_map/while/body/eval_jaxpr/qhgd,thd->hgqt/dot_general | solution.py:152
  420.9 10.9 %fusion.148 = (f32[4,2,512]{2,1,0:T(2,128)}, f32[4,2,512,1024]{3,2,1,0:T(8,128)S(1)}) fusion(f32[4,512,2,1024]{3,1,2,0:T(8,128)} %fusion.146, f32[4,2,512]{2,1,0:T(2,128)} %dynamic-slice_bitcast_fusion.2, bf16[1024,4,64]{0,2,1:T(8,128)(2,1)} %get-tuple-element.492, bf16[1024,4,2,64]{0,3,2,1:T(8,128)(2,1)} %get-tuple-element.489, s32[]{:T(128)S(6)} %select_n.52, ...), kind=kOutput, calls=%fused_computation.24.clone.1 | convolution fusion | flops 557838336 | bytes 35160068 | tf_op jit(solution)/shard_map/while/body/eval_jaxpr/qhgd,thd->hgqt/dot_general | solution.py:79
  431.8 7.4 fusion.149
  439.2 5.4 fusion.151
  444.6 3.9 fusion.150
  448.5 6.2 fusion.152
  455.7 19.5 %dynamic_update_slice.21 = f32[2,512,4,2,64]{1,0,4,3,2:T(2,128)} dynamic-update-slice(f32[2,512,4,2,64]{1,0,4,3,2:T(2,128)} %get-tuple-element.472, f32[1,512,4,2,64]{1,0,4,3,2:T(1,128)S(1)} %copy.63, s32[]{:T(128)S(6)} %copy.80, s32[]{:T(128)} %constant.39.clone.1..sunk.1, s32[]{:T(128)} %constant.39.clone.1..sunk.1, s32[]{:T(128)} %constant.39.clone.1..sunk.1, s32[]{:T(128)} %constant.39.clone.1..sunk.1) | dynamic-update-slice | bytes 2097156 | tf_op jit(solution)/shard_map/while/body/jit(dynamic_update_index_in_dim)/dynamic_update_slice | solution.py:97
  475.3 4.4 reshape.220
  491.5 2.6 add_convert_fusion
  494.2 9.4 %convolution_convert_fusion.2 = bf16[1024,1024]{1,0:T(8,128)(2,1)} fusion(bf16[1024,2304]{1,0:T(8,128)(2,1)} %get-tuple-element.261, bf16[2304,1024]{1,0:T(8,128)(2,1)} %param.26), kind=kOutput, calls=%fused_computation.106 | convolution fusion | flops 4832886784 | bytes 11534336 | tf_op jit(solution)/shard_map/dot_general | solution.py:115
  503.7 16.8 %convolution_convert_fusion = bf16[1024,4608]{1,0:T(8,128)(2,1)} fusion(bf16[1024,1024]{1,0:T(8,128)(2,1)} %all-gather.7.cloned.1.call-done, bf16[1024,2304]{1,0:T(8,128)(2,1)} %get-tuple-element.260, bf16[1024,2304]{1,0:T(8,128)(2,1)} %get-tuple-element.259), kind=kOutput, calls=%fused_computation.55 | convolution fusion | flops 9687269376 | bytes 20971520 | tf_op jit(solution)/shard_map/sd,sf->df/dot_general | solution.py:127
  520.4 13.1 %convert_element_type.140 = bf16[1024,2,2304]{2,1,0:T(2,128)(2,1)} reshape(bf16[1024,4608]{1,0:T(8,128)(2,1)} %convolution_convert_fusion) | data formatting | bytes 18874368 | tf_op jit(solution)/shard_map/convert_element_type | solution.py:215
  533.5 3.8 convolution_convert_fusion.3
  537.3 3.7 copy.36
  547.8 30.5 %reduce-scatter.14.cloned.1.call-done = bf16[512,1024]{1,0:T(8,128)(2,1)} async-done(((bf16[1024,1024]{1,0:T(8,128)(2,1)}), bf16[512,1024]{1,0:T(8,128)(2,1)}) %reduce-scatter.14.cloned.1.call-update) | async-done | bytes 1048592 | tf_op jit(solution)/shard_map/reduce_scatter | solution.py:190
  580.7 39.8 %all-reduce.2 = (f32[1024]{0:T(1024)}, f32[64]{0:T(128)}, f32[64]{0:T(128)}, f32[1024]{0:T(1024)}) all-reduce(f32[1024]{0:T(1024)S(1)} %get-tuple-element.203, f32[64]{0:T(128)S(1)} %reduce_sum.144, f32[64]{0:T(128)S(1)} %get-tuple-element.199, f32[1024]{0:T(1024)S(1)} %copy-done.43), channel_id=1, replica_groups=mesh['dp'=16,'tensor'=2] {'dp','tensor'}, use_global_device_ids=true, to_apply=%region_20.21 | all-reduce | flops 2176 | bytes 17408 | tf_op jit(solution)/shard_map/psum | solution.py:201
  620.6 4.3 fusion.56
  624.9 194.4 %all-reduce.6.cloned.1.call-done = (bf16[1024,2,256]{2,1,0:T(2,128)(2,1)}, bf16[1024,2,2304]{2,1,0:T(2,128)(2,1)}) async-done(((bf16[1024,2,256]{2,1,0:T(2,128)(2,1)}, bf16[1024,2,2304]{2,1,0:T(2,128)(2,1)}), (bf16[1024,2,256]{2,1,0:T(2,128)(2,1)}, bf16[1024,2,2304]{2,1,0:T(2,128)(2,1)})) %all-reduce.6.cloned.1.call-update) | async-done | bytes 10485776
  (227 shorter events, 63.6 us)
Async XLA Ops:
  7.2 44.8 %copy-start = (bf16[1024,512]{1,0:T(8,128)(2,1)S(1)}, bf16[1024,512]{1,0:T(8,128)(2,1)}, u32[]{:S(2)}) copy-start(bf16[1024,512]{1,0:T(8,128)(2,1)} %param.19) | copy-start | bytes 3145732
  7.2 4.9 copy-start.21
  7.2 40.8 %all-gather.5.cloned.1.call-start = ((), (), s32[]{:S(2)}) async-start(), calls=%async_computation.7 | async-start | bytes 3145728 | tf_op jit(solution)/shard_map/all_gather | solution.py:63
  12.0 143.0 %reduce-scatter.8.cloned.1.call-start = ((), (), s32[]{:S(2)}) async-start(), calls=%async_computation.8 | async-start | bytes 6291456 | tf_op jit(solution)/shard_map/reduce_scatter | solution.py:99
  12.3 38.5 %copy-start.14 = (bf16[128,8,2,256]{3,1,2,0:T(8,128)(2,1)}, bf16[128,8,2,256]{3,1,2,0:T(8,128)(2,1)S(1)}, u32[]{:S(2)}) copy-start(bf16[128,8,2,256]{3,1,2,0:T(8,128)(2,1)S(1)} %copy.59) | copy-start | bytes 3145732
  14.1 42.0 %copy-start.18 = (f32[1024,32]{0,1:T(8,128)}, f32[1024,32]{0,1:T(8,128)S(1)}, u32[]{:S(2)}) copy-start(f32[1024,32]{0,1:T(8,128)S(1)} %get-tuple-element.279) | copy-start | bytes 393220
  50.9 3.9 copy-start.10
  50.9 2.5 copy-start.52
  95.0 2.3 copy-start.25
  100.6 56.7 %copy-start.34 = (f32[1024]{0:T(1024)S(1)}, f32[1024]{0:T(1024)}, u32[]{:S(2)}) copy-start(f32[1024]{0:T(1024)} %param.24) | copy-start | bytes 12292
  100.6 91.4 %all-gather.7.cloned.1.call-start = ((), (), s32[]{:S(2)}) async-start(), calls=%async_computation.9 | async-start | bytes 3145728 | tf_op jit(solution)/shard_map/all_gather | solution.py:107
  157.3 138.4 %copy-start.2 = (f32[512,1024]{1,0:T(8,128)}, f32[512,1024]{1,0:T(8,128)S(1)}, u32[]{:S(2)}) copy-start(f32[512,1024]{1,0:T(8,128)S(1)} %get-tuple-element.254) | copy-start | bytes 6291460
  157.3 138.3 %copy-start.36 = (f32[512]{0:T(512)}, f32[512]{0:T(512)S(1)}, u32[]{:S(2)}) copy-start(f32[512]{0:T(512)S(1)} %add_rsqrt_fusion.2) | copy-start | bytes 6148
  158.8 67.9 %all-gather.9.cloned.1.call-start = ((), (), s32[]{:S(2)}) async-start(), calls=%async_computation.11 | async-start | bytes 3145728 | tf_op jit(solution)/shard_map/all_gather | solution.py:121
  159.4 133.6 %reduce-scatter.12.cloned.1.call-start = ((), (), s32[]{:S(2)}) async-start(), calls=%async_computation.12 | async-start | bytes 3145728 | tf_op jit(solution)/shard_map/reduce_scatter | solution.py:130
  261.0 69.6 %all-gather.11.cloned.1.call-start = ((), (), s32[]{:S(2)}) async-start(), calls=%async_computation.13 | async-start | bytes 3145728 | tf_op jit(solution)/shard_map/all_gather | solution.py:140
  293.0 2.7 copy-start.12
  293.0 2.7 copy-start.13
  297.3 245.6 %reduce-scatter.20.cloned.1.call-start = ((), (), s32[]{:S(2)}) async-start(), calls=%async_computation.17 | async-start | bytes 5013504 | tf_op jit(solution)/shard_map/reduce_scatter | solution.py:217
  306.8 23.8 %copy-start.17 = (bf16[64,8,2,512]{3,1,2,0:T(8,128)(2,1)S(1)}, bf16[64,8,2,512]{3,1,2,0:T(8,128)(2,1)}, u32[]{:S(2)}) copy-start(bf16[64,8,2,512]{3,1,2,0:T(8,128)(2,1)} %copy-done.16) | copy-start | bytes 3145732
  306.8 237.9 %reduce-scatter.18.cloned.1.call-start = ((), (), s32[]{:S(2)}) async-start(), calls=%async_computation.16 | async-start | bytes 1114112 | tf_op jit(solution)/shard_map/reduce_scatter | solution.py:211
  308.8 25.8 %copy-start.26 = (bf16[512,1024]{1,0:T(8,128)(2,1)S(1)}, bf16[512,1024]{1,0:T(8,128)(2,1)}, u32[]{:S(2)}) copy-start(bf16[512,1024]{1,0:T(8,128)(2,1)} %param.23) | copy-start | bytes 3145732
  334.5 211.8 %reduce-scatter.16.cloned.1.call-start = ((), (), s32[]{:S(2)}) async-start(), calls=%async_computation.15 | async-start | bytes 1114112 | tf_op jit(solution)/shard_map/reduce_scatter | solution.py:205
  338.6 5.2 copy-start.32
  372.4 4.4 copy-start.1
  372.4 4.3 copy-start.5
  385.7 20.6 %copy-start.33 = (f32[2,4,2,512]{3,2,1,0:T(2,128)S(1)}, f32[2,4,2,512]{3,2,1,0:T(2,128)}, u32[]{:S(2)}) copy-start(f32[2,4,2,512]{3,2,1,0:T(2,128)} %copy-done.32) | copy-start | bytes 98308 | tf_op jit(solution)/shard_map/while
  406.3 5.1 copy-start.32
  439.2 5.4 copy-start.1
  439.2 5.4 copy-start.5
  454.6 20.6 %copy-start.33 = (f32[2,4,2,512]{3,2,1,0:T(2,128)S(1)}, f32[2,4,2,512]{3,2,1,0:T(2,128)}, u32[]{:S(2)}) copy-start(f32[2,4,2,512]{3,2,1,0:T(2,128)} %copy-done.32) | copy-start | bytes 98308 | tf_op jit(solution)/shard_map/while
  475.2 4.4 copy-start.6
  475.2 4.5 copy-start.19
  475.2 4.5 copy-start.20
  479.8 2.2 copy-start.9
  479.8 2.2 copy-start.29
  479.8 2.2 copy-start.47
  484.5 2.4 copy-start.7
  486.8 91.5 %reduce-scatter.14.cloned.1.call-start = ((), (), s32[]{:S(2)}) async-start(), calls=%async_computation.14 | async-start | bytes 3145728 | tf_op jit(solution)/shard_map/reduce_scatter | solution.py:190
  494.1 126.4 %reduce-scatter.10.cloned.1.call-start = ((), (), s32[]{:S(2)}) async-start(), calls=%async_computation.10 | async-start | bytes 3145728 | tf_op jit(solution)/shard_map/reduce_scatter | solution.py:114
  503.6 315.7 %all-reduce.6.cloned.1.call-start = ((), (), s32[]{:S(2)}) async-start(), calls=%async_computation.18 | async-start | bytes 20971520
  541.0 37.4 %copy-start.38 = (f32[1024]{0:T(1024)S(1)}, f32[1024]{0:T(1024)}, u32[]{:S(2)}) copy-start(f32[1024]{0:T(1024)} %param.18) | copy-start | bytes 12292
  541.0 37.4 %copy-start.40 = (f32[512]{0:T(512)S(1)}, f32[512]{0:T(512)}, u32[]{:S(2)}) copy-start(f32[512]{0:T(512)} %copy-done.39) | copy-start | bytes 6148
  541.0 39.7 %copy-start.43 = (f32[1024]{0:T(1024)S(1)}, f32[1024]{0:T(1024)}, u32[]{:S(2)}) copy-start(f32[1024]{0:T(1024)} %get-tuple-element.201) | copy-start | bytes 12292
  541.0 79.5 %copy-start.3 = (f32[512,1024]{1,0:T(8,128)S(1)}, f32[512,1024]{1,0:T(8,128)}, u32[]{:S(2)}) copy-start(f32[512,1024]{1,0:T(8,128)} %copy-done.2) | copy-start | bytes 6291460
  541.0 79.5 %copy-start.35 = (f32[1024]{0:T(1024)S(1)}, f32[1024]{0:T(1024)}, u32[]{:S(2)}) copy-start(f32[1024]{0:T(1024)} %param.24) | copy-start | bytes 12292
  541.0 79.5 %copy-start.37 = (f32[512]{0:T(512)S(1)}, f32[512]{0:T(512)}, u32[]{:S(2)}) copy-start(f32[512]{0:T(512)} %copy-done.36) | copy-start | bytes 6148
  541.0 79.5 %copy-start.42 = (f32[512]{0:T(512)S(1)}, f32[512]{0:T(512)}, u32[]{:S(2)}) copy-start(f32[512]{0:T(512)} %copy-done.41) | copy-start | bytes 6148
  (24 other events, 28.7 us)
Sparse Core Ops, SparseCore 0:
  12.1 35.8 all-gather.4
  100.7 54.2 reduce-scatter.7
  158.9 33.1 all-gather.6
  193.5 33.1 all-gather.8
  261.1 31.8 reduce-scatter.11
  297.4 33.1 all-gather.10
  334.5 75.5 reduce-scatter.19
  414.1 56.4 reduce-scatter.17
  487.0 57.6 reduce-scatter.15
  547.4 30.9 reduce-scatter.13
  580.6 32.4 reduce-scatter.9
  617.8 201.3 all-reduce.5
where the time goes:
time: 839 us; the launch traced here: 830 us
  waiting for transfers between devices  408 us (49%)
  matrix products  203 us (24%)
  local copies, waits for them, and re-layouts  89.2 us (11%)
  other arithmetic  65.1 us (8%)
  blocking collectives  39.8 us (5%)
  between operations  15.9 us (2%)
    unnamed x13, waiting for transfers between devices  195 us
    reduce_scatter x1, waiting for transfers between devices, shards(): lax.psum_scatter(jnp.dot(attended_low, w_o, preferred_element_type=f32),...  54.4 us
    dynamic_update_slice x4, local copies, waits for them, and re-layouts, shards(): attended, log_sums = lax.map(attend, starts)  41.2 us
    psum x1, blocking collectives, shards(): lax.psum((gain_attn_part, gain_ffn_part, q_gain_part, k_gain_part), ('dp'...  39.8 us
    all_gather x1, waiting for transfers between devices, shards(): attn_all = lax.all_gather(attn_in, 'tensor', axis=0, tiled=True)  33.9 us
    reduce_scatter x1, waiting for transfers between devices, shards(): lax.psum_scatter(jnp.einsum('sf,df->sd', grad_gu, w_gu_flat, preferred_el...  31.5 us
    dot_general x4, matrix products, scores_of(): jnp.einsum('qhgd,thd->hgqt', q_block, keys, preferred_element_type=f32)  30.9 us
    reduce_scatter x1, waiting for transfers between devices, shards(): lax.psum_scatter((jnp.einsum('sc,dc->sd', grad_q_raw, w_q, preferred_elem...  30.5 us
  transfers between devices with their start and end apart: 12, of which 8 were waited for; matrix products, arithmetic and copies ran while one was open for 31% of the time, Pallas kernels for 0%

commit v1 on v0

--- a/solution.py
+++ b/solution.py
@@ -1,12 +1,737 @@
+import functools
 import math
 
 import jax
 import jax.numpy as jnp
 from jax import lax
+from jax.experimental import pallas as pl
+from jax.experimental.pallas import tpu as pltpu
 from jax.sharding import PartitionSpec as P
 
 EPS = 1e-06
 THETA = 1000000.0
+LOG2E = 1.4426950408889634
+LN2 = 0.6931471805599453
+BLOCK = 256
+PAIR = 128
+SAME = 256.0
+F32 = jnp.float32
+BF16 = jnp.bfloat16
+VMEM_LIMIT = 56 * 1024 * 1024
+
+
+def dot_nn(a, b):
+    return lax.dot_general(a, b, (((1,), (0,)), ((), ())), preferred_element_type=F32)
+
+
+def dot_nt(a, b):
+    return lax.dot_general(a, b, (((1,), (1,)), ((), ())), preferred_element_type=F32)
+
+
+def lane_of(shape):
+    return lax.broadcasted_iota(jnp.int32, shape, len(shape) - 1)
+
+
+def head_mean(values):
+    high = values.astype(BF16)
+    low = (values - high.astype(F32)).astype(BF16)
+    row = lax.broadcasted_iota(jnp.int32, (PAIR, PAIR), 0) // 64
+    col = lax.broadcasted_iota(jnp.int32, (PAIR, PAIR), 1) // 64
+    mean = jnp.where(row == col, 1.0 / 64.0, 0.0).astype(BF16)
+    return dot_nn(high, mean) + dot_nn(low, mean)
+
+
+def swap_halves(values):
+    first = lane_of(values.shape) % 64 < 32
+    return jnp.where(first, pltpu.roll(values, 96, 1), pltpu.roll(values, 32, 1))
+
+
+def rope(values, cosine, sine):
+    return values * cosine + swap_halves(values) * sine
+
+
+def row_norm(x):
+    return lax.rsqrt(jnp.mean(x * x, axis=-1, keepdims=True) + EPS)
+
+
+def qkv_kernel(
+    x_ref, gain_ref, wq_ref, wk_ref, wv_ref, qg_ref, kg_ref, cos_ref, sin_ref,
+    attn_ref, q_ref, kd_ref, vd_ref, qraw_ref, kraw_ref,
+):
+    x = x_ref[...].astype(F32)
+    attn = (x * row_norm(x) * gain_ref[...]).astype(BF16)
+    attn_ref[...] = attn
+    q = dot_nn(attn, wq_ref[...])
+    k = dot_nn(attn, wk_ref[...])
+    v = dot_nn(attn, wv_ref[...])
+    qraw_ref[...] = q.astype(BF16)
+    kraw_ref[...] = k.astype(BF16)
+    cosine, sine = cos_ref[...], sin_ref[...]
+    for g in range(q.shape[1] // PAIR):
+        at = slice(g * PAIR, (g + 1) * PAIR)
+        u = q[:, at]
+        n = u * lax.rsqrt(head_mean(u * u) + EPS)
+        q_ref[:, at] = (rope(n * qg_ref[...], cosine, sine) * (LOG2E / 8.0)).astype(BF16)
+    low = lane_of((x.shape[0], PAIR)) < 64
+    for p in range(k.shape[1] // PAIR):
+        at = slice(p * PAIR, (p + 1) * PAIR)
+        u = k[:, at]
+        n = u * lax.rsqrt(head_mean(u * u) + EPS)
+        roped = rope(n * kg_ref[...], cosine, sine)
+        for src, dst in ((roped, kd_ref), (v[:, at], vd_ref)):
+            turned = pltpu.roll(src, 64, 1)
+            dst[:, 2 * p * PAIR : (2 * p + 1) * PAIR] = jnp.where(low, src, turned).astype(BF16)
+            dst[:, (2 * p + 1) * PAIR : (2 * p + 2) * PAIR] = jnp.where(low, turned, src).astype(BF16)
+
+
+def qkv(x, gain, w_q, w_kv, qg, kg, cosine, sine, half):
+    rows, width = x.shape
+    qc, kc = w_q.shape[1], w_kv.shape[1] // 2
+    nb = rows // BLOCK
+    whole = lambda shape, *at: pl.BlockSpec(shape, lambda i: at)
+    row = lambda cols: pl.BlockSpec((BLOCK, cols), lambda i: (i, 0))
+    table = pl.BlockSpec((BLOCK, PAIR), lambda i: (i + half * nb, 0))
+    return pl.pallas_call(
+        qkv_kernel,
+        grid=(nb,),
+        in_specs=[
+            row(width), whole((1, width), 0, 0), whole((width, qc), 0, 0),
+            whole((width, kc), 0, 0), whole((width, kc), 0, 1),
+            whole((1, PAIR), 0, 0), whole((1, PAIR), 0, 0), table, table,
+        ],
+        out_specs=[row(width), row(qc), row(2 * kc), row(2 * kc), row(qc), row(kc)],
+        out_shape=[
+            jax.ShapeDtypeStruct((rows, c), BF16) for c in (width, qc, 2 * kc, 2 * kc, qc, kc)
+        ],
+        compiler_params=pltpu.CompilerParams(vmem_limit_bytes=VMEM_LIMIT),
+        cost_estimate=pl.CostEstimate(
+            flops=2 * rows * width * (qc + 2 * kc), bytes_accessed=10 * rows * width, transcendentals=0
+        ),
+        name="qkv",
+    )(x, gain, w_q, w_kv, w_kv, qg, kg, cosine, sine)
+
+
+def attn_fwd_kernel(
+    s_ref, q_ref, kown_ref, koth_ref, vown_ref, voth_ref, segq_ref, segk_ref,
+    o_ref, linv_ref, kx0, kx1, vx0, vx1, acc,
+):
+    rows = q_ref.shape[0]
+    own = s_ref[0]
+    first = s_ref[1]
+    nb = rows // BLOCK
+    low = lane_of((rows, PAIR)) < 64
+    zero = jnp.zeros((rows, PAIR), BF16)
+
+    @pl.when(pl.program_id(0) == 0)
+    def _():
+        one = jnp.ones((2 * rows, PAIR), F32)
+        both = lane_of((2 * rows, PAIR)) < 64
+        kx0[:, PAIR:] = segk_ref[...]
+        kx1[:, PAIR:] = segk_ref[...]
+        vx0[:, PAIR:] = jnp.where(both, one, 0.0).astype(BF16)
+        vx1[:, PAIR:] = jnp.where(both, 0.0, one).astype(BF16)
+
+    for part, (k_ref, v_ref) in enumerate(((kown_ref, vown_ref), (koth_ref, voth_ref))):
+        at = slice(part * rows, (part + 1) * rows)
+        kx0[at, :PAIR] = jnp.where(low, k_ref[...], zero)
+        kx1[at, :PAIR] = jnp.where(low, zero, k_ref[...])
+        vx0[at, :PAIR] = jnp.where(low, v_ref[...], zero)
+        vx1[at, :PAIR] = jnp.where(low, zero, v_ref[...])
+
+    for i in range(nb):
+        at = slice(i * BLOCK, (i + 1) * BLOCK)
+        q = jnp.concatenate([q_ref[at, :], segq_ref[at, :]], axis=1)
+        block = first + i
+
+        def step(kb, diagonal):
+            here = pl.ds(pl.multiple_of(lax.rem(kb + own, 2 * nb) * BLOCK, BLOCK), BLOCK)
+            total = None
+            for kx, vx in ((kx0, vx0), (kx1, vx1)):
+                s = dot_nt(q, kx[here, :])
+                if diagonal:
+                    r = lax.broadcasted_iota(jnp.int32, s.shape, 0)
+                    s = jnp.where(lane_of(s.shape) <= r, s, -1e30)
+                term = dot_nn(jnp.exp2(s).astype(BF16), vx[here, :])
+                total = term if total is None else total + term
+            return total
+
+        acc[...] = step(block, True)
+
+        def body(kb, carry):
+            acc[...] += step(kb, False)
+            return carry
+
+        lax.fori_loop(s_ref[2 + block], block, body, 0)
+        inverse = 1.0 / acc[:, PAIR:]
+        o_ref[at, :] = (acc[:, :PAIR] * inverse).astype(BF16)
+        linv_ref[at, :] = inverse
+
+
+def attn_fwd(scalars, q, k_own, k_oth, v_own, v_oth, segq, segk, half):
+    rows, qc = q.shape
+    groups = qc // PAIR
+    col = pl.BlockSpec((rows, PAIR), lambda g, s: (0, g))
+    return pl.pallas_call(
+        attn_fwd_kernel,
+        grid_spec=pltpu.PrefetchScalarGridSpec(
+            num_scalar_prefetch=1,
+            grid=(groups,),
+            in_specs=[col] * 5
+            + [
+                pl.BlockSpec((rows, PAIR), lambda g, s: (half, 0)),
+                pl.BlockSpec((2 * rows, PAIR), lambda g, s: (0, 0)),
+            ],
+            out_specs=[col, col],
+            scratch_shapes=[pltpu.VMEM((2 * rows, 2 * PAIR), BF16)] * 4
+            + [pltpu.VMEM((BLOCK, 2 * PAIR), F32)],
+        ),
+        out_shape=[
+            jax.ShapeDtypeStruct((rows, qc), BF16),
+            jax.ShapeDtypeStruct((rows, qc), F32),
+        ],
+        compiler_params=pltpu.CompilerParams(vmem_limit_bytes=VMEM_LIMIT),
+        cost_estimate=pl.CostEstimate(
+            flops=16 * rows * rows * qc, bytes_accessed=12 * rows * qc, transcendentals=0
+        ),
+        name="attn_fwd",
+    )(scalars, q, k_own, k_oth, v_own, v_oth, segq, segk)
+
+
+def attn_bwd_kernel(
+    s_ref, q_own, q_oth, kd_own, kd_oth, vd_own, vd_oth, do_own, do_oth, o_own, o_oth,
+    linv_own, linv_oth, qraw_own, qraw_oth, kraw_own, kraw_oth, segq_ref, segk_ref,
+    cos_ref, sin_ref, qg_ref, kg_ref,
+    gq_own, gq_oth, gk_own, gk_oth, gv_own, gv_oth, qgain_ref, kgain_ref,
+    qx, dox, kx0, kx1, vx0, vx1, kt, dqt, dk0, dk1, dv0, dv1, dks, dvs,
+):
+    rows = q_own.shape[0]
+    own = s_ref[0]
+    nb = rows // BLOCK
+    low = lane_of((rows, PAIR)) < 64
+    zero = jnp.zeros((rows, PAIR), BF16)
+    parts = (
+        (q_own, kd_own, vd_own, do_own, o_own, linv_own),
+        (q_oth, kd_oth, vd_oth, do_oth, o_oth, linv_oth),
+    )
+
+    @pl.when(pl.program_id(0) == 0)
+    def _():
+        one = jnp.ones((2 * rows, PAIR), F32)
+        both = lane_of((2 * rows, PAIR)) < 64
+        qx[:, PAIR:] = segq_ref[...]
+        kx0[:, PAIR:] = segk_ref[...]
+        kx1[:, PAIR:] = segk_ref[...]
+        vx0[:, PAIR:] = jnp.where(both, -one, 0.0).astype(BF16)
+        vx1[:, PAIR:] = jnp.where(both, 0.0, -one).astype(BF16)
+        qgain_ref[...] = jnp.zeros_like(qgain_ref)
+        kgain_ref[...] = jnp.zeros_like(kgain_ref)
+
+    def place(block):
+        return pl.ds(pl.multiple_of(lax.rem(block + own, 2 * nb) * BLOCK, BLOCK), BLOCK)
+
+    for gi in range(2):
+        lanes = slice(gi * PAIR, (gi + 1) * PAIR)
+        for part, (q_ref, k_ref, v_ref, do_ref, o_ref, linv_ref) in enumerate(parts):
+            at = slice(part * rows, (part + 1) * rows)
+            qx[at, :PAIR] = q_ref[:, lanes]
+            k = k_ref[:, lanes]
+            kx0[at, :PAIR] = jnp.where(low, k, zero)
+            kx1[at, :PAIR] = jnp.where(low, zero, k)
+            v = v_ref[:, lanes]
+            vx0[at, :PAIR] = jnp.where(low, v, zero)
+            vx1[at, :PAIR] = jnp.where(low, zero, v)
+            kt[:, at] = jnp.transpose(k.astype(F32))[:64, :].astype(BF16)
+            scaled = do_ref[:, lanes].astype(F32) * linv_ref[:, lanes]
+            dox[at, :PAIR] = scaled.astype(BF16)
+            dox[at, PAIR:] = (scaled * o_ref[:, lanes].astype(F32)).astype(BF16)
+        for ref in (dqt, dk0, dk1, dv0, dv1):
+            ref[...] = jnp.zeros_like(ref)
+
+        def step(qb, kb, diagonal):
+            qs, ks = place(qb), place(kb)
+            q, do = qx[qs, :], dox[qs, :]
+            for h, (kx, vx, dk, dv) in enumerate(((kx0, vx0, dk0, dv0), (kx1, vx1, dk1, dv1))):
+                s = dot_nt(kx[ks, :], q)
+                if diagonal:
+                    r = lax.broadcasted_iota(jnp.int32, s.shape, 0)
+                    s = jnp.where(r <= lane_of(s.shape), s, -1e30)
+                e = jnp.exp2(s)
+                ds = (e * dot_nt(vx[ks, :], do)).astype(BF16)
+                dv[ks, :] += dot_nn(e.astype(BF16), do[:, :PAIR])
+                dk[ks, :] += dot_nn(ds, q[:, :PAIR])
+                dqt[h * 64 : (h + 1) * 64, qs] += dot_nn(kt[:, ks], ds)
+
+        def q_body(qb, carry):
+            step(qb, qb, True)
+
+            def k_body(kb, c):
+                step(qb, kb, False)
+                return c
+
+            lax.fori_loop(s_ref[2 + qb], qb, k_body, 0)
+            return carry
+
+        lax.fori_loop(0, 2 * nb, q_body, 0)
+
+        for part, (g_ref, raw_ref) in enumerate(((gq_own, qraw_own), (gq_oth, qraw_oth))):
+            at = slice(part * rows, (part + 1) * rows)
+            dq = jnp.transpose(dqt[:, at]) * 0.125
+            normed_grad = rope(dq, cos_ref[at, :], -sin_ref[at, :])
+            raw = raw_ref[:, lanes].astype(F32)
+            inverse = lax.rsqrt(head_mean(raw * raw) + EPS)
+            u = raw * inverse
+            qgain_ref[...] += jnp.sum(normed_grad * u, axis=0, keepdims=True)
+            w = normed_grad * qg_ref[...]
+            g_ref[:, lanes] = (inverse * (w - u * head_mean(w * u))).astype(BF16)
+            for a, b, total in ((dk0, dk1, dks), (dv0, dv1, dvs)):
+                both = jnp.where(low, a[at, :], b[at, :])
+                both = both + pltpu.roll(both, 64, 1)
+                if gi == 0:
+                    total[at, :] = both
+                else:
+                    total[at, :] = jnp.where(low, total[at, :], both)
+
+    for part, (gk_ref, gv_ref, raw_ref) in enumerate(
+        ((gk_own, gv_own, kraw_own), (gk_oth, gv_oth, kraw_oth))
+    ):
+        at = slice(part * rows, (part + 1) * rows)
+        normed_grad = rope(dks[at, :] * LN2, cos_ref[at, :], -sin_ref[at, :])
+        raw = raw_ref[...].astype(F32)
+        inverse = lax.rsqrt(head_mean(raw * raw) + EPS)
+        u = raw * inverse
+        kgain_ref[...] += jnp.sum(normed_grad * u, axis=0, keepdims=True)
+        w = normed_grad * kg_ref[...]
+        gk_ref[...] = (inverse * (w - u * head_mean(w * u))).astype(BF16)
+        gv_ref[...] = dvs[at, :].astype(BF16)
+
+
+def attn_bwd(scalars, pairs, segq, segk, cosine, sine, qg, kg):
+    (q, kd, vd, do, o, linv, qraw, kraw) = pairs
+    rows, qc = q[0].shape
+    kc = kraw[0].shape[1]
+    two = pl.BlockSpec((rows, 2 * PAIR), lambda p, s: (0, p))
+    one = pl.BlockSpec((rows, PAIR), lambda p, s: (0, p))
+    table = pl.BlockSpec((2 * rows, PAIR), lambda p, s: (0, 0))
+    gain = pl.BlockSpec((1, PAIR), lambda p, s: (0, 0))
+    operands = [a for pair in (q, kd, vd, do, o, linv, qraw, kraw) for a in pair]
+    return pl.pallas_call(
+        attn_bwd_kernel,
+        grid_spec=pltpu.PrefetchScalarGridSpec(
+            num_scalar_prefetch=1,
+            grid=(qc // (2 * PAIR),),
+            in_specs=[two] * 14 + [one] * 2 + [table] * 4 + [gain] * 2,
+            out_specs=[two] * 2 + [one] * 4 + [gain] * 2,
+            scratch_shapes=[pltpu.VMEM((2 * rows, 2 * PAIR), BF16)] * 6
+            + [pltpu.VMEM((64, 2 * rows), BF16), pltpu.VMEM((PAIR, 2 * rows), F32)]
+            + [pltpu.VMEM((2 * rows, PAIR), F32)] * 6,
+        ),
+        out_shape=[jax.ShapeDtypeStruct((rows, qc), BF16)] * 2
+        + [jax.ShapeDtypeStruct((rows, kc), BF16)] * 4
+        + [jax.ShapeDtypeStruct((1, PAIR), F32)] * 2,
+        compiler_params=pltpu.CompilerParams(vmem_limit_bytes=VMEM_LIMIT),
+        cost_estimate=pl.CostEstimate(
+            flops=80 * rows * rows * qc, bytes_accessed=32 * rows * qc, transcendentals=0
+        ),
+        name="attn_bwd",
+    )(scalars, *operands, segq, segk, cosine, sine, qg, kg)
+
+
+def resid_kernel(mine_ref, theirs_ref, wm_ref, wt_ref, x_ref, gain_ref, resid_ref, ffn_ref):
+    resid = (
+        x_ref[...].astype(F32)
+        + dot_nn(mine_ref[...], wm_ref[...])
+        + dot_nn(theirs_ref[...], wt_ref[...])
+    )
+    resid_ref[...] = resid
+    ffn_ref[...] = (resid * row_norm(resid) * gain_ref[...]).astype(BF16)
+
+
+def resid_norm(mine, theirs, w_mine, w_theirs, x, gain):
+    rows, width = x.shape
+    cols = mine.shape[1]
+    row = lambda c: pl.BlockSpec((BLOCK, c), lambda i: (i, 0))
+    whole = lambda r, c: pl.BlockSpec((r, c), lambda i: (0, 0))
+    return pl.pallas_call(
+        resid_kernel,
+        grid=(rows // BLOCK,),
+        in_specs=[row(cols), row(cols), whole(cols, width), whole(cols, width), row(width), whole(1, width)],
+        out_specs=[row(width), row(width)],
+        out_shape=[jax.ShapeDtypeStruct((rows, width), F32), jax.ShapeDtypeStruct((rows, width), BF16)],
+        compiler_params=pltpu.CompilerParams(vmem_limit_bytes=VMEM_LIMIT),
+        cost_estimate=pl.CostEstimate(
+            flops=4 * rows * width * cols, bytes_accessed=12 * rows * width, transcendentals=0
+        ),
+        name="resid",
+    )(mine, theirs, w_mine, w_theirs, x, gain)
+
+
+def resid_back_kernel(
+    part_ref, recv_ref, resid_ref, cot_ref, gain_ref, wm_ref, wt_ref,
+    gres_ref, branch_ref, mine_ref, theirs_ref, gsum_ref,
+):
+    grad = part_ref[...] + recv_ref[...].astype(F32)
+    resid = resid_ref[...]
+    inverse = row_norm(resid)
+    normed = resid * inverse
+
+    @pl.when(pl.program_id(0) == 0)
+    def _():
+        gsum_ref[...] = jnp.zeros_like(gsum_ref)
+
+    gsum_ref[...] += jnp.sum(grad * normed, axis=0, keepdims=True)
+    w = grad * gain_ref[...]
+    gres = cot_ref[...].astype(F32) + inverse * (w - normed * jnp.mean(w * normed, axis=-1, keepdims=True))
+    gres_ref[...] = gres
+    branch = gres.astype(BF16)
+    branch_ref[...] = branch
+    theirs_ref[...] = dot_nt(branch, wt_ref[...]).astype(BF16)
+    mine_ref[...] = dot_nt(branch, wm_ref[...]).astype(BF16)
+
+
+def resid_back(part, recv, resid, cot, gain, w_mine, w_theirs):
+    rows, width = resid.shape
+    cols = w_mine.shape[0]
+    row = lambda c: pl.BlockSpec((BLOCK, c), lambda i: (i, 0))
+    whole = lambda r, c: pl.BlockSpec((r, c), lambda i: (0, 0))
+    return pl.pallas_call(
+        resid_back_kernel,
+        grid=(rows // BLOCK,),
+        in_specs=[row(width)] * 4 + [whole(1, width), whole(cols, width), whole(cols, width)],
+        out_specs=[row(width), row(width), row(cols), row(cols), whole(1, width)],
+        out_shape=[
+            jax.ShapeDtypeStruct((rows, width), F32), jax.ShapeDtypeStruct((rows, width), BF16),
+            jax.ShapeDtypeStruct((rows, cols), BF16), jax.ShapeDtypeStruct((rows, cols), BF16),
+            jax.ShapeDtypeStruct((1, width), F32),
+        ],
+        compiler_params=pltpu.CompilerParams(vmem_limit_bytes=VMEM_LIMIT),
+        cost_estimate=pl.CostEstimate(
+            flops=4 * rows * width * cols, bytes_accessed=16 * rows * width, transcendentals=0
+        ),
+        name="resid_back",
+    )(part, recv, resid, cot, gain, w_mine, w_theirs)
+
+
+def ffn_kernel(x_ref, c_ref, wg_ref, wu_ref, wd_ref, mixed_ref, gg_ref, gu_ref, y_ref, gf_ref, yacc, gacc):
+    x, c = x_ref[...], c_ref[...]
+    gate = dot_nn(x, wg_ref[...])
+    up = dot_nn(x, wu_ref[...])
+    grad = dot_nt(c, wd_ref[...])
+    sig = 0.5 * jnp.tanh(0.5 * gate) + 0.5
+    silu = gate * sig
+    mixed = (silu * up).astype(BF16)
+    gg = (grad * up * (sig + silu * (1.0 - sig))).astype(BF16)
+    gu = (grad * silu).astype(BF16)
+    mixed_ref[...] = mixed
+    gg_ref[...] = gg
+    gu_ref[...] = gu
+    y = dot_nn(mixed, wd_ref[...])
+    gf = dot_nt(gg, wg_ref[...]) + dot_nt(gu, wu_ref[...])
+    step = pl.program_id(0)
+
+    @pl.when(step == 0)
+    def _():
+        yacc[...] = y
+        gacc[...] = gf
+
+    @pl.when(step > 0)
+    def _():
+        yacc[...] += y
+        gacc[...] += gf
+
+    @pl.when(step == pl.num_programs(0) - 1)
+    def _():
+        y_ref[...] = yacc[...].astype(y_ref.dtype)
+        gf_ref[...] = gacc[...].astype(gf_ref.dtype)
+
+
+def ffn(x, c, w_gu, w_down, dtype):
+    rows, width = x.shape
+    hidden = w_down.shape[0]
+    tile = BLOCK
+    nf = hidden // tile
+    whole = pl.BlockSpec((rows, width), lambda f: (0, 0))
+    mid = pl.BlockSpec((rows, tile), lambda f: (0, f))
+    return pl.pallas_call(
+        ffn_kernel,
+        grid=(nf,),
+        in_specs=[
+            whole, whole,
+            pl.BlockSpec((width, tile), lambda f: (0, f)),
+            pl.BlockSpec((width, tile), lambda f: (0, f + nf)),
+            pl.BlockSpec((tile, width), lambda f: (f, 0)),
+        ],
+        out_specs=[mid, mid, mid, whole, whole],
+        out_shape=[jax.ShapeDtypeStruct((rows, hidden), BF16)] * 3
+        + [jax.ShapeDtypeStruct((rows, width), dtype)] * 2,
+        scratch_shapes=[pltpu.VMEM((rows, width), F32)] * 2,
+        compiler_params=pltpu.CompilerParams(vmem_limit_bytes=VMEM_LIMIT),
+        cost_estimate=pl.CostEstimate(
+            flops=12 * rows * width * hidden, bytes_accessed=6 * width * hidden, transcendentals=0
+        ),
+        name="ffn",
+    )(x, c, w_gu, w_gu, w_down)
+
+
+def grad_kernel(s_ref, xo_ref, xt_ref, yo_ref, yt_ref, send_ref, keep_ref, turned):
+    rows, width = xo_ref.shape
+    mine = s_ref[0]
+
+    @pl.when(pl.program_id(0) == 0)
+    def _():
+        for part, x_ref in enumerate((xo_ref, xt_ref)):
+            for k in range(width // PAIR):
+                piece = jnp.transpose(x_ref[:, k * PAIR : (k + 1) * PAIR].astype(F32)).astype(BF16)
+                for c in range(2):
+                    turned[c, k * 64 : (k + 1) * 64, part * rows : (part + 1) * rows] = piece[
+                        c * 64 : (c + 1) * 64, :
+                    ]
+
+    for which, out_ref in ((1 - mine, send_ref), (mine, keep_ref)):
+        left = turned[which]
+        out_ref[...] = (
+            dot_nn(left[:, :rows], yo_ref[...]) + dot_nn(left[:, rows:], yt_ref[...])
+        ).astype(BF16)
+
+
+def weight_grad(core, x, y, tile):
+    rows, width = x[0].shape
+    cols = y[0].shape[1]
+    whole = pl.BlockSpec((rows, width), lambda f, s: (0, 0))
+    right = pl.BlockSpec((rows, tile), lambda f, s: (0, f))
+    out = pl.BlockSpec((width // 2, tile), lambda f, s: (0, f))
+    return pl.pallas_call(
+        grad_kernel,
+        grid_spec=pltpu.PrefetchScalarGridSpec(
+            num_scalar_prefetch=1,
+            grid=(cols // tile,),
+            in_specs=[whole, whole, right, right],
+            out_specs=[out, out],
+            scratch_shapes=[pltpu.VMEM((2, width // 2, 2 * rows), BF16)],
+        ),
+        out_shape=[jax.ShapeDtypeStruct((width // 2, cols), BF16)] * 2,
+        compiler_params=pltpu.CompilerParams(vmem_limit_bytes=VMEM_LIMIT),
+        cost_estimate=pl.CostEstimate(
+            flops=4 * rows * width * cols, bytes_accessed=6 * rows * cols, transcendentals=0
+        ),
+        name="weight_grad",
+    )(core, x[0], x[1], y[0], y[1])
+
+
+def attn_in_grad_kernel(
+    x_ref, gq_ref, gk_ref, gv_ref, wq_ref, wk_ref, wv_ref, out_ref, gsum_ref
+):
+    out = dot_nt(gq_ref[...], wq_ref[...]) + dot_nt(gk_ref[...], wk_ref[...]) + dot_nt(gv_ref[...], wv_ref[...])
+    out_ref[...] = out.astype(out_ref.dtype)
+    x = x_ref[...].astype(F32)
+
+    @pl.when(pl.program_id(0) == 0)
+    def _():
+        gsum_ref[...] = jnp.zeros_like(gsum_ref)
+
+    gsum_ref[...] += jnp.sum(out * (x * row_norm(x)), axis=0, keepdims=True)
+
+
+def attn_in_grad(x, gq, gk, gv, w_q, w_kv, dtype):
+    rows, width = x.shape
+    qc, kc = gq.shape[1], gk.shape[1]
+    row = lambda c: pl.BlockSpec((BLOCK, c), lambda i: (i, 0))
+    whole = lambda shape, *at: pl.BlockSpec(shape, lambda i: at)
+    return pl.pallas_call(
+        attn_in_grad_kernel,
+        grid=(rows // BLOCK,),
+        in_specs=[
+            row(width), row(qc), row(kc), row(kc),
+            whole((width, qc), 0, 0), whole((width, kc), 0, 0), whole((width, kc), 0, 1),
+        ],
+        out_specs=[row(width), whole((1, width), 0, 0)],
+        out_shape=[jax.ShapeDtypeStruct((rows, width), dtype), jax.ShapeDtypeStruct((1, width), F32)],
+        compiler_params=pltpu.CompilerParams(vmem_limit_bytes=VMEM_LIMIT),
+        cost_estimate=pl.CostEstimate(
+            flops=2 * rows * width * (qc + 2 * kc), bytes_accessed=8 * rows * width, transcendentals=0
+        ),
+        name="attn_in_grad",
+    )(x, gq, gk, gv, w_q, w_kv, w_kv)
+
+
+def final_kernel(part_ref, recv_ref, x_ref, gres_ref, gain_ref, out_ref):
+    x = x_ref[...].astype(F32)
+    inverse = row_norm(x)
+    normed = x * inverse
+    w = (part_ref[...] + recv_ref[...].astype(F32)) * gain_ref[...]
+    out_ref[...] = gres_ref[...] + inverse * (w - normed * jnp.mean(w * normed, axis=-1, keepdims=True))
+
+
+def final(part, recv, x, gres, gain):
+    rows, width = x.shape
+    row = pl.BlockSpec((PAIR, width), lambda i: (i, 0))
+    return pl.pallas_call(
+        final_kernel,
+        grid=(rows // PAIR,),
+        in_specs=[row] * 4 + [pl.BlockSpec((1, width), lambda i: (0, 0))],
+        out_specs=row,
+        out_shape=jax.ShapeDtypeStruct((rows, width), F32),
+        compiler_params=pltpu.CompilerParams(vmem_limit_bytes=VMEM_LIMIT),
+        cost_estimate=pl.CostEstimate(flops=10 * rows * width, bytes_accessed=16 * rows * width, transcendentals=0),
+        name="final",
+    )(part, recv, x, gres, gain)
+
+
+def swap(value, axis, size, bit):
+    return lax.ppermute(value, axis, [(i, i ^ bit) for i in range(size)])
+
+
+def pick(value, axis, index):
+    return lax.dynamic_index_in_dim(value, index, axis, keepdims=False)
+
+
+def scatter_sum(send, keep, position, size, order):
+    received = swap(send, "dp", size, 1)
+    blocks = size // 2
+    cols = keep.shape[-1]
+    rest = [b for b in range(size.bit_length() - 2, 0, -1)]
+    shape = (2,) * len(rest) + (keep.shape[0] // blocks, cols)
+    keep, received = keep.reshape(shape), received.reshape(shape)
+    for bit in order:
+        axis = rest.index(bit)
+        mine = (position >> bit) & 1
+
+        def half(index):
+            total = pick(keep, axis, index).astype(F32) + pick(received, axis, index).astype(F32)
+            return total.astype(BF16)
+
+        going, keep = half(1 - mine), half(mine)
+        received = swap(going, "dp", size, 1 << bit)
+        rest.remove(bit)
+    return keep.astype(F32) + received.astype(F32)
+
+
+def sum_all(value, n_dp, n_tensor):
+    for bit in range(n_dp.bit_length() - 1):
+        value = value + swap(value, "dp", n_dp, 1 << bit)
+    return value + swap(value, "tensor", n_tensor, 1)
+
+
+def after(value, *others):
+    return lax.optimization_barrier((value,) + others)[0]
+
+
+def paired(
+    n_dp, tokens, doc_ids, gain_attn, w_q, w_kv, q_gain, k_gain, w_o, gain_ffn, w_gu, w_down, cotangent
+):
+    rows, width = tokens.shape
+    head_dim = q_gain.shape[0]
+    hidden = w_down.shape[0]
+    seq = doc_ids.shape[1]
+    t = lax.axis_index("tensor")
+    d = lax.axis_index("dp")
+    over = functools.partial(swap, axis="tensor", size=2, bit=1)
+
+    tokens_oth = over(tokens)
+    w_o_oth = over(after(w_o, tokens_oth))
+    cot_oth = over(after(cotangent, tokens_oth))
+
+    segment = doc_ids[0]
+    nb = seq // BLOCK
+    heads_of_blocks = segment.reshape(nb, BLOCK)
+    first_doc, last_doc = heads_of_blocks[:, 0], heads_of_blocks[:, -1]
+    below = jnp.arange(nb)[None, :] < jnp.arange(nb)[:, None]
+    lowest = jnp.sum((below & (last_doc[None, :] < first_doc[:, None])).astype(jnp.int32), axis=1)
+    shift = t * (nb // 2)
+    table = lambda first: jnp.concatenate([jnp.stack([shift, first]).astype(jnp.int32), lowest])
+    scalars_own = table(shift)
+    scalars_oth = table(nb // 2 - shift)
+    segment = jnp.where(t == 0, segment, jnp.roll(segment, rows))
+    lanes = jnp.arange(PAIR, dtype=jnp.int32)[None, :]
+    match = lanes == segment[:, None]
+    marker = lanes == 8
+    segk = (match | marker).astype(BF16)
+    segq = (jnp.where(match, SAME, 0.0) - jnp.where(marker, SAME, 0.0)).astype(BF16)
+    half_dim = head_dim // 2
+    frequency = jnp.exp(-math.log(THETA) * 2.0 * jnp.arange(half_dim, dtype=F32) / head_dim)
+    position = (jnp.arange(seq, dtype=jnp.int32) + t * rows) % seq
+    angles = position.astype(F32)[:, None] * frequency[None, :]
+    cos, sin = jnp.cos(angles), jnp.sin(angles)
+    cosine = jnp.concatenate([cos] * 4, axis=1)
+    sine = jnp.concatenate([-sin, sin] * 2, axis=1)
+    gain1, gain2 = gain_attn.reshape(1, width), gain_ffn.reshape(1, width)
+    qg = jnp.concatenate([q_gain, q_gain]).reshape(1, PAIR)
+    kg = jnp.concatenate([k_gain, k_gain]).reshape(1, PAIR)
+    w_kv = w_kv.reshape(width, -1)
+    w_gu = w_gu.reshape(width, 2 * hidden)
+    core = (d & 1).astype(jnp.int32).reshape(1)
+
+    attn_own, q_own, kd_own, vd_own, qraw_own, kraw_own = qkv(
+        tokens, gain1, w_q, w_kv, qg, kg, cosine, sine, 0
+    )
+    attn_oth, q_oth, kd_oth, vd_oth, qraw_oth, kraw_oth = qkv(
+        tokens_oth, gain1, w_q, w_kv, qg, kg, cosine, sine, 1
+    )
+    o_oth, linv_oth = attn_fwd(scalars_oth, q_oth, kd_own, kd_oth, vd_own, vd_oth, segq, segk, 1)
+    theirs = over(o_oth)
+    o_own, linv_own = attn_fwd(scalars_own, q_own, kd_own, kd_oth, vd_own, vd_oth, segq, segk, 0)
+    resid, ffn_own = resid_norm(o_own, theirs, w_o, w_o_oth, tokens, gain2)
+
+    ffn_oth = over(ffn_own)
+    mixed_own, gg_own, gu_own, y_own, gf_own = ffn(ffn_own, cotangent, w_gu, w_down, F32)
+    mixed_oth, gg_oth, gu_oth, y_oth, gf_oth = ffn(ffn_oth, cot_oth, w_gu, w_down, BF16)
+    gf_recv = over(gf_oth)
+    down = weight_grad(core, (cotangent, cot_oth), (mixed_own, mixed_oth), 768)
+    gate = weight_grad(core, (ffn_own, ffn_oth), (gg_own, gg_oth), 768)
+    up = weight_grad(core, (ffn_own, ffn_oth), (gu_own, gu_oth), 768)
+    gres, branch, do_own, do_send, gain_ffn_part = resid_back(
+        gf_own, gf_recv, resid, cotangent, gain2, w_o, w_o_oth
+    )
+    do_oth = over(do_send)
+    branch_oth = over(after(branch, do_oth))
+    y_recv = over(after(y_oth, branch_oth))
+    output = (resid + y_own + y_recv.astype(F32)).astype(BF16)
+
+    gq_own, gq_oth, gk_own, gk_oth, gv_own, gv_oth, q_gain_part, k_gain_part = attn_bwd(
+        scalars_own,
+        (
+            (q_own, q_oth), (kd_own, kd_oth), (vd_own, vd_oth), (do_own, do_oth), (o_own, o_oth),
+            (linv_own, linv_oth), (qraw_own, qraw_oth), (kraw_own, kraw_oth),
+        ),
+        segq, segk, cosine, sine, qg, kg,
+    )
+    ga_oth, sum_oth = attn_in_grad(tokens_oth, gq_oth, gk_oth, gv_oth, w_q, w_kv, BF16)
+    ga_recv = over(ga_oth)
+    ga_own, sum_own = attn_in_grad(tokens, gq_own, gk_own, gv_own, w_q, w_kv, F32)
+    out_proj = weight_grad(core, (branch, branch_oth), (o_own, o_oth), 512)
+    grad_q = weight_grad(core, (attn_own, attn_oth), (gq_own, gq_oth), 512)
+    grad_k = weight_grad(core, (attn_own, attn_oth), (gk_own, gk_oth), 256)
+    grad_v = weight_grad(core, (attn_own, attn_oth), (gv_own, gv_oth), 256)
+    grad_tokens = final(ga_own, ga_recv, tokens, gres, gain1)
+
+    high = n_dp.bit_length() - 2
+    along = list(range(1, high + 1))
+    turned = along[1:2] + along[:1] + along[2:]
+    shard_down = scatter_sum(*down, d, n_dp, turned)
+    shard_gate = scatter_sum(*gate, d, n_dp, along)
+    shard_up = scatter_sum(*up, d, n_dp, along)
+    shard_o = scatter_sum(*out_proj, d, n_dp, along)
+    shard_q = scatter_sum(*grad_q, d, n_dp, along)
+    shard_k = scatter_sum(*grad_k, d, n_dp, along)
+    shard_v = scatter_sum(*grad_v, d, n_dp, along)
+    gains = jnp.concatenate(
+        [(sum_own + sum_oth).reshape(-1, PAIR), gain_ffn_part.reshape(-1, PAIR), q_gain_part, k_gain_part]
+    )
+    gains = sum_all(gains, n_dp, 2)
+    m = width // PAIR
+    fold = lambda row: row[:head_dim] + row[head_dim:]
+    return (
+        output,
+        grad_tokens,
+        gains[:m].reshape(width),
+        shard_q,
+        jnp.stack([shard_k, shard_v], axis=1),
+        fold(gains[2 * m]),
+        fold(gains[2 * m + 1]),
+        shard_o.T,
+        gains[m : 2 * m].reshape(width),
+        jnp.stack([shard_gate, shard_up], axis=1),
+        shard_down.T,
+    )
 
 
 def normalize(values):
@@ -261,4 +986,6 @@
         P("dp", None, "tensor"),
         P("tensor", "dp"),
     )
-    return jax.shard_map(shards, mesh=mesh, in_specs=in_specs, out_specs=out_specs, check_vma=False)
+    paired_axes = mesh.shape["tensor"] == 2 and mesh.shape["dp"] == 16
+    body = functools.partial(paired, mesh.shape["dp"]) if paired_axes else shards
+    return jax.shard_map(body, mesh=mesh, in_specs=in_specs, out_specs=out_specs, check_vma=False)

time: 839 us -> 424 us (0.51)
  waiting for transfers between devices: 408 us -> 144 us
  matrix products: 203 us -> 0 us
  Pallas kernels: 0 us -> 189 us
  local copies, waits for them, and re-layouts: 89.2 us -> 20.5 us
  blocking collectives: 39.8 us -> 0 us
  other arithmetic: 65.1 us -> 25.8 us
  starting transfers between devices: 0.9 us -> 39.2 us
  between operations: 15.9 us -> 1.44 us
    dot_general x29 -> x0, matrix products: 203 us -> none  [the longest x4 30.9 us: scores_of(): jnp.einsum('qhgd,thd->hgqt', q_block, keys, preferred_element_type=f32)]
    unnamed x13 -> x0, waiting for transfers between devices: 195 us -> none
    pallas_call x0 -> x19, Pallas kernels: none -> 189 us  [the longest x2 50.1 us: ffn(): pl.pallas_call(ffn_kernel, grid=(nf,), in_specs=[whole, whole, pl.BlockSp...]
    ppermute x0 -> x43, waiting for transfers between devices: none -> 144 us  [swap(): return lax.ppermute(value, axis, [(i, i ^ bit) for i in range(size)])]
    reduce_scatter x7 -> x0, waiting for transfers between devices: 116 us -> none  [the longest x1 54.4 us: shards(): lax.psum_scatter(jnp.dot(attended_low, w_o, preferred_element_type=f32),...]
    all_gather x4 -> x0, waiting for transfers between devices: 96.7 us -> none  [the longest x1 33.9 us: shards(): attn_all = lax.all_gather(attn_in, 'tensor', axis=0, tiled=True)]
    dynamic_update_slice x4 -> x0, local copies, waits for them, and re-layouts: 41.2 us -> none  [shards(): attended, log_sums = lax.map(attend, starts)]
    psum x1 -> x0, blocking collectives: 39.8 us -> none  [shards(): lax.psum((gain_attn_part, gain_ffn_part, q_gain_part, k_gain_part), ('dp'...]
  transfers between devices with their start and end apart: 12 -> 43, of which waited for: 8 -> 20; matrix products, arithmetic and copies ran while one was open for 31% -> 10% of each run, Pallas kernels for 0% -> 38%
where the time goes in v1:
time: 424 us; the launch traced here: 421 us
  Pallas kernels  189 us (45%)
  waiting for transfers between devices  144 us (34%)
  starting transfers between devices  39.2 us (9%)
  other arithmetic  25.8 us (6%)
  local copies, waits for them, and re-layouts  20.5 us (5%)
    ppermute x43, waiting for transfers between devices, swap(): return lax.ppermute(value, axis, [(i, i ^ bit) for i in range(size)])  144 us
    pallas_call x2, Pallas kernels, ffn(): pl.pallas_call(ffn_kernel, grid=(nf,), in_specs=[whole, whole, pl.BlockSp...  50.1 us
    pallas_call x7, Pallas kernels, weight_grad(): pl.pallas_call(grad_kernel, grid_spec=pltpu.PrefetchScalarGridSpec(num_sc...  43.7 us
    ppermute x43, starting transfers between devices, swap(): return lax.ppermute(value, axis, [(i, i ^ bit) for i in range(size)])  39.2 us
    pallas_call x1, Pallas kernels, attn_bwd(): pl.pallas_call(attn_bwd_kernel, grid_spec=pltpu.PrefetchScalarGridSpec(nu...  33.8 us
    pallas_call x2, Pallas kernels, attn_fwd(): pl.pallas_call(attn_fwd_kernel, grid_spec=pltpu.PrefetchScalarGridSpec(nu...  23.8 us
    unnamed x71, local copies, waits for them, and re-layouts  19.8 us
    pallas_call x2, Pallas kernels, qkv(): pl.pallas_call(qkv_kernel, grid=(nb,), in_specs=[row(width), whole((1, wi...  12.1 us
  transfers between devices with their start and end apart: 43, of which 20 were waited for; matrix products, arithmetic and copies ran while one was open for 10% of the time, Pallas kernels for 38%

profile of v1, /device:TPU:0, one launch (start us, length us, event | category | flops | bytes accessed | tf_op | source)
XLA Modules:
  0.0 420.6 jit_solution(17934354971283186945)
XLA Ops:
  0.7 3.0 collective-permute-start
  3.7 2.4 copy.208
  11.8 6.2 %qkv.2 = (bf16[512,1024]{1,0:T(8,128)(2,1)}, bf16[512,512]{1,0:T(8,128)(2,1)}, bf16[512,512]{1,0:T(8,128)(2,1)}, bf16[512,512]{1,0:T(8,128)(2,1)}, bf16[512,512]{1,0:T(8,128)(2,1)}, /*index=5*/bf16[512,256]{1,0:T(8,128)(2,1)}) custom-call(bf16[512,1024]{1,0:T(8,128)(2,1)} %x_ref.7, f32[1,1024]{1,0:T(1,128)} %bitcast.306, bf16[1024,512]{1,0:T(8,128)(2,1)} %wq_ref.7, ...), custom_call_target="tpu_custom_call" | custom-call | flops 1073741824 | bytes 5242880 | tf_op jit(solution)/shard_map/qkv/pallas_call | solution.py:94
  19.9 7.2 %collective-permute-done.x_ref = bf16[512,1024]{1,0:T(8,128)(2,1)S(1)} collective-permute-done((bf16[512,1024]{1,0:T(8,128)(2,1)}, bf16[512,1024]{1,0:T(8,128)(2,1)S(1)}, u32[]{:S(2)}, u32[]{:S(2)}) %collective-permute-start) | collective-permute-done | bytes 1048608 | tf_op jit(solution)/shard_map/ppermute | solution.py:580
  29.7 6.0 %qkv.3 = (bf16[512,1024]{1,0:T(8,128)(2,1)}, bf16[512,512]{1,0:T(8,128)(2,1)}, bf16[512,512]{1,0:T(8,128)(2,1)}, bf16[512,512]{1,0:T(8,128)(2,1)}, bf16[512,512]{1,0:T(8,128)(2,1)}, /*index=5*/bf16[512,256]{1,0:T(8,128)(2,1)}) custom-call(bf16[512,1024]{1,0:T(8,128)(2,1)} %copy-done.1, f32[1,1024]{1,0:T(1,128)} %bitcast.307, bf16[1024,512]{1,0:T(8,128)(2,1)} %wq_ref.7, ...), custom_call_target="tpu_custom_call" | custom-call | flops 1073741824 | bytes 5242880 | tf_op jit(solution)/shard_map/qkv/pallas_call | solution.py:94
  35.7 14.0 %attn_fwd.3 = (bf16[512,512]{1,0:T(8,128)(2,1)}, f32[512,512]{1,0:T(8,128)}) custom-call(s32[6]{0:T(128)} %get-tuple-element.195.s_ref, bf16[512,512]{1,0:T(8,128)(2,1)} %get-tuple-element.80.q_ref.q_oth, bf16[512,512]{1,0:T(8,128)(2,1)} %get-tuple-element.75.kown_ref.kd_own, bf16[512,512]{1,0:T(8,128)(2,1)} %get-tuple-element.76.koth_ref.kd_oth, ...), custom_call_target="tpu_custom_call" | custom-call | flops 2147483648 | bytes 3145728 | tf_op jit(solution)/shard_map/attn_fwd/pallas_call | solution.py:174
  49.7 2.0 collective-permute-start.4
  51.7 9.8 %attn_fwd.2 = (bf16[512,512]{1,0:T(8,128)(2,1)}, f32[512,512]{1,0:T(8,128)}) custom-call(s32[6]{0:T(128)} %get-tuple-element.196.s_ref, bf16[512,512]{1,0:T(8,128)(2,1)} %get-tuple-element.74.q_ref.q_own, bf16[512,512]{1,0:T(8,128)(2,1)} %get-tuple-element.75.kown_ref.kd_own, bf16[512,512]{1,0:T(8,128)(2,1)} %get-tuple-element.76.koth_ref.kd_oth, ...), custom_call_target="tpu_custom_call" | custom-call | flops 2147483648 | bytes 3145728 | tf_op jit(solution)/shard_map/attn_fwd/pallas_call | solution.py:174
  61.5 3.2 collective-permute-done.1.theirs_ref
  65.9 4.7 %resid.1 = (f32[512,1024]{1,0:T(8,128)}, bf16[512,1024]{1,0:T(8,128)(2,1)}) custom-call(bf16[512,512]{1,0:T(8,128)(2,1)} %get-tuple-element.79.mine_ref.o_own.yo_ref, bf16[512,512]{1,0:T(8,128)(2,1)} %copy-done.10, bf16[512,1024]{1,0:T(8,128)(2,1)} %wm_ref.3, bf16[512,1024]{1,0:T(8,128)(2,1)} %copy-done.3, bf16[512,1024]{1,0:T(8,128)(2,1)} %x_ref.7, ...), custom_call_target="tpu_custom_call" | custom-call | flops 1073741824 | bytes 6291456 | tf_op jit(solution)/shard_map/resid/pallas_call | solution.py:354
  71.6 9.1 %copy.209 = bf16[128,8,2,2304]{3,1,2,0:T(8,128)(2,1)} copy(bf16[128,8,2,2304]{3,2,1,0:T(2,128)(2,1)} %bitcast.272) | data formatting | bytes 18874368
  80.7 6.7 %collective-permute-done.4.c_ref.xt_ref = bf16[512,1024]{1,0:T(8,128)(2,1)} collective-permute-done((bf16[512,1024]{1,0:T(8,128)(2,1)S(1)}, bf16[512,1024]{1,0:T(8,128)(2,1)}, u32[]{:S(2)}, u32[]{:S(2)}) %collective-permute-start.4) | collective-permute-done | bytes 1048608 | tf_op jit(solution)/shard_map/ppermute | solution.py:580
  87.3 20.2 %collective-permute-done.3.x_ref.xt_ref = bf16[512,1024]{1,0:T(8,128)(2,1)S(1)} collective-permute-done((bf16[512,1024]{1,0:T(8,128)(2,1)}, bf16[512,1024]{1,0:T(8,128)(2,1)S(1)}, u32[]{:S(2)}, u32[]{:S(2)}) %collective-permute-start.3) | collective-permute-done | bytes 1048608 | tf_op jit(solution)/shard_map/ppermute | solution.py:580
  108.5 24.5 %ffn.3 = (bf16[512,2304]{1,0:T(8,128)(2,1)}, bf16[512,2304]{1,0:T(8,128)(2,1)}, bf16[512,2304]{1,0:T(8,128)(2,1)}, bf16[512,1024]{1,0:T(8,128)(2,1)}, bf16[512,1024]{1,0:T(8,128)(2,1)}) custom-call(bf16[512,1024]{1,0:T(8,128)(2,1)} %copy-done.27, bf16[512,1024]{1,0:T(8,128)(2,1)} %collective-permute-done.4.c_ref.xt_ref, bf16[1024,4608]{1,0:T(8,128)(2,1)} %bitcast.273, ...), custom_call_target="tpu_custom_call" | custom-call | flops 14495514624 | bytes 14155776 | tf_op jit(solution)/shard_map/ffn/pallas_call | solution.py:454
  134.5 25.6 %ffn.2 = (bf16[512,2304]{1,0:T(8,128)(2,1)}, bf16[512,2304]{1,0:T(8,128)(2,1)}, bf16[512,2304]{1,0:T(8,128)(2,1)}, f32[512,1024]{1,0:T(8,128)}, f32[512,1024]{1,0:T(8,128)}) custom-call(bf16[512,1024]{1,0:T(8,128)(2,1)} %get-tuple-element.84.x_ref.xo_ref, bf16[512,1024]{1,0:T(8,128)(2,1)} %xo_ref.1, bf16[1024,4608]{1,0:T(8,128)(2,1)} %bitcast.275, ...), custom_call_target="tpu_custom_call" | custom-call | flops 14495514624 | bytes 14155776 | tf_op jit(solution)/shard_map/ffn/pallas_call | solution.py:454
  161.1 6.2 %resid_back.1 = (f32[512,1024]{1,0:T(8,128)}, bf16[512,1024]{1,0:T(8,128)(2,1)}, bf16[512,512]{1,0:T(8,128)(2,1)}, bf16[512,512]{1,0:T(8,128)(2,1)}, f32[1,1024]{1,0:T(1,128)}) custom-call(f32[512,1024]{1,0:T(8,128)} %get-tuple-element.88.part_ref, bf16[512,1024]{1,0:T(8,128)(2,1)} %copy-done.9, f32[512,1024]{1,0:T(8,128)} %get-tuple-element.83.resid_ref, ...), custom_call_target="tpu_custom_call" | custom-call | flops 1073741824 | bytes 8388608 | tf_op jit(solution)/shard_map/resid_back/pallas_call | solution.py:396
  168.0 9.1 %weight_grad.13 = (bf16[512,2304]{1,0:T(8,128)(2,1)}, bf16[512,2304]{1,0:T(8,128)(2,1)}) custom-call(s32[1]{0:T(128)} %bitcast.14.s_ref, bf16[512,1024]{1,0:T(8,128)(2,1)} %xo_ref.1, bf16[512,1024]{1,0:T(8,128)(2,1)} %collective-permute-done.4.c_ref.xt_ref, bf16[512,2304]{1,0:T(8,128)(2,1)} %get-tuple-element.133.yo_ref, ...), custom_call_target="tpu_custom_call" | custom-call | flops 4831838208 | bytes 7077888 | tf_op jit(solution)/shard_map/weight_grad/pallas_call | solution.py:502
  177.1 2.9 collective-permute-done.6.do_oth
  180.8 33.8 %attn_bwd.1 = (bf16[512,512]{1,0:T(8,128)(2,1)}, bf16[512,512]{1,0:T(8,128)(2,1)}, bf16[512,256]{1,0:T(8,128)(2,1)}, bf16[512,256]{1,0:T(8,128)(2,1)}, bf16[512,...) custom-call(s32[6]{0:T(128)} %get-tuple-element.196.s_ref, ...), custom_call_target="tpu_custom_call" | custom-call | flops 10737418240 | bytes 8388608 | tf_op jit(solution)/shard_map/attn_bwd/pallas_call | solution.py:317
  214.6 5.0 %attn_in_grad.2 = (f32[512,1024]{1,0:T(8,128)}, f32[1,1024]{1,0:T(1,128)}) custom-call(bf16[512,1024]{1,0:T(8,128)(2,1)} %x_ref.7, bf16[512,512]{1,0:T(8,128)(2,1)} %get-tuple-element.101.gq_ref.yo_ref, bf16[512,256]{1,0:T(8,128)(2,1)} %get-tuple-element.102.gk_ref.yo_ref, bf16[512,256]{1,0:T(8,128)(2,1)} %get-tuple-element.103.gv_ref.yo_ref, ...), custom_call_target="tpu_custom_call" | custom-call | flops 1073741824 | bytes 4194304 | tf_op jit(solution)/shard_map/attn_in_grad/pallas_call | solution.py:539
  219.6 4.7 %attn_in_grad.3 = (bf16[512,1024]{1,0:T(8,128)(2,1)}, f32[1,1024]{1,0:T(1,128)}) custom-call(bf16[512,1024]{1,0:T(8,128)(2,1)} %copy-done.1, bf16[512,512]{1,0:T(8,128)(2,1)} %get-tuple-element.105.gq_ref.yt_ref, bf16[512,256]{1,0:T(8,128)(2,1)} %get-tuple-element.106.gk_ref.yt_ref, bf16[512,256]{1,0:T(8,128)(2,1)} %get-tuple-element.107.gv_ref.yt_ref, ...), custom_call_target="tpu_custom_call" | custom-call | flops 1073741824 | bytes 4194304 | tf_op jit(solution)/shard_map/attn_in_grad/pallas_call | solution.py:539
  225.1 9.1 %weight_grad.11 = (bf16[512,2304]{1,0:T(8,128)(2,1)}, bf16[512,2304]{1,0:T(8,128)(2,1)}) custom-call(s32[1]{0:T(128)} %bitcast.14.s_ref, bf16[512,1024]{1,0:T(8,128)(2,1)} %get-tuple-element.84.x_ref.xo_ref, bf16[512,1024]{1,0:T(8,128)(2,1)} %copy-done.27, bf16[512,2304]{1,0:T(8,128)(2,1)} %get-tuple-element.125.yo_ref, ...), custom_call_target="tpu_custom_call" | custom-call | flops 4831838208 | bytes 7077888 | tf_op jit(solution)/shard_map/weight_grad/pallas_call | solution.py:502
  235.5 9.0 %weight_grad.12 = (bf16[512,2304]{1,0:T(8,128)(2,1)}, bf16[512,2304]{1,0:T(8,128)(2,1)}) custom-call(s32[1]{0:T(128)} %bitcast.14.s_ref, bf16[512,1024]{1,0:T(8,128)(2,1)} %get-tuple-element.84.x_ref.xo_ref, bf16[512,1024]{1,0:T(8,128)(2,1)} %copy-done.27, bf16[512,2304]{1,0:T(8,128)(2,1)} %get-tuple-element.129.yo_ref, ...), custom_call_target="tpu_custom_call" | custom-call | flops 4831838208 | bytes 7077888 | tf_op jit(solution)/shard_map/weight_grad/pallas_call | solution.py:502
  244.5 2.4 collective-permute-start.12
  246.9 4.5 %weight_grad.7 = (bf16[512,512]{1,0:T(8,128)(2,1)}, bf16[512,512]{1,0:T(8,128)(2,1)}) custom-call(s32[1]{0:T(128)} %bitcast.14.s_ref, bf16[512,1024]{1,0:T(8,128)(2,1)} %get-tuple-element.115.xo_ref, bf16[512,1024]{1,0:T(8,128)(2,1)} %get-tuple-element.116.xt_ref, bf16[512,512]{1,0:T(8,128)(2,1)} %get-tuple-element.101.gq_ref.yo_ref, ...), custom_call_target="tpu_custom_call" | custom-call | flops 1073741824 | bytes 1572864 | tf_op jit(solution)/shard_map/weight_grad/pallas_call | solution.py:502
  251.4 2.7 collective-permute-start.13
  254.1 3.8 weight_grad.8
  258.3 3.8 weight_grad.9
  267.1 3.3 collective-permute-done.20
  272.4 4.2 %collective-permute-done.21 = bf16[2,64,256]{2,1,0:T(8,128)(2,1)S(1)} collective-permute-done((bf16[2,64,256]{2,1,0:T(8,128)(2,1)S(1)}, bf16[2,64,256]{2,1,0:T(8,128)(2,1)S(1)}, u32[]{:S(2)}, u32[]{:S(2)}) %collective-permute-start.21) | collective-permute-done | bytes 65568 | tf_op jit(solution)/shard_map/ppermute | solution.py:580
  276.6 4.2 %collective-permute-done.25 = bf16[2,64,256]{2,1,0:T(8,128)(2,1)S(1)} collective-permute-done((bf16[2,64,256]{2,1,0:T(8,128)(2,1)S(1)}, bf16[2,64,256]{2,1,0:T(8,128)(2,1)S(1)}, u32[]{:S(2)}, u32[]{:S(2)}) %collective-permute-start.25) | collective-permute-done | bytes 65568 | tf_op jit(solution)/shard_map/ppermute | solution.py:580
  281.8 3.9 collective-permute-done.22
  285.7 2.2 collective-permute-start.7
  288.5 4.3 %collective-permute-done.26 = bf16[64,256]{1,0:T(8,128)(2,1)S(1)} collective-permute-done((bf16[64,256]{1,0:T(8,128)(2,1)S(1)}, bf16[64,256]{1,0:T(8,128)(2,1)S(1)}, u32[]{:S(2)}, u32[]{:S(2)}) %collective-permute-start.26) | collective-permute-done | bytes 32800 | tf_op jit(solution)/shard_map/ppermute | solution.py:580
  294.4 4.7 %collective-permute-done.16 = bf16[2,2,64,512]{3,2,1,0:T(8,128)(2,1)S(1)} collective-permute-done((bf16[2,2,64,512]{3,2,1,0:T(8,128)(2,1)S(1)}, bf16[2,2,64,512]{3,2,1,0:T(8,128)(2,1)S(1)}, u32[]{:S(2)}, u32[]{:S(2)}) %collective-permute-start.16) | collective-permute-done | bytes 262176 | tf_op jit(solution)/shard_map/ppermute | solution.py:580
  301.6 2.0 collective-permute-start.40
  305.3 6.6 %collective-permute-done.7.xt_ref = bf16[512,1024]{1,0:T(8,128)(2,1)S(1)} collective-permute-done((bf16[512,1024]{1,0:T(8,128)(2,1)S(1)}, bf16[512,1024]{1,0:T(8,128)(2,1)S(1)}, u32[]{:S(2)}, u32[]{:S(2)}) %collective-permute-start.7) | collective-permute-done | bytes 1048608 | tf_op jit(solution)/shard_map/ppermute | solution.py:580
  313.7 4.5 %weight_grad.10 = (bf16[512,512]{1,0:T(8,128)(2,1)}, bf16[512,512]{1,0:T(8,128)(2,1)}) custom-call(s32[1]{0:T(128)} %bitcast.14.s_ref, bf16[512,1024]{1,0:T(8,128)(2,1)} %get-tuple-element.92.xo_ref, bf16[512,1024]{1,0:T(8,128)(2,1)} %copy-done.28, bf16[512,512]{1,0:T(8,128)(2,1)} %get-tuple-element.79.mine_ref.o_own.yo_ref, ...), custom_call_target="tpu_custom_call" | custom-call | flops 1073741824 | bytes 1572864 | tf_op jit(solution)/shard_map/weight_grad/pallas_call | solution.py:502
  322.9 4.9 %collective-permute-done.18 = bf16[64,512]{1,0:T(8,128)(2,1)S(1)} collective-permute-done((bf16[64,512]{1,0:T(8,128)(2,1)S(1)}, bf16[64,512]{1,0:T(8,128)(2,1)S(1)}, u32[]{:S(2)}, u32[]{:S(2)}) %collective-permute-start.18) | collective-permute-done | bytes 65568 | tf_op jit(solution)/shard_map/ppermute | solution.py:580
  330.3 2.0 collective-permute-start.8
  332.3 5.3 %final.1 = f32[512,1024]{1,0:T(8,128)} custom-call(f32[512,1024]{1,0:T(8,128)} %get-tuple-element.104.part_ref, bf16[512,1024]{1,0:T(8,128)(2,1)} %collective-permute-done.9.recv_ref, bf16[512,1024]{1,0:T(8,128)(2,1)} %x_ref.7, f32[512,1024]{1,0:T(8,128)} %get-tuple-element.109.gres_ref, f32[1,1024]{1,0:T(1,128)} %bitcast.308), custom_call_target="tpu_custom_call" | custom-call | flops 5242880 | bytes 8388608 | tf_op jit(solution)/shard_map/final/pallas_call | solution.py:567
  337.7 26.7 %collective-permute-done.28 = bf16[2,2,64,512]{3,2,1,0:T(8,128)(2,1)S(1)} collective-permute-done((bf16[2,2,64,512]{3,2,1,0:T(8,128)(2,1)S(1)}, bf16[2,2,64,512]{3,2,1,0:T(8,128)(2,1)S(1)}, u32[]{:S(2)}, u32[]{:S(2)}) %collective-permute-start.28) | collective-permute-done | bytes 262176 | tf_op jit(solution)/shard_map/ppermute | solution.py:580
  367.9 2.1 collective-permute-start.33
  371.8 13.3 %collective-permute-done.30 = bf16[64,512]{1,0:T(8,128)(2,1)S(1)} collective-permute-done((bf16[64,512]{1,0:T(8,128)(2,1)S(1)}, bf16[64,512]{1,0:T(8,128)(2,1)S(1)}, u32[]{:S(2)}, u32[]{:S(2)}) %collective-permute-start.30) | collective-permute-done | bytes 65568 | tf_op jit(solution)/shard_map/ppermute | solution.py:580
  387.5 3.4 collective-permute-start.42
  391.2 8.4 %collective-permute-done.37 = bf16[2,64,2304]{2,1,0:T(8,128)(2,1)S(1)} collective-permute-done((bf16[2,64,2304]{2,1,0:T(8,128)(2,1)S(1)}, bf16[2,64,2304]{2,1,0:T(8,128)(2,1)S(1)}, u32[]{:S(2)}, u32[]{:S(2)}) %collective-permute-start.37) | collective-permute-done | bytes 589856 | tf_op jit(solution)/shard_map/ppermute | solution.py:580
  400.7 13.5 %collective-permute-done.34 = bf16[64,2304]{1,0:T(8,128)(2,1)S(1)} collective-permute-done((bf16[64,2304]{1,0:T(8,128)(2,1)S(1)}, bf16[64,2304]{1,0:T(8,128)(2,1)S(1)}, u32[]{:S(2)}, u32[]{:S(2)}) %collective-permute-start.34) | collective-permute-done | bytes 294944 | tf_op jit(solution)/shard_map/ppermute | solution.py:580
  414.3 3.1 collective-permute-done.38
  (191 shorter events, 55.2 us)
Async XLA Ops:
  0.7 26.4 %collective-permute-start = (bf16[512,1024]{1,0:T(8,128)(2,1)}, bf16[512,1024]{1,0:T(8,128)(2,1)S(1)}, u32[]{:S(2)}, u32[]{:S(2)}) collective-permute-start(bf16[512,1024]{1,0:T(8,128)(2,1)} %x_ref.7), channel_id=1, source_target_pairs={{0,1},{1,0},{2,3},{3,2},{4,5},{5,4},{6,7},{7,6},{8,9},{9,8},{10,11... | collective-permute-start | bytes 3145736 | tf_op jit(solution)/shard_map/ppermute | solution.py:580
  11.8 15.3 %copy-start.2 = (bf16[512,1024]{1,0:T(8,128)(2,1)S(1)}, bf16[512,1024]{1,0:T(8,128)(2,1)}, u32[]{:S(2)}) copy-start(bf16[512,1024]{1,0:T(8,128)(2,1)} %wm_ref.3) | copy-start | bytes 3145732
  27.1 37.7 %collective-permute-start.2 = (bf16[512,1024]{1,0:T(8,128)(2,1)S(1)}, bf16[512,1024]{1,0:T(8,128)(2,1)S(1)}, u32[]{:S(2)}, u32[]{:S(2)}) collective-permute-start(bf16[512,1024]{1,0:T(8,128)(2,1)S(1)} %copy-done.2), channel_id=1, source_target_pairs={{0,1},{1,0},{2,3},{3,2},{4,5},{5,4},{6,7},{7,6},{8,9},{9,8},{10,11... | collective-permute-start | bytes 3145736 | tf_op jit(solution)/shard_map/ppermute | solution.py:580
  49.7 15.1 %collective-permute-start.1 = (bf16[512,512]{1,0:T(8,128)(2,1)}, bf16[512,512]{1,0:T(8,128)(2,1)S(1)}, u32[]{:S(2)}, u32[]{:S(2)}) collective-permute-start(bf16[512,512]{1,0:T(8,128)(2,1)} %get-tuple-element.81.o_oth.yt_ref), channel_id=1, source_target_pairs={{0,1},{1,0},{2,3},{3,2},{4,5},{5,4},{6,7},{7,6},{8,9},{9,8},{10,11... | collective-permute-start | bytes 1572872 | tf_op jit(solution)/shard_map/ppermute | solution.py:580
  49.7 37.6 %collective-permute-start.4 = (bf16[512,1024]{1,0:T(8,128)(2,1)S(1)}, bf16[512,1024]{1,0:T(8,128)(2,1)}, u32[]{:S(2)}, u32[]{:S(2)}) collective-permute-start(bf16[512,1024]{1,0:T(8,128)(2,1)S(1)} %copy-done.8), channel_id=1, source_target_pairs={{0,1},{1,0},{2,3},{3,2},{4,5},{5,4},{6,7},{7,6},{8,9},{9,8},{10,11... | collective-permute-start | bytes 3145736 | tf_op jit(solution)/shard_map/ppermute | solution.py:580
  70.6 37.0 %collective-permute-start.3 = (bf16[512,1024]{1,0:T(8,128)(2,1)}, bf16[512,1024]{1,0:T(8,128)(2,1)S(1)}, u32[]{:S(2)}, u32[]{:S(2)}) collective-permute-start(bf16[512,1024]{1,0:T(8,128)(2,1)} %get-tuple-element.84.x_ref.xo_ref), channel_id=1, source_target_pairs={{0,1},{1,0},{2,3},{3,2},{4,5},{5,4},{6,7},{7,6},{8,9},{9,8},{10,11... | collective-permute-start | bytes 3145736 | tf_op jit(solution)/shard_map/ppermute | solution.py:580
  133.0 27.1 %collective-permute-start.5 = (bf16[512,1024]{1,0:T(8,128)(2,1)}, bf16[512,1024]{1,0:T(8,128)(2,1)S(1)}, u32[]{:S(2)}, u32[]{:S(2)}) collective-permute-start(bf16[512,1024]{1,0:T(8,128)(2,1)} %get-tuple-element.89), channel_id=1, source_target_pairs={{0,1},{1,0},{2,3},{3,2},{4,5},{5,4},{6,7},{7,6},{8,9},{9,8},{10,11... | collective-permute-start | bytes 3145736 | tf_op jit(solution)/shard_map/ppermute | solution.py:580
  167.3 12.6 %collective-permute-start.6 = (bf16[512,512]{1,0:T(8,128)(2,1)}, bf16[512,512]{1,0:T(8,128)(2,1)S(1)}, u32[]{:S(2)}, u32[]{:S(2)}) collective-permute-start(bf16[512,512]{1,0:T(8,128)(2,1)} %get-tuple-element.91), channel_id=1, source_target_pairs={{0,1},{1,0},{2,3},{3,2},{4,5},{5,4},{6,7},{7,6},{8,9},{9,8},{10,11... | collective-permute-start | bytes 1572872 | tf_op jit(solution)/shard_map/ppermute | solution.py:580
  177.1 122.9 %collective-permute-start.39 = (bf16[512,2304]{1,0:T(8,128)(2,1)}, bf16[512,2304]{1,0:T(8,128)(2,1)S(1)}, u32[]{:S(2)}, u32[]{:S(2)}) collective-permute-start(bf16[512,2304]{1,0:T(8,128)(2,1)} %get-tuple-element.136), channel_id=1, source_target_pairs={{0,2},{2,0},{4,6},{6,4},{8,10},{10,8},{12,14},{14,12},{16,18},{18,... | collective-permute-start | bytes 7077896 | tf_op jit(solution)/shard_map/ppermute | solution.py:580
  225.1 9.6 %collective-permute-start.10 = (f32[18,128]{1,0:T(8,128)S(1)}, f32[18,128]{1,0:T(8,128)S(1)}, u32[]{:S(2)}, u32[]{:S(2)}) collective-permute-start(f32[18,128]{1,0:T(8,128)S(1)} %pad_maximum_fusion.4), channel_id=1, source_target_pairs={{0,2},{2,0},{4,6},{6,4},{8,10},{10,8},{12,14},{14,12},{16,18},{18,... | collective-permute-start | bytes 27656 | tf_op jit(solution)/shard_map/ppermute | solution.py:580
  234.2 67.4 %collective-permute-start.31 = (bf16[512,2304]{1,0:T(8,128)(2,1)}, bf16[512,2304]{1,0:T(8,128)(2,1)S(1)}, u32[]{:S(2)}, u32[]{:S(2)}) collective-permute-start(bf16[512,2304]{1,0:T(8,128)(2,1)} %get-tuple-element.128), channel_id=1, source_target_pairs={{0,2},{2,0},{4,6},{6,4},{8,10},{10,8},{12,14},{14,12},{16,18},{18,... | collective-permute-start | bytes 7077896 | tf_op jit(solution)/shard_map/ppermute | solution.py:580
  234.7 9.8 %collective-permute-start.11 = (f32[18,128]{1,0:T(8,128)S(1)}, f32[18,128]{1,0:T(8,128)S(1)}, u32[]{:S(2)}, u32[]{:S(2)}) collective-permute-start(f32[18,128]{1,0:T(8,128)S(1)} %fusion.73), channel_id=1, source_target_pairs={{0,4},{2,6},{4,0},{6,2},{8,12},{10,14},{12,8},{14,10},{16,20},{18,... | collective-permute-start | bytes 27656 | tf_op jit(solution)/shard_map/ppermute | solution.py:580
  244.5 73.7 %collective-permute-start.35 = (bf16[512,2304]{1,0:T(8,128)(2,1)}, bf16[512,2304]{1,0:T(8,128)(2,1)S(1)}, u32[]{:S(2)}, u32[]{:S(2)}) collective-permute-start(bf16[512,2304]{1,0:T(8,128)(2,1)} %get-tuple-element.132), channel_id=1, source_target_pairs={{0,2},{2,0},{4,6},{6,4},{8,10},{10,8},{12,14},{14,12},{16,18},{18,... | collective-permute-start | bytes 7077896 | tf_op jit(solution)/shard_map/ppermute | solution.py:580
  244.5 6.9 %collective-permute-start.12 = (f32[18,128]{1,0:T(8,128)S(1)}, f32[18,128]{1,0:T(8,128)S(1)}, u32[]{:S(2)}, u32[]{:S(2)}) collective-permute-start(f32[18,128]{1,0:T(8,128)S(1)} %add.361), channel_id=1, source_target_pairs={{0,8},{2,10},{4,12},{6,14},{8,0},{10,2},{12,4},{14,6},{16,24},{18,... | collective-permute-start | bytes 27656 | tf_op jit(solution)/shard_map/ppermute | solution.py:580
  251.4 6.4 %collective-permute-start.13 = (f32[18,128]{1,0:T(8,128)S(1)}, f32[18,128]{1,0:T(8,128)S(1)}, u32[]{:S(2)}, u32[]{:S(2)}) collective-permute-start(f32[18,128]{1,0:T(8,128)S(1)} %add.362), channel_id=1, source_target_pairs={{0,16},{2,18},{4,20},{6,22},{8,24},{10,26},{12,28},{14,30},{16,0},... | collective-permute-start | bytes 27656 | tf_op jit(solution)/shard_map/ppermute | solution.py:580
  257.9 4.3 %collective-permute-start.14 = (f32[18,128]{1,0:T(8,128)S(1)}, f32[18,128]{1,0:T(8,128)S(1)}, u32[]{:S(2)}, u32[]{:S(2)}) collective-permute-start(f32[18,128]{1,0:T(8,128)S(1)} %add.363), channel_id=1, source_target_pairs={{0,1},{1,0},{2,3},{3,2},{4,5},{5,4},{6,7},{7,6},{8,9},{9,8},{10,11... | collective-permute-start | bytes 27656 | tf_op jit(solution)/shard_map/ppermute | solution.py:580
  262.1 1.8 collective-permute-start.19
  262.2 2.4 collective-permute-start.23
  263.9 21.8 %copy-start.26 = (bf16[512,1024]{1,0:T(8,128)(2,1)S(1)}, bf16[512,1024]{1,0:T(8,128)(2,1)}, u32[]{:S(2)}) copy-start(bf16[512,1024]{1,0:T(8,128)(2,1)} %get-tuple-element.92.xo_ref) | copy-start | bytes 3145732
  263.9 24.5 %copy-start.12 = (bf16[512,512]{1,0:T(8,128)(2,1)S(1)}, bf16[512,512]{1,0:T(8,128)(2,1)}, u32[]{:S(2)}) copy-start(bf16[512,512]{1,0:T(8,128)(2,1)} %get-tuple-element.117) | copy-start | bytes 1572868
  264.0 6.4 %collective-permute-start.20 = (bf16[2,2,64,256]{3,2,1,0:T(8,128)(2,1)S(1)}, bf16[2,2,64,256]{3,2,1,0:T(8,128)(2,1)S(1)}, u32[]{:S(2)}, u32[]{:S(2)}) collective-permute-start(bf16[2,2,64,256]{3,2,1,0:T(8,128)(2,1)S(1)} %fusion.36), channel_id=1, source_target_pairs={{0,4},{2,6},{4,0},{6,2},{8,12},{10,14},{12,8},{14,10},{16,20},{18,... | collective-permute-start | bytes 393224 | tf_op jit(solution)/shard_map/ppermute | solution.py:580
  265.5 6.8 %collective-permute-start.24 = (bf16[2,2,64,256]{3,2,1,0:T(8,128)(2,1)S(1)}, bf16[2,2,64,256]{3,2,1,0:T(8,128)(2,1)S(1)}, u32[]{:S(2)}, u32[]{:S(2)}) collective-permute-start(bf16[2,2,64,256]{3,2,1,0:T(8,128)(2,1)S(1)} %fusion.37), channel_id=1, source_target_pairs={{0,4},{2,6},{4,0},{6,2},{8,12},{10,14},{12,8},{14,10},{16,20},{18,... | collective-permute-start | bytes 393224 | tf_op jit(solution)/shard_map/ppermute | solution.py:580
  270.4 17.5 %collective-permute-start.15 = (bf16[512,512]{1,0:T(8,128)(2,1)S(1)}, bf16[512,512]{1,0:T(8,128)(2,1)S(1)}, u32[]{:S(2)}, u32[]{:S(2)}) collective-permute-start(bf16[512,512]{1,0:T(8,128)(2,1)S(1)} %copy-done.29), channel_id=1, source_target_pairs={{0,2},{2,0},{4,6},{6,4},{8,10},{10,8},{12,14},{14,12},{16,18},{18,... | collective-permute-start | bytes 1572872 | tf_op jit(solution)/shard_map/ppermute | solution.py:580
  272.3 4.3 %collective-permute-start.21 = (bf16[2,64,256]{2,1,0:T(8,128)(2,1)S(1)}, bf16[2,64,256]{2,1,0:T(8,128)(2,1)S(1)}, u32[]{:S(2)}, u32[]{:S(2)}) collective-permute-start(bf16[2,64,256]{2,1,0:T(8,128)(2,1)S(1)} %get-tuple-element.181), channel_id=1, source_target_pairs={{0,8},{2,10},{4,12},{6,14},{8,0},{10,2},{12,4},{14,6},{16,24},{18,... | collective-permute-start | bytes 196616 | tf_op jit(solution)/shard_map/ppermute | solution.py:580
  276.6 4.3 %collective-permute-start.25 = (bf16[2,64,256]{2,1,0:T(8,128)(2,1)S(1)}, bf16[2,64,256]{2,1,0:T(8,128)(2,1)S(1)}, u32[]{:S(2)}, u32[]{:S(2)}) collective-permute-start(bf16[2,64,256]{2,1,0:T(8,128)(2,1)S(1)} %get-tuple-element.183), channel_id=1, source_target_pairs={{0,8},{2,10},{4,12},{6,14},{8,0},{10,2},{12,4},{14,6},{16,24},{18,... | collective-permute-start | bytes 196616 | tf_op jit(solution)/shard_map/ppermute | solution.py:580
  280.9 4.8 %collective-permute-start.22 = (bf16[64,256]{1,0:T(8,128)(2,1)S(1)}, bf16[64,256]{1,0:T(8,128)(2,1)S(1)}, u32[]{:S(2)}, u32[]{:S(2)}) collective-permute-start(bf16[64,256]{1,0:T(8,128)(2,1)S(1)} %fusion.62), channel_id=1, source_target_pairs={{0,16},{2,18},{4,20},{6,22},{8,24},{10,26},{12,28},{14,30},{16,0},... | collective-permute-start | bytes 98312 | tf_op jit(solution)/shard_map/ppermute | solution.py:580
  285.7 26.3 %collective-permute-start.7 = (bf16[512,1024]{1,0:T(8,128)(2,1)S(1)}, bf16[512,1024]{1,0:T(8,128)(2,1)S(1)}, u32[]{:S(2)}, u32[]{:S(2)}) collective-permute-start(bf16[512,1024]{1,0:T(8,128)(2,1)S(1)} %copy-done.26), channel_id=1, source_target_pairs={{0,1},{1,0},{2,3},{3,2},{4,5},{5,4},{6,7},{7,6},{8,9},{9,8},{10,11... | collective-permute-start | bytes 3145736 | tf_op jit(solution)/shard_map/ppermute | solution.py:580
  287.9 4.9 %collective-permute-start.26 = (bf16[64,256]{1,0:T(8,128)(2,1)S(1)}, bf16[64,256]{1,0:T(8,128)(2,1)S(1)}, u32[]{:S(2)}, u32[]{:S(2)}) collective-permute-start(bf16[64,256]{1,0:T(8,128)(2,1)S(1)} %fusion.64), channel_id=1, source_target_pairs={{0,16},{2,18},{4,20},{6,22},{8,24},{10,26},{12,28},{14,30},{16,0},... | collective-permute-start | bytes 98312 | tf_op jit(solution)/shard_map/ppermute | solution.py:580
  292.8 6.4 %collective-permute-start.16 = (bf16[2,2,64,512]{3,2,1,0:T(8,128)(2,1)S(1)}, bf16[2,2,64,512]{3,2,1,0:T(8,128)(2,1)S(1)}, u32[]{:S(2)}, u32[]{:S(2)}) collective-permute-start(bf16[2,2,64,512]{3,2,1,0:T(8,128)(2,1)S(1)} %fusion.29), channel_id=1, source_target_pairs={{0,4},{2,6},{4,0},{6,2},{8,12},{10,14},{12,8},{14,10},{16,20},{18,... | collective-permute-start | bytes 786440 | tf_op jit(solution)/shard_map/ppermute | solution.py:580
  299.1 31.1 %collective-permute-start.9 = (bf16[512,1024]{1,0:T(8,128)(2,1)}, bf16[512,1024]{1,0:T(8,128)(2,1)}, u32[]{:S(2)}, u32[]{:S(2)}) collective-permute-start(bf16[512,1024]{1,0:T(8,128)(2,1)} %get-tuple-element.108), channel_id=1, source_target_pairs={{0,1},{1,0},{2,3},{3,2},{4,5},{5,4},{6,7},{7,6},{8,9},{9,8},{10,11... | collective-permute-start | bytes 3145736 | tf_op jit(solution)/shard_map/ppermute | solution.py:580
  299.9 19.9 %collective-permute-start.17 = (bf16[2,64,512]{2,1,0:T(8,128)(2,1)}, bf16[2,64,512]{2,1,0:T(8,128)(2,1)}, u32[]{:S(2)}, u32[]{:S(2)}) collective-permute-start(bf16[2,64,512]{2,1,0:T(8,128)(2,1)} %get-tuple-element.179), channel_id=1, source_target_pairs={{0,8},{2,10},{4,12},{6,14},{8,0},{10,2},{12,4},{14,6},{16,24},{18,... | collective-permute-start | bytes 393224 | tf_op jit(solution)/shard_map/ppermute | solution.py:580
  301.6 63.0 %collective-permute-start.40 = (bf16[2,2,64,2304]{3,2,1,0:T(8,128)(2,1)}, bf16[2,2,64,2304]{3,2,1,0:T(8,128)(2,1)}, u32[]{:S(2)}, u32[]{:S(2)}) collective-permute-start(bf16[2,2,64,2304]{3,2,1,0:T(8,128)(2,1)} %fusion.2), channel_id=1, source_target_pairs={{0,8},{2,10},{4,12},{6,14},{8,0},{10,2},{12,4},{14,6},{16,24},{18,... | collective-permute-start | bytes 3538952 | tf_op jit(solution)/shard_map/ppermute | solution.py:580
  312.9 53.3 %collective-permute-start.32 = (bf16[2,2,64,2304]{3,2,1,0:T(8,128)(2,1)}, bf16[2,2,64,2304]{3,2,1,0:T(8,128)(2,1)}, u32[]{:S(2)}, u32[]{:S(2)}) collective-permute-start(bf16[2,2,64,2304]{3,2,1,0:T(8,128)(2,1)} %fusion), channel_id=1, source_target_pairs={{0,4},{2,6},{4,0},{6,2},{8,12},{10,14},{12,8},{14,10},{16,20},{18,... | collective-permute-start | bytes 3538952 | tf_op jit(solution)/shard_map/ppermute | solution.py:580
  318.2 3.7 collective-permute-start.27
  319.8 51.6 %collective-permute-start.36 = (bf16[2,2,64,2304]{3,2,1,0:T(8,128)(2,1)}, bf16[2,2,64,2304]{3,2,1,0:T(8,128)(2,1)S(1)}, u32[]{:S(2)}, u32[]{:S(2)}) collective-permute-start(bf16[2,2,64,2304]{3,2,1,0:T(8,128)(2,1)} %fusion.1), channel_id=1, source_target_pairs={{0,4},{2,6},{4,0},{6,2},{8,12},{10,14},{12,8},{14,10},{16,20},{18,... | collective-permute-start | bytes 3538952 | tf_op jit(solution)/shard_map/ppermute | solution.py:580
  321.9 5.9 %collective-permute-start.18 = (bf16[64,512]{1,0:T(8,128)(2,1)S(1)}, bf16[64,512]{1,0:T(8,128)(2,1)S(1)}, u32[]{:S(2)}, u32[]{:S(2)}) collective-permute-start(bf16[64,512]{1,0:T(8,128)(2,1)S(1)} %fusion.50), channel_id=1, source_target_pairs={{0,16},{2,18},{4,20},{6,22},{8,24},{10,26},{12,28},{14,30},{16,0},... | collective-permute-start | bytes 196616 | tf_op jit(solution)/shard_map/ppermute | solution.py:580
  327.8 36.6 %collective-permute-start.28 = (bf16[2,2,64,512]{3,2,1,0:T(8,128)(2,1)S(1)}, bf16[2,2,64,512]{3,2,1,0:T(8,128)(2,1)S(1)}, u32[]{:S(2)}, u32[]{:S(2)}) collective-permute-start(bf16[2,2,64,512]{3,2,1,0:T(8,128)(2,1)S(1)} %fusion.30), channel_id=1, source_target_pairs={{0,4},{2,6},{4,0},{6,2},{8,12},{10,14},{12,8},{14,10},{16,20},{18,... | collective-permute-start | bytes 786440 | tf_op jit(solution)/shard_map/ppermute | solution.py:580
  330.3 55.5 %collective-permute-start.8 = (bf16[512,1024]{1,0:T(8,128)(2,1)}, bf16[512,1024]{1,0:T(8,128)(2,1)S(1)}, u32[]{:S(2)}, u32[]{:S(2)}) collective-permute-start(bf16[512,1024]{1,0:T(8,128)(2,1)} %get-tuple-element.93), channel_id=1, source_target_pairs={{0,1},{1,0},{2,3},{3,2},{4,5},{5,4},{6,7},{7,6},{8,9},{9,8},{10,11... | collective-permute-start | bytes 3145736 | tf_op jit(solution)/shard_map/ppermute | solution.py:580
  364.5 6.5 %collective-permute-start.29 = (bf16[2,64,512]{2,1,0:T(8,128)(2,1)S(1)}, bf16[2,64,512]{2,1,0:T(8,128)(2,1)S(1)}, u32[]{:S(2)}, u32[]{:S(2)}) collective-permute-start(bf16[2,64,512]{2,1,0:T(8,128)(2,1)S(1)} %get-tuple-element.177), channel_id=1, source_target_pairs={{0,8},{2,10},{4,12},{6,14},{8,0},{10,2},{12,4},{14,6},{16,24},{18,... | collective-permute-start | bytes 393224 | tf_op jit(solution)/shard_map/ppermute | solution.py:580
  366.1 21.3 %collective-permute-start.41 = (bf16[2,64,2304]{2,1,0:T(8,128)(2,1)S(1)}, bf16[2,64,2304]{2,1,0:T(8,128)(2,1)S(1)}, u32[]{:S(2)}, u32[]{:S(2)}) collective-permute-start(bf16[2,64,2304]{2,1,0:T(8,128)(2,1)S(1)} %get-tuple-element.171), channel_id=1, source_target_pairs={{0,4},{2,6},{4,0},{6,2},{8,12},{10,14},{12,8},{14,10},{16,20},{18,... | collective-permute-start | bytes 1769480 | tf_op jit(solution)/shard_map/ppermute | solution.py:580
  366.2 19.6 %copy-start.7 = (f32[512,1024]{1,0:T(8,128)S(1)}, f32[512,1024]{1,0:T(8,128)}, u32[]{:S(2)}) copy-start(f32[512,1024]{1,0:T(8,128)} %get-tuple-element.85) | copy-start | bytes 6291460
  367.9 23.1 %collective-permute-start.33 = (bf16[2,64,2304]{2,1,0:T(8,128)(2,1)S(1)}, bf16[2,64,2304]{2,1,0:T(8,128)(2,1)S(1)}, u32[]{:S(2)}, u32[]{:S(2)}) collective-permute-start(bf16[2,64,2304]{2,1,0:T(8,128)(2,1)S(1)} %get-tuple-element.173), channel_id=1, source_target_pairs={{0,8},{2,10},{4,12},{6,14},{8,0},{10,2},{12,4},{14,6},{16,24},{18,... | collective-permute-start | bytes 1769480 | tf_op jit(solution)/shard_map/ppermute | solution.py:580
  371.0 14.8 %copy-start = (f32[512,1024]{1,0:T(8,128)S(1)}, f32[512,1024]{1,0:T(8,128)}, u32[]{:S(2)}) copy-start(f32[512,1024]{1,0:T(8,128)} %get-tuple-element.83.resid_ref) | copy-start | bytes 6291460
  371.0 14.1 %collective-permute-start.30 = (bf16[64,512]{1,0:T(8,128)(2,1)S(1)}, bf16[64,512]{1,0:T(8,128)(2,1)S(1)}, u32[]{:S(2)}, u32[]{:S(2)}) collective-permute-start(bf16[64,512]{1,0:T(8,128)(2,1)S(1)} %fusion.54), channel_id=1, source_target_pairs={{0,16},{2,18},{4,20},{6,22},{8,24},{10,26},{12,28},{14,30},{16,0},... | collective-permute-start | bytes 196616 | tf_op jit(solution)/shard_map/ppermute | solution.py:580
  371.7 27.9 %collective-permute-start.37 = (bf16[2,64,2304]{2,1,0:T(8,128)(2,1)S(1)}, bf16[2,64,2304]{2,1,0:T(8,128)(2,1)S(1)}, u32[]{:S(2)}, u32[]{:S(2)}) collective-permute-start(bf16[2,64,2304]{2,1,0:T(8,128)(2,1)S(1)} %get-tuple-element.175), channel_id=1, source_target_pairs={{0,8},{2,10},{4,12},{6,14},{8,0},{10,2},{12,4},{14,6},{16,24},{18,... | collective-permute-start | bytes 1769480 | tf_op jit(solution)/shard_map/ppermute | solution.py:580
  387.5 31.9 %collective-permute-start.42 = (bf16[64,2304]{1,0:T(8,128)(2,1)S(1)}, bf16[64,2304]{1,0:T(8,128)(2,1)S(1)}, u32[]{:S(2)}, u32[]{:S(2)}) collective-permute-start(bf16[64,2304]{1,0:T(8,128)(2,1)S(1)} %fusion.28), channel_id=1, source_target_pairs={{0,16},{2,18},{4,20},{6,22},{8,24},{10,26},{12,28},{14,30},{16,0},... | collective-permute-start | bytes 884744 | tf_op jit(solution)/shard_map/ppermute | solution.py:580
  391.1 23.1 %collective-permute-start.34 = (bf16[64,2304]{1,0:T(8,128)(2,1)S(1)}, bf16[64,2304]{1,0:T(8,128)(2,1)S(1)}, u32[]{:S(2)}, u32[]{:S(2)}) collective-permute-start(bf16[64,2304]{1,0:T(8,128)(2,1)S(1)} %fusion.24), channel_id=1, source_target_pairs={{0,16},{2,18},{4,20},{6,22},{8,24},{10,26},{12,28},{14,30},{16,0},... | collective-permute-start | bytes 884744 | tf_op jit(solution)/shard_map/ppermute | solution.py:580
  399.6 17.7 %collective-permute-start.38 = (bf16[64,2304]{1,0:T(8,128)(2,1)S(1)}, bf16[64,2304]{1,0:T(8,128)(2,1)S(1)}, u32[]{:S(2)}, u32[]{:S(2)}) collective-permute-start(bf16[64,2304]{1,0:T(8,128)(2,1)S(1)} %fusion.26), channel_id=1, source_target_pairs={{0,16},{2,18},{4,20},{6,22},{8,24},{10,26},{12,28},{14,30},{16,0},... | collective-permute-start | bytes 884744 | tf_op jit(solution)/shard_map/ppermute | solution.py:580
  (27 other events, 135.0 us)

commit v2 on v0

--- a/solution.py
+++ b/solution.py
@@ -1,12 +1,984 @@
+import functools
 import math
 
 import jax
 import jax.numpy as jnp
 from jax import lax
+from jax.experimental import pallas as pl
+from jax.experimental.pallas import tpu as pltpu
 from jax.sharding import PartitionSpec as P
 
 EPS = 1e-06
 THETA = 1000000.0
+LOG2E = 1.4426950408889634
+LN2 = 0.6931471805599453
+BLOCK = 256
+PAIR = 128
+SAME = 256.0
+F32 = jnp.float32
+BF16 = jnp.bfloat16
+COST_RATE = 1.0e13
+VMEM_LIMIT = 56 * 1024 * 1024
+BACK_VMEM = 61 * 1024 * 1024
+
+
+def dot_nn(a, b):
+    return lax.dot_general(a, b, (((1,), (0,)), ((), ())), preferred_element_type=F32)
+
+
+def dot_nt(a, b):
+    return lax.dot_general(a, b, (((1,), (1,)), ((), ())), preferred_element_type=F32)
+
+
+def cost(seconds):
+    return pl.CostEstimate(flops=int(seconds * COST_RATE), bytes_accessed=0, transcendentals=0)
+
+
+def lane_of(shape):
+    return lax.broadcasted_iota(jnp.int32, shape, len(shape) - 1)
+
+
+def head_mean(values):
+    high = values.astype(BF16)
+    low = (values - high.astype(F32)).astype(BF16)
+    row = lax.broadcasted_iota(jnp.int32, (PAIR, PAIR), 0) // 64
+    col = lax.broadcasted_iota(jnp.int32, (PAIR, PAIR), 1) // 64
+    mean = jnp.where(row == col, 1.0 / 64.0, 0.0).astype(BF16)
+    return dot_nn(high, mean) + dot_nn(low, mean)
+
+
+def swap_halves(values):
+    first = lane_of(values.shape) % 64 < 32
+    return jnp.where(first, pltpu.roll(values, 96, 1), pltpu.roll(values, 32, 1))
+
+
+def rope(values, cosine, sine):
+    return values * cosine + swap_halves(values) * sine
+
+
+def row_norm(x):
+    return lax.rsqrt(jnp.mean(x * x, axis=-1, keepdims=True) + EPS)
+
+
+def qkv_kernel(
+    x_ref, gain_ref, wq_ref, wk_ref, wv_ref, qg_ref, kg_ref, cos_ref, sin_ref,
+    attn_ref, q_ref, kd_ref, vd_ref, qraw_ref, kraw_ref,
+):
+    x = x_ref[...].astype(F32)
+    attn = (x * row_norm(x) * gain_ref[...]).astype(BF16)
+    attn_ref[...] = attn
+    q = dot_nn(attn, wq_ref[...])
+    k = dot_nn(attn, wk_ref[...])
+    v = dot_nn(attn, wv_ref[...])
+    qraw_ref[...] = q.astype(BF16)
+    kraw_ref[...] = k.astype(BF16)
+    cosine, sine = cos_ref[...], sin_ref[...]
+    for g in range(q.shape[1] // PAIR):
+        at = slice(g * PAIR, (g + 1) * PAIR)
+        u = q[:, at]
+        n = u * lax.rsqrt(head_mean(u * u) + EPS)
+        q_ref[:, at] = (rope(n * qg_ref[...], cosine, sine) * (LOG2E / 8.0)).astype(BF16)
+    low = lane_of((x.shape[0], PAIR)) < 64
+    for p in range(k.shape[1] // PAIR):
+        at = slice(p * PAIR, (p + 1) * PAIR)
+        u = k[:, at]
+        n = u * lax.rsqrt(head_mean(u * u) + EPS)
+        roped = rope(n * kg_ref[...], cosine, sine)
+        for src, dst in ((roped, kd_ref), (v[:, at], vd_ref)):
+            turned = pltpu.roll(src, 64, 1)
+            dst[:, 2 * p * PAIR : (2 * p + 1) * PAIR] = jnp.where(low, src, turned).astype(BF16)
+            dst[:, (2 * p + 1) * PAIR : (2 * p + 2) * PAIR] = jnp.where(low, turned, src).astype(BF16)
+
+
+def qkv(x, gain, w_q, w_kv, qg, kg, cosine, sine, half):
+    rows, width = x.shape
+    qc, kc = w_q.shape[1], w_kv.shape[1] // 2
+    nb = rows // BLOCK
+    whole = lambda shape, *at: pl.BlockSpec(shape, lambda i: at)
+    row = lambda cols: pl.BlockSpec((BLOCK, cols), lambda i: (i, 0))
+    table = pl.BlockSpec((BLOCK, PAIR), lambda i: (i + half * nb, 0))
+    return pl.pallas_call(
+        qkv_kernel,
+        grid=(nb,),
+        in_specs=[
+            row(width), whole((1, width), 0, 0), whole((width, qc), 0, 0),
+            whole((width, kc), 0, 0), whole((width, kc), 0, 1),
+            whole((1, PAIR), 0, 0), whole((1, PAIR), 0, 0), table, table,
+        ],
+        out_specs=[row(width), row(qc), row(2 * kc), row(2 * kc), row(qc), row(kc)],
+        out_shape=[
+            jax.ShapeDtypeStruct((rows, c), BF16) for c in (width, qc, 2 * kc, 2 * kc, qc, kc)
+        ],
+        compiler_params=pltpu.CompilerParams(vmem_limit_bytes=VMEM_LIMIT),
+        cost_estimate=cost(5e-6),
+        name="qkv",
+    )(x, gain, w_q, w_kv, w_kv, qg, kg, cosine, sine)
+
+
+def attn_fwd_kernel(
+    s_ref, q_ref, kown_ref, koth_ref, vown_ref, voth_ref, segq_ref, segk_ref,
+    o_ref, linv_ref, kx0, kx1, vx0, vx1, acc,
+):
+    rows = q_ref.shape[0]
+    own = s_ref[0]
+    first = s_ref[1]
+    nb = rows // BLOCK
+    low = lane_of((rows, PAIR)) < 64
+    zero = jnp.zeros((rows, PAIR), BF16)
+
+    @pl.when(pl.program_id(0) == 0)
+    def _():
+        one = jnp.ones((2 * rows, PAIR), F32)
+        both = lane_of((2 * rows, PAIR)) < 64
+        kx0[:, PAIR:] = segk_ref[...]
+        kx1[:, PAIR:] = segk_ref[...]
+        vx0[:, PAIR:] = jnp.where(both, one, 0.0).astype(BF16)
+        vx1[:, PAIR:] = jnp.where(both, 0.0, one).astype(BF16)
+
+    for part, (k_ref, v_ref) in enumerate(((kown_ref, vown_ref), (koth_ref, voth_ref))):
+        at = slice(part * rows, (part + 1) * rows)
+        kx0[at, :PAIR] = jnp.where(low, k_ref[...], zero)
+        kx1[at, :PAIR] = jnp.where(low, zero, k_ref[...])
+        vx0[at, :PAIR] = jnp.where(low, v_ref[...], zero)
+        vx1[at, :PAIR] = jnp.where(low, zero, v_ref[...])
+
+    for i in range(nb):
+        at = slice(i * BLOCK, (i + 1) * BLOCK)
+        q = jnp.concatenate([q_ref[at, :], segq_ref[at, :]], axis=1)
+        block = first + i
+
+        def step(kb, diagonal):
+            here = pl.ds(pl.multiple_of(lax.rem(kb + own, 2 * nb) * BLOCK, BLOCK), BLOCK)
+            total = None
+            for kx, vx in ((kx0, vx0), (kx1, vx1)):
+                s = dot_nt(q, kx[here, :])
+                if diagonal:
+                    r = lax.broadcasted_iota(jnp.int32, s.shape, 0)
+                    s = jnp.where(lane_of(s.shape) <= r, s, -1e30)
+                term = dot_nn(jnp.exp2(s).astype(BF16), vx[here, :])
+                total = term if total is None else total + term
+            return total
+
+        acc[...] = step(block, True)
+
+        def body(kb, carry):
+            acc[...] += step(kb, False)
+            return carry
+
+        lax.fori_loop(s_ref[2 + block], block, body, 0)
+        inverse = 1.0 / acc[:, PAIR:]
+        o_ref[at, :] = (acc[:, :PAIR] * inverse).astype(BF16)
+        linv_ref[at, :] = inverse
+
+
+def attn_fwd(scalars, q, k_own, k_oth, v_own, v_oth, segq, segk, half):
+    rows, qc = q.shape
+    groups = qc // PAIR
+    col = pl.BlockSpec((rows, PAIR), lambda g, s: (0, g))
+    return pl.pallas_call(
+        attn_fwd_kernel,
+        grid_spec=pltpu.PrefetchScalarGridSpec(
+            num_scalar_prefetch=1,
+            grid=(groups,),
+            in_specs=[col] * 5
+            + [
+                pl.BlockSpec((rows, PAIR), lambda g, s: (half, 0)),
+                pl.BlockSpec((2 * rows, PAIR), lambda g, s: (0, 0)),
+            ],
+            out_specs=[col, col],
+            scratch_shapes=[pltpu.VMEM((2 * rows, 2 * PAIR), BF16)] * 4
+            + [pltpu.VMEM((BLOCK, 2 * PAIR), F32)],
+        ),
+        out_shape=[
+            jax.ShapeDtypeStruct((rows, qc), BF16),
+            jax.ShapeDtypeStruct((rows, qc), F32),
+        ],
+        compiler_params=pltpu.CompilerParams(vmem_limit_bytes=VMEM_LIMIT),
+        cost_estimate=cost(10e-6),
+        name="attn_fwd",
+    )(scalars, q, k_own, k_oth, v_own, v_oth, segq, segk)
+
+
+def resid_kernel(mine_ref, theirs_ref, wm_ref, wt_ref, x_ref, gain_ref, resid_ref, ffn_ref):
+    resid = (
+        x_ref[...].astype(F32)
+        + dot_nn(mine_ref[...], wm_ref[...])
+        + dot_nn(theirs_ref[...], wt_ref[...])
+    )
+    resid_ref[...] = resid
+    ffn_ref[...] = (resid * row_norm(resid) * gain_ref[...]).astype(BF16)
+
+
+def resid_norm(mine, theirs, w_mine, w_theirs, x, gain):
+    rows, width = x.shape
+    cols = mine.shape[1]
+    row = lambda c: pl.BlockSpec((BLOCK, c), lambda i: (i, 0))
+    whole = lambda r, c: pl.BlockSpec((r, c), lambda i: (0, 0))
+    return pl.pallas_call(
+        resid_kernel,
+        grid=(rows // BLOCK,),
+        in_specs=[row(cols), row(cols), whole(cols, width), whole(cols, width), row(width), whole(1, width)],
+        out_specs=[row(width), row(width)],
+        out_shape=[jax.ShapeDtypeStruct((rows, width), F32), jax.ShapeDtypeStruct((rows, width), BF16)],
+        compiler_params=pltpu.CompilerParams(vmem_limit_bytes=VMEM_LIMIT),
+        cost_estimate=cost(4e-6),
+        name="resid",
+    )(mine, theirs, w_mine, w_theirs, x, gain)
+
+
+def ffn_kernel(x_ref, c_ref, wg_ref, wu_ref, wd_ref, h_ref, y_ref, gf_ref, yacc, gacc):
+    x, c = x_ref[...], c_ref[...]
+    gate = dot_nn(x, wg_ref[...])
+    up = dot_nn(x, wu_ref[...])
+    grad = dot_nt(c, wd_ref[...])
+    sig = 0.5 * jnp.tanh(0.5 * gate) + 0.5
+    silu = gate * sig
+    mixed = (silu * up).astype(BF16)
+    gg = (grad * up * (sig + silu * (1.0 - sig))).astype(BF16)
+    gu = (grad * silu).astype(BF16)
+    for i, value in enumerate((mixed, gg, gu)):
+        h_ref[i] = value
+    y = dot_nn(mixed, wd_ref[...])
+    gf = dot_nt(gg, wg_ref[...]) + dot_nt(gu, wu_ref[...])
+    step = pl.program_id(0)
+
+    @pl.when(step == 0)
+    def _():
+        yacc[...] = y
+        gacc[...] = gf
+
+    @pl.when(step > 0)
+    def _():
+        yacc[...] += y
+        gacc[...] += gf
+
+    @pl.when(step == pl.num_programs(0) - 1)
+    def _():
+        y_ref[...] = yacc[...].astype(y_ref.dtype)
+        gf_ref[...] = gacc[...].astype(gf_ref.dtype)
+
+
+def ffn(x, c, w_gu, w_down, dtype):
+    rows, width = x.shape
+    hidden = w_down.shape[0]
+    tile = CHUNK
+    nf = hidden // tile
+    whole = pl.BlockSpec((rows, width), lambda f: (0, 0))
+    mid = pl.BlockSpec((3, rows, tile), lambda f: (0, 0, f))
+    return pl.pallas_call(
+        ffn_kernel,
+        grid=(nf,),
+        in_specs=[
+            whole, whole,
+            pl.BlockSpec((width, tile), lambda f: (0, f)),
+            pl.BlockSpec((width, tile), lambda f: (0, f + nf)),
+            pl.BlockSpec((tile, width), lambda f: (f, 0)),
+        ],
+        out_specs=[mid, whole, whole],
+        out_shape=[jax.ShapeDtypeStruct((3, rows, hidden), BF16)]
+        + [jax.ShapeDtypeStruct((rows, width), dtype)] * 2,
+        scratch_shapes=[pltpu.VMEM((rows, width), F32)] * 2,
+        compiler_params=pltpu.CompilerParams(vmem_limit_bytes=VMEM_LIMIT),
+        cost_estimate=cost(20e-6),
+        name="ffn",
+    )(x, c, w_gu, w_gu, w_down)
+
+
+MESH = pl.DeviceIdType.MESH
+CHUNK = 768
+SPLIT = 512
+BITS = 3
+
+
+def dot_tn(a, b):
+    return lax.dot_general(a, b, (((0,), (0,)), ((), ())), preferred_element_type=F32)
+
+
+BACK_INPUTS = (
+    "h_own", "h_oth", "cot_own", "cot_oth", "ffn_own", "ffn_oth", "attn_own", "attn_oth", "tok_own", "tok_oth",
+    "gf_own", "gf_send", "y_own", "y_send", "resid", "wo_mine", "wo_oth", "w_q", "w_kv",
+    "q_own", "q_oth", "kd_own", "kd_oth", "vd_own", "vd_oth", "o_own", "o_oth", "linv_own", "linv_oth",
+    "qraw_own", "qraw_oth", "kraw_own", "kraw_oth",
+)
+BACK_TABLES = ("segq", "segk", "cos", "sin", "gain1", "gain2", "qg", "kg")
+BACK_OUTPUTS = ("output", "grad_tokens", "shards", "gains", "y_recv")
+
+
+class Names:
+    def __init__(self, names, refs):
+        self.__dict__.update(zip(names, refs))
+
+
+def back_kernel(n_dp, scratch_names, *refs):
+    m = Names(BACK_INPUTS + BACK_TABLES + BACK_OUTPUTS + scratch_names, refs)
+    rows, width = m.resid.shape
+    hidden = m.h_own.shape[2]
+    per_x = hidden // CHUNK
+    n_wide = 3 * per_x
+    n_chunks = n_wide + 2
+    nb = 2 * rows // BLOCK
+    t = lax.axis_index("tensor")
+    d = lax.axis_index("dp")
+    core = lax.rem(d, 2)
+    x = lax.rem(d // 2, 2)
+    zl = lax.rem(d // 4, 2)
+    zh = d // 8
+    over_t = {"tensor": 1 - t}
+    over_core = {"dp": d + 1 - 2 * core}
+    over_x = {"dp": d + 2 - 4 * x}
+    over_zl = {"dp": d + 4 - 8 * zl}
+    over_zh = {"dp": d + 8 - 16 * zh}
+    partners = (over_t, over_core, over_x, over_zl, over_zh)
+    low = lane_of((rows, PAIR)) < 64
+    own_rows, oth_rows = pl.ds(0, rows), pl.ds(rows, rows)
+
+    barrier = pltpu.get_barrier_semaphore()
+    for p in partners:
+        pl.semaphore_signal(barrier, inc=1, device_id=p, device_id_type=MESH)
+    pl.semaphore_wait(barrier, len(partners))
+
+    def tensor_copy(i, src, dst):
+        return pltpu.make_async_remote_copy(
+            src_ref=src, dst_ref=dst, send_sem=m.t_send.at[i], recv_sem=m.t_recv.at[i],
+            device_id=over_t, device_id_type=MESH,
+        )
+
+    gf_copy = tensor_copy(0, m.gf_send, m.gf_recv)
+    do_copy = tensor_copy(1, m.do_send, m.do_recv)
+    branch_copy = tensor_copy(2, m.branch, m.branch_recv)
+    y_copy = tensor_copy(3, m.y_send, m.y_recv)
+    ga_copy = tensor_copy(4, m.branch, m.gf_recv)
+
+    def rs_copy(stage, c, src, dst, device):
+        return pltpu.make_async_remote_copy(
+            src_ref=src, dst_ref=dst, send_sem=m.rs_send.at[stage, c], recv_sem=m.rs_recv.at[stage, c],
+            device_id=device, device_id_type=MESH,
+        )
+
+    left, right = pl.ds(0, SPLIT), pl.ds(SPLIT, CHUNK - SPLIT)
+    every = pl.ds(0, 2)
+    block_rows = m.sums.shape[4]
+    full_rows = pl.ds(0, block_rows)
+
+    def core_copy(c):
+        return rs_copy(0, c, m.core_send.at[lax.rem(c, 2)], m.sums.at[c], over_core)
+
+    def first_copies(c):
+        return (
+            rs_copy(1, c, m.sums.at[c, every, every, 1 - x, full_rows, left], m.r1a.at[c], over_x),
+            rs_copy(2, c, m.sums.at[c, every, 1 - zl, every, full_rows, right], m.r1b.at[c], over_zl),
+        )
+
+    def second_copies(c):
+        return (
+            rs_copy(3, c, m.sums.at[c, every, 1 - zl, x, full_rows, left], m.r2a.at[c], over_zl),
+            rs_copy(4, c, m.sums.at[c, every, zl, 1 - x, full_rows, right], m.r2b.at[c], over_x),
+        )
+
+    def third_copy(c):
+        return rs_copy(5, c, m.sums.at[c, 1 - zh, zl, x], m.r3.at[c], over_zh)
+
+    def local(i, src, dst):
+        return pltpu.make_async_copy(src, dst, m.l_sem.at[i])
+
+    def both(i, src_own, src_oth, dst):
+        return (local(i, src_own, dst.at[own_rows]), local(i + 1, src_oth, dst.at[oth_rows]))
+
+    def start(copies):
+        for copy in copies:
+            copy.start()
+
+    def wait(copies):
+        for copy in copies:
+            copy.wait()
+
+    def add_core(c):
+        core_copy(c).wait_recv()
+        for a in range(2):
+            for b in range(2):
+                for e in range(2):
+                    m.sums[c, a, b, e] = (
+                        m.sums[c, a, b, e].astype(F32) + m.kept[lax.rem(c, 2), a, b, e].astype(F32)
+                    ).astype(BF16)
+
+    def total_copy(c):
+        slot = lax.rem(c, 2)
+        return pltpu.make_async_copy(m.totals.at[slot], m.shards.at[c], m.s_sem.at[slot])
+
+    def tick(i):
+        @pl.when(i < n_chunks)
+        def _():
+            a_copy, b_copy = first_copies(i)
+            a_copy.wait_recv()
+            b_copy.wait_recv()
+            for a in range(2):
+                for b in range(2):
+                    m.sums[i, a, b, x, :, :SPLIT] = (
+                        m.sums[i, a, b, x, :, :SPLIT].astype(F32) + m.r1a[i, a, b].astype(F32)
+                    ).astype(BF16)
+                    m.sums[i, a, zl, b, :, SPLIT:] = (
+                        m.sums[i, a, zl, b, :, SPLIT:].astype(F32) + m.r1b[i, a, b].astype(F32)
+                    ).astype(BF16)
+            start(second_copies(i))
+
+        @pl.when(i + 2 < n_chunks)
+        def _():
+            start(first_copies(i + 2))
+
+        @pl.when((i >= 1) & (i < n_chunks + 1))
+        def _():
+            c = i - 1
+            a_copy, b_copy = second_copies(c)
+            a_copy.wait_recv()
+            b_copy.wait_recv()
+            for a in range(2):
+                m.sums[c, a, zl, x, :, :SPLIT] = (
+                    m.sums[c, a, zl, x, :, :SPLIT].astype(F32) + m.r2a[c, a].astype(F32)
+                ).astype(BF16)
+                m.sums[c, a, zl, x, :, SPLIT:] = (
+                    m.sums[c, a, zl, x, :, SPLIT:].astype(F32) + m.r2b[c, a].astype(F32)
+                ).astype(BF16)
+            third_copy(c).start()
+
+        @pl.when((i >= 2) & (i < n_chunks + 2))
+        def _():
+            c = i - 2
+            third_copy(c).wait_recv()
+
+            @pl.when(c >= 2)
+            def _():
+                total_copy(c - 2).wait()
+
+            m.totals[lax.rem(c, 2)] = m.sums[c, zh, zl, x].astype(F32) + m.r3[c].astype(F32)
+            total_copy(c).start()
+
+    def pack(dst, own_ref, oth_ref):
+        for part, ref in enumerate((own_ref, oth_ref)):
+            at = pl.ds(part * rows, rows)
+            for k in range(width // (2 * PAIR)):
+                a = ref[:, 2 * k * PAIR : (2 * k + 1) * PAIR].astype(F32)
+                b = ref[:, (2 * k + 1) * PAIR : (2 * k + 2) * PAIR].astype(F32)
+                lanes = slice(k * PAIR, (k + 1) * PAIR)
+                m.packed[dst, 0, at, lanes] = jnp.where(low, a, pltpu.roll(b, 64, 1)).astype(BF16)
+                m.packed[dst, 1, at, lanes] = jnp.where(low, pltpu.roll(a, 64, 1), b).astype(BF16)
+
+    def put(ref, slot, lanes, value):
+        for a in range(2):
+            for b in range(2):
+                for e in range(2):
+                    k = ((a * 2 + b) * 2 + e) * block_rows
+                    ref[slot, a, b, e, :, lanes] = value[k : k + block_rows].astype(BF16)
+
+    gf_copy.start()
+    stage_cot = both(0, m.cot_own, m.cot_oth, m.stage)
+    stage_ffn = both(0, m.ffn_own, m.ffn_oth, m.stage)
+    stage_attn = both(0, m.attn_own, m.attn_oth, m.stage)
+    start(stage_cot)
+    loads = [
+        local(2, m.gf_own, m.gres), local(3, m.resid, m.resid_v), local(4, m.wo_mine, m.wom_v),
+        local(5, m.wo_oth, m.wot_v), local(6, m.cot_own, m.cot_v), local(7, m.w_q, m.wq_v), local(8, m.w_kv, m.wkv_v),
+        *both(9, m.o_own, m.o_oth, m.o_v), *both(11, m.kraw_own, m.kraw_oth, m.kraw_v),
+    ]
+
+    def tiles(g):
+        slot = lax.rem(g, 2)
+        lanes = pl.ds(pl.multiple_of(g * PAIR, PAIR), PAIR)
+        out = []
+        for j, (own, oth, dst) in enumerate((
+            (m.q_own, m.q_oth, m.q_v), (m.kd_own, m.kd_oth, m.kd_v), (m.vd_own, m.vd_oth, m.vd_v),
+            (m.qraw_own, m.qraw_oth, m.qraw_v), (m.linv_own, m.linv_oth, m.linv_v),
+        )):
+            out.append(pltpu.make_async_copy(own.at[:, lanes], dst.at[slot, own_rows], m.g_sem.at[slot, 2 * j]))
+            out.append(pltpu.make_async_copy(oth.at[:, lanes], dst.at[slot, oth_rows], m.g_sem.at[slot, 2 * j + 1]))
+        return out
+
+    def wide_phase(y_v):
+        def fetch(c):
+            slot = lax.rem(c, 2)
+            cols = pl.ds(pl.multiple_of(lax.rem(c, per_x) * CHUNK, CHUNK), CHUNK)
+            return [
+                pltpu.make_async_copy(
+                    h.at[c // per_x, :, cols], y_v.at[slot, at], m.h_sem.at[slot, j]
+                )
+                for j, (h, at) in enumerate(((m.h_own, own_rows), (m.h_oth, oth_rows)))
+            ]
+
+        start(fetch(0))
+        wait(stage_cot)
+        pack(0, m.stage.at[own_rows], m.stage.at[oth_rows])
+        start(stage_ffn)
+        start(loads)
+
+        def chunk(c, which):
+            slot = lax.rem(c, 2)
+            wait(fetch(c))
+
+            @pl.when(c + 1 < n_wide)
+            def _():
+                start(fetch(c + 1))
+
+            @pl.when(c >= 2)
+            def _():
+                core_copy(c - 2).wait_send()
+
+            put(m.core_send, slot, slice(None), dot_tn(m.packed[which, 1 - core], y_v[slot]))
+            core_copy(c).start()
+            put(m.kept, slot, slice(None), dot_tn(m.packed[which, core], y_v[slot]))
+
+            @pl.when(c >= 1)
+            def _():
+                add_core(c - 1)
+
+            @pl.when((c >= 1) & (c <= 2))
+            def _():
+                start(first_copies(c - 1))
+
+            @pl.when(c == n_wide - 3)
+            def _():
+                tick(0)
+
+        def first(c, carry):
+            chunk(c, 0)
+            return carry
+
+        lax.fori_loop(0, per_x, first, 0)
+        wait(stage_ffn)
+        pack(1, m.stage.at[own_rows], m.stage.at[oth_rows])
+        start(stage_attn)
+
+        def second(c, carry):
+            chunk(c, 1)
+            return carry
+
+        lax.fori_loop(per_x, n_wide, second, 0)
+        add_core(n_wide - 1)
+        tick(1)
+
+    pl.run_scoped(wide_phase, pltpu.VMEM((2, 2 * rows, CHUNK), BF16))
+    start(tiles(0))
+
+    wait(loads)
+    gf_copy.wait_recv()
+    gain_sum = jnp.zeros((1, width), F32)
+    for i in range(rows // BLOCK):
+        at = slice(i * BLOCK, (i + 1) * BLOCK)
+        grad = m.gres[at, :] + m.gf_recv[at, :].astype(F32)
+        resid = m.resid_v[at, :]
+        inverse = row_norm(resid)
+        normed = resid * inverse
+        gain_sum += jnp.sum(grad * normed, axis=0, keepdims=True)
+        w = grad * m.gain2[...]
+        gres = m.cot_v[at, :].astype(F32) + inverse * (
+            w - normed * jnp.mean(w * normed, axis=-1, keepdims=True)
+        )
+        m.gres[at, :] = gres
+        branch = gres.astype(BF16)
+        m.branch[at, :] = branch
+        m.do_send[at, :] = dot_nt(branch, m.wot_v[...]).astype(BF16)
+    do_copy.start()
+    m.do_own[...] = dot_nt(m.branch[...], m.wom_v[...]).astype(BF16)
+    for r in range(width // PAIR):
+        m.mine[width // PAIR + r : width // PAIR + r + 1, :] = gain_sum[:, r * PAIR : (r + 1) * PAIR]
+    wait(stage_attn)
+    pack(0, m.stage.at[own_rows], m.stage.at[oth_rows])
+    tick(2)
+    do_copy.wait_recv()
+    branch_copy.start()
+    tick(3)
+
+    def narrow_chunk(p):
+        c = n_wide + p
+        slot = lax.rem(c, 2)
+        core_copy(c - 2).wait_send()
+        cols = pl.ds(pl.multiple_of(p * SPLIT, SPLIT), SPLIT)
+        o_cols = pl.ds(pl.multiple_of(p * (CHUNK - SPLIT), CHUNK - SPLIT), CHUNK - SPLIT)
+        for which, dst in ((1 - core, m.core_send), (core, m.kept)):
+            put(dst, slot, slice(0, SPLIT), dot_tn(m.packed[0, which], m.g_v[:, cols]))
+            put(dst, slot, slice(SPLIT, CHUNK), dot_tn(m.packed[1, which], m.o_v[:, o_cols]))
+        core_copy(c).start()
+
+    def place(block):
+        return pl.ds(pl.multiple_of(lax.rem(block + t * (nb // 2), nb) * BLOCK, BLOCK), BLOCK)
+
+    m.qgain[...] = jnp.zeros_like(m.qgain)
+    m.kgain[...] = jnp.zeros_like(m.kgain)
+
+    def attention_phase(qx, dox, kx0, kx1, vx0, vx1, kt, dqt, dk0, dk1, dv0, dv1, dks, dvs):
+        all_low = lane_of((2 * rows, PAIR)) < 64
+        one = jnp.ones((2 * rows, PAIR), F32)
+        zero = jnp.zeros((2 * rows, PAIR), BF16)
+        qx[:, PAIR:] = m.segq[...]
+        kx0[:, PAIR:] = m.segk[...]
+        kx1[:, PAIR:] = m.segk[...]
+        vx0[:, PAIR:] = jnp.where(all_low, -one, 0.0).astype(BF16)
+        vx1[:, PAIR:] = jnp.where(all_low, 0.0, -one).astype(BF16)
+
+        def step(qb, kb, diagonal):
+            qs, ks = place(qb), place(kb)
+            q, do = qx[qs, :], dox[qs, :]
+            for h, (kx, vx, dk, dv) in enumerate(((kx0, vx0, dk0, dv0), (kx1, vx1, dk1, dv1))):
+                s = dot_nt(kx[ks, :], q)
+                if diagonal:
+                    r = lax.broadcasted_iota(jnp.int32, s.shape, 0)
+                    s = jnp.where(r <= lane_of(s.shape), s, -1e30)
+                e = jnp.exp2(s)
+                ds = (e * dot_nt(vx[ks, :], do)).astype(BF16)
+                dv[ks, :] += dot_nn(e.astype(BF16), do[:, :PAIR])
+                dk[ks, :] += dot_nn(ds, q[:, :PAIR])
+                dqt[h * 64 : (h + 1) * 64, qs] += dot_nn(kt[:, ks], ds)
+
+        def group(g, carry):
+            slot = lax.rem(g, 2)
+            lanes = pl.ds(pl.multiple_of(g * PAIR, PAIR), PAIR)
+            p = g // 2
+            wait(tiles(g))
+
+            @pl.when(g + 1 < 4)
+            def _():
+                start(tiles(g + 1))
+
+            qx[:, :PAIR] = m.q_v[slot]
+            k, v = m.kd_v[slot], m.vd_v[slot]
+            kx0[:, :PAIR] = jnp.where(all_low, k, zero)
+            kx1[:, :PAIR] = jnp.where(all_low, zero, k)
+            vx0[:, :PAIR] = jnp.where(all_low, v, zero)
+            vx1[:, :PAIR] = jnp.where(all_low, zero, v)
+            kt[...] = jnp.transpose(k.astype(F32))[:64, :].astype(BF16)
+            for at, do_ref in ((own_rows, m.do_own), (oth_rows, m.do_recv)):
+                scaled = do_ref[:, lanes].astype(F32) * m.linv_v[slot, at, :]
+                dox[at, :PAIR] = scaled.astype(BF16)
+                dox[at, PAIR:] = (scaled * m.o_v[at, lanes].astype(F32)).astype(BF16)
+            for ref in (dqt, dk0, dk1, dv0, dv1):
+                ref[...] = jnp.zeros_like(ref)
+
+            def q_body(qb, c):
+                step(qb, qb, True)
+
+                def k_body(kb, cc):
+                    step(qb, kb, False)
+                    return cc
+
+                lax.fori_loop(jnp.maximum(qb - 2, 0), qb, k_body, 0)
+                return c
+
+            lax.fori_loop(0, nb, q_body, 0)
+
+            g_lanes = pl.ds(pl.multiple_of(p * SPLIT + slot * PAIR, PAIR), PAIR)
+            for at in (own_rows, oth_rows):
+                dq = jnp.transpose(dqt[:, at]) * 0.125
+                normed_grad = rope(dq, m.cos[at, :], -m.sin[at, :])
+                raw = m.qraw_v[slot, at, :].astype(F32)
+                inverse = lax.rsqrt(head_mean(raw * raw) + EPS)
+                u = raw * inverse
+                m.qgain[...] += jnp.sum(normed_grad * u, axis=0, keepdims=True)
+                w = normed_grad * m.qg[...]
+                m.g_v[at, g_lanes] = (inverse * (w - u * head_mean(w * u))).astype(BF16)
+
+            def gathered(a, b, at):
+                joined = jnp.where(low, a[at, :], b[at, :])
+                return joined + pltpu.roll(joined, 64, 1)
+
+            @pl.when(slot == 0)
+            def _():
+                for at in (own_rows, oth_rows):
+                    dks[at, :] = gathered(dk0, dk1, at)
+                    dvs[at, :] = gathered(dv0, dv1, at)
+
+            @pl.when(slot == 1)
+            def _():
+                k_lanes = pl.ds(pl.multiple_of(p * SPLIT + 2 * PAIR, PAIR), PAIR)
+                v_lanes = pl.ds(pl.multiple_of(p * SPLIT + 3 * PAIR, PAIR), PAIR)
+                raw_lanes = pl.ds(pl.multiple_of(p * PAIR, PAIR), PAIR)
+                for at in (own_rows, oth_rows):
+                    dk = jnp.where(low, dks[at, :], gathered(dk0, dk1, at)) * LN2
+                    dv = jnp.where(low, dvs[at, :], gathered(dv0, dv1, at))
+                    normed_grad = rope(dk, m.cos[at, :], -m.sin[at, :])
+                    raw = m.kraw_v[at, raw_lanes].astype(F32)
+                    inverse = lax.rsqrt(head_mean(raw * raw) + EPS)
+                    u = raw * inverse
+                    m.kgain[...] += jnp.sum(normed_grad * u, axis=0, keepdims=True)
+                    w = normed_grad * m.kg[...]
+                    m.g_v[at, k_lanes] = (inverse * (w - u * head_mean(w * u))).astype(BF16)
+                    m.g_v[at, v_lanes] = dv.astype(BF16)
+
+                @pl.when(p == 0)
+                def _():
+                    branch_copy.wait_recv()
+                    y_copy.start()
+                    pack(1, m.branch, m.branch_recv)
+
+                narrow_chunk(p)
+
+            @pl.when(g == 2)
+            def _():
+                add_core(n_wide)
+
+            tick(4 + g)
+            return carry
+
+        lax.fori_loop(0, 4, group, 0)
+
+    pl.run_scoped(
+        attention_phase,
+        *[pltpu.VMEM((2 * rows, 2 * PAIR), BF16)] * 6,
+        pltpu.VMEM((64, 2 * rows), BF16), pltpu.VMEM((PAIR, 2 * rows), F32),
+        *[pltpu.VMEM((2 * rows, PAIR), F32)] * 6,
+    )
+
+    def attn_in_grad(at):
+        out = None
+        qc, kc = m.wq_v.shape[1], m.wkv_v.shape[1] // 2
+        for p in range(2):
+            for ref, base, begin, size in (
+                (m.wq_v, 0, 0, 2 * PAIR), (m.wkv_v, 0, 2 * PAIR, PAIR), (m.wkv_v, kc, 3 * PAIR, PAIR)
+            ):
+                term = dot_nt(
+                    m.g_v[at, p * SPLIT + begin : p * SPLIT + begin + size],
+                    ref[:, base + p * size : base + (p + 1) * size],
+                )
+                out = term if out is None else out + term
+        return out
+
+    def end_phase(ga_own, y_v, y_other):
+        tok_v, out_v = m.stage, m.cot_v
+        start(both(0, m.tok_own, m.tok_oth, tok_v))
+        load_y = local(2, m.y_own, y_v)
+        load_y.start()
+        wait(both(0, m.tok_own, m.tok_oth, tok_v))
+
+        def grad_and_gain(at):
+            grad = attn_in_grad(at)
+            tokens = tok_v[at, :].astype(F32)
+            return grad, jnp.sum(grad * (tokens * row_norm(tokens)), axis=0, keepdims=True)
+
+        branch_copy.wait_send()
+        total = jnp.zeros((1, width), F32)
+        for i in range(rows // BLOCK):
+            grad, part = grad_and_gain(pl.ds(rows + i * BLOCK, BLOCK))
+            m.branch[i * BLOCK : (i + 1) * BLOCK, :] = grad.astype(BF16)
+            total += part
+        ga_copy.start()
+        add_core(n_chunks - 1)
+        tick(n_chunks - 3)
+        for i in range(rows // BLOCK):
+            grad, part = grad_and_gain(pl.ds(i * BLOCK, BLOCK))
+            ga_own[i * BLOCK : (i + 1) * BLOCK, :] = grad
+            total += part
+        for r in range(width // PAIR):
+            m.mine[r : r + 1, :] = total[:, r * PAIR : (r + 1) * PAIR]
+        last = 2 * width // PAIR
+        m.mine[last : last + 1, :] = m.qgain[...]
+        m.mine[last + 1 : last + 2, :] = m.kgain[...]
+        m.mine[last + 2 :, :] = jnp.zeros((m.mine.shape[0] - last - 2, PAIR), F32)
+
+        def gain_copy(i, device):
+            return pltpu.make_async_remote_copy(
+                src_ref=m.gain_out.at[i], dst_ref=m.gain_in.at[i], send_sem=m.gain_sem.at[0, i],
+                recv_sem=m.gain_sem.at[1, i], device_id=device, device_id_type=MESH,
+            )
+
+        for i, device in enumerate(partners):
+            m.gain_out[i] = m.mine[...]
+            gain_copy(i, device).start()
+            if i == 2:
+                y_copy.wait_recv()
+                load_y.wait()
+                arrived = local(4, m.y_recv, y_other)
+                arrived.start()
+                arrived.wait()
+                out_v[...] = (m.resid_v[...] + y_v[...] + y_other[...].astype(F32)).astype(BF16)
+                local(3, out_v, m.output).start()
+            if i >= 1:
+                tick(n_chunks - 3 + i)
+            gain_copy(i, device).wait_recv()
+            m.mine[...] += m.gain_in[i]
+        m.gains[...] = m.mine[...]
+        ga_copy.wait_recv()
+        for i in range(rows // PAIR):
+            at = slice(i * PAIR, (i + 1) * PAIR)
+            tokens = tok_v[at, :].astype(F32)
+            inverse = row_norm(tokens)
+            normed = tokens * inverse
+            w = (ga_own[at, :] + m.gf_recv[at, :].astype(F32)) * m.gain1[...]
+            ga_own[at, :] = m.gres[at, :] + inverse * (
+                w - normed * jnp.mean(w * normed, axis=-1, keepdims=True)
+            )
+            local(4 + i, ga_own.at[pl.ds(i * PAIR, PAIR)], m.grad_tokens.at[pl.ds(i * PAIR, PAIR)]).start()
+        for copy in (gf_copy, do_copy, y_copy, ga_copy):
+            copy.wait_send()
+        for i, device in enumerate(partners):
+            gain_copy(i, device).wait_send()
+        for c in (n_chunks - 2, n_chunks - 1):
+            core_copy(c).wait_send()
+
+        def drain(c, carry):
+            for copy in (*first_copies(c), *second_copies(c), third_copy(c)):
+                copy.wait_send()
+            return carry
+
+        lax.fori_loop(0, n_chunks, drain, 0)
+        local(3, out_v, m.output).wait()
+        for i in range(rows // PAIR):
+            local(4 + i, ga_own.at[pl.ds(i * PAIR, PAIR)], m.grad_tokens.at[pl.ds(i * PAIR, PAIR)]).wait()
+        for c in (n_chunks - 2, n_chunks - 1):
+            total_copy(c).wait()
+
+    pl.run_scoped(
+        end_phase,
+        pltpu.VMEM((rows, width), F32), pltpu.VMEM((rows, width), F32), pltpu.VMEM((rows, width), BF16),
+    )
+
+
+def back(n_dp, values, tables):
+    rows, width = values["resid"].shape
+    hidden = values["h_own"].shape[2]
+    seq = 2 * rows
+    qc = values["w_q"].shape[1]
+    n_chunks = 3 * hidden // CHUNK + 2
+    block = width // n_dp
+    vm = pltpu.VMEM
+    dma = pltpu.SemaphoreType.DMA
+    scratch = dict(
+        stage=vm((seq, width), BF16), packed=vm((2, 2, seq, width // 2), BF16),
+        core_send=vm((2, 2, 2, 2, block, CHUNK), BF16), kept=vm((2, 2, 2, 2, block, CHUNK), BF16),
+        sums=vm((n_chunks, 2, 2, 2, block, CHUNK), BF16),
+        r1a=vm((n_chunks, 2, 2, block, SPLIT), BF16), r1b=vm((n_chunks, 2, 2, block, CHUNK - SPLIT), BF16),
+        r2a=vm((n_chunks, 2, block, SPLIT), BF16), r2b=vm((n_chunks, 2, block, CHUNK - SPLIT), BF16),
+        r3=vm((n_chunks, block, CHUNK), BF16), totals=vm((2, block, CHUNK), F32),
+        gres=vm((rows, width), F32), resid_v=vm((rows, width), F32), cot_v=vm((rows, width), BF16),
+        wom_v=vm((qc, width), BF16), wot_v=vm((qc, width), BF16),
+        wq_v=vm((width, qc), BF16), wkv_v=vm((width, qc), BF16),
+        o_v=vm((seq, qc), BF16), kraw_v=vm((seq, qc // 2), BF16),
+        q_v=vm((2, seq, PAIR), BF16), kd_v=vm((2, seq, PAIR), BF16), vd_v=vm((2, seq, PAIR), BF16),
+        qraw_v=vm((2, seq, PAIR), BF16), linv_v=vm((2, seq, PAIR), F32),
+        g_v=vm((seq, 2 * SPLIT), BF16), do_own=vm((rows, qc), BF16),
+        gf_recv=vm((rows, width), BF16), do_send=vm((rows, qc), BF16), do_recv=vm((rows, qc), BF16),
+        branch=vm((rows, width), BF16), branch_recv=vm((rows, width), BF16),
+        qgain=vm((1, PAIR), F32), kgain=vm((1, PAIR), F32), mine=vm((24, PAIR), F32),
+        gain_out=vm((5, 24, PAIR), F32), gain_in=vm((5, 24, PAIR), F32),
+        t_send=dma((5,)), t_recv=dma((5,)), rs_send=dma((6, n_chunks)), rs_recv=dma((6, n_chunks)),
+        l_sem=dma((13,)), g_sem=dma((2, 10)), h_sem=dma((2, 2)), s_sem=dma((2,)), gain_sem=dma((2, 5)),
+    )
+    anywhere = pl.BlockSpec(memory_space=pl.ANY)
+    vmem = pl.BlockSpec(memory_space=pltpu.VMEM)
+    return pl.pallas_call(
+        functools.partial(back_kernel, n_dp, tuple(scratch)),
+        in_specs=[anywhere] * len(BACK_INPUTS) + [vmem] * len(BACK_TABLES),
+        out_specs=[anywhere, anywhere, anywhere, vmem, anywhere],
+        out_shape=[
+            jax.ShapeDtypeStruct((rows, width), BF16), jax.ShapeDtypeStruct((rows, width), F32),
+            jax.ShapeDtypeStruct((n_chunks, block, CHUNK), F32), jax.ShapeDtypeStruct((24, PAIR), F32),
+            jax.ShapeDtypeStruct((rows, width), BF16),
+        ],
+        scratch_shapes=list(scratch.values()),
+        compiler_params=pltpu.CompilerParams(
+            vmem_limit_bytes=BACK_VMEM, collective_id=0, has_side_effects=True
+        ),
+        cost_estimate=cost(100e-6),
+        name="back",
+    )(*[values[k] for k in BACK_INPUTS], *[tables[k] for k in BACK_TABLES])
+
+
+def swap(value, axis, size, bit):
+    return lax.ppermute(value, axis, [(i, i ^ bit) for i in range(size)])
+
+
+def after(value, *others):
+    return lax.optimization_barrier((value,) + others)[0]
+
+
+def paired(
+    n_dp, tokens, doc_ids, gain_attn, w_q, w_kv, q_gain, k_gain, w_o, gain_ffn, w_gu, w_down, cotangent
+):
+    rows, width = tokens.shape
+    head_dim = q_gain.shape[0]
+    hidden = w_down.shape[0]
+    seq = doc_ids.shape[1]
+    t = lax.axis_index("tensor")
+    d = lax.axis_index("dp")
+    over = functools.partial(swap, axis="tensor", size=2, bit=1)
+
+    tokens_oth = over(tokens)
+    w_o_oth = over(after(w_o, tokens_oth))
+    cot_oth = over(after(cotangent, tokens_oth))
+
+    segment = doc_ids[0]
+    nb = seq // BLOCK
+    heads_of_blocks = segment.reshape(nb, BLOCK)
+    first_doc, last_doc = heads_of_blocks[:, 0], heads_of_blocks[:, -1]
+    below = jnp.arange(nb)[None, :] < jnp.arange(nb)[:, None]
+    lowest = jnp.sum((below & (last_doc[None, :] < first_doc[:, None])).astype(jnp.int32), axis=1)
+    shift = t * (nb // 2)
+    table = lambda first: jnp.concatenate([jnp.stack([shift, first]).astype(jnp.int32), lowest])
+    scalars_own = table(shift)
+    scalars_oth = table(nb // 2 - shift)
+    segment = jnp.where(t == 0, segment, jnp.roll(segment, rows))
+    lanes = jnp.arange(PAIR, dtype=jnp.int32)[None, :]
+    match = lanes == segment[:, None]
+    marker = lanes == 8
+    segk = (match | marker).astype(BF16)
+    segq = (jnp.where(match, SAME, 0.0) - jnp.where(marker, SAME, 0.0)).astype(BF16)
+    half_dim = head_dim // 2
+    frequency = jnp.exp(-math.log(THETA) * 2.0 * jnp.arange(half_dim, dtype=F32) / head_dim)
+    position = (jnp.arange(seq, dtype=jnp.int32) + t * rows) % seq
+    angles = position.astype(F32)[:, None] * frequency[None, :]
+    cos, sin = jnp.cos(angles), jnp.sin(angles)
+    cosine = jnp.concatenate([cos] * 4, axis=1)
+    sine = jnp.concatenate([-sin, sin] * 2, axis=1)
+    gain1, gain2 = gain_attn.reshape(1, width), gain_ffn.reshape(1, width)
+    qg = jnp.concatenate([q_gain, q_gain]).reshape(1, PAIR)
+    kg = jnp.concatenate([k_gain, k_gain]).reshape(1, PAIR)
+    w_kv = w_kv.reshape(width, -1)
+    w_gu = w_gu.reshape(width, 2 * hidden)
+    core = (d & 1).astype(jnp.int32).reshape(1)
+
+    attn_own, q_own, kd_own, vd_own, qraw_own, kraw_own = qkv(
+        tokens, gain1, w_q, w_kv, qg, kg, cosine, sine, 0
+    )
+    attn_oth, q_oth, kd_oth, vd_oth, qraw_oth, kraw_oth = qkv(
+        tokens_oth, gain1, w_q, w_kv, qg, kg, cosine, sine, 1
+    )
+    o_oth, linv_oth = attn_fwd(scalars_oth, q_oth, kd_own, kd_oth, vd_own, vd_oth, segq, segk, 1)
+    theirs = over(o_oth)
+    o_own, linv_own = attn_fwd(scalars_own, q_own, kd_own, kd_oth, vd_own, vd_oth, segq, segk, 0)
+    resid, ffn_own = resid_norm(o_own, theirs, w_o, w_o_oth, tokens, gain2)
+
+    ffn_oth = over(ffn_own)
+    h_own, y_own, gf_own = ffn(ffn_own, cotangent, w_gu, w_down, F32)
+    h_oth, y_oth, gf_oth = ffn(after(ffn_oth, gf_own), cot_oth, w_gu, w_down, BF16)
+
+    output, grad_tokens, shards, gains, _ = back(
+        n_dp,
+        dict(
+            h_own=h_own, h_oth=h_oth, cot_own=cotangent, cot_oth=cot_oth, ffn_own=ffn_own, ffn_oth=ffn_oth,
+            attn_own=attn_own, attn_oth=attn_oth, tok_own=tokens, tok_oth=tokens_oth,
+            gf_own=gf_own, gf_send=gf_oth, y_own=y_own, y_send=y_oth, resid=resid,
+            wo_mine=w_o, wo_oth=w_o_oth, w_q=w_q, w_kv=w_kv,
+            q_own=q_own, q_oth=q_oth, kd_own=kd_own, kd_oth=kd_oth, vd_own=vd_own, vd_oth=vd_oth,
+            o_own=o_own, o_oth=o_oth, linv_own=linv_own, linv_oth=linv_oth,
+            qraw_own=qraw_own, qraw_oth=qraw_oth, kraw_own=kraw_own, kraw_oth=kraw_oth,
+        ),
+        dict(segq=segq, segk=segk, cos=cosine, sin=sine, gain1=gain1, gain2=gain2, qg=qg, kg=kg),
+    )
+    m = width // PAIR
+    per_x = hidden // CHUNK
+    fold = lambda row: row[:head_dim] + row[head_dim:]
+    side = lambda i: jnp.concatenate([shards[i * per_x + j] for j in range(per_x)], axis=1)
+    pairs = [shards[3 * per_x + p] for p in range(2)]
+    join = lambda a, b: jnp.concatenate([pair[:, a:b] for pair in pairs], axis=1)
+    return (
+        output,
+        grad_tokens,
+        gains[:m].reshape(width),
+        join(0, 2 * PAIR),
+        jnp.stack([join(2 * PAIR, 3 * PAIR), join(3 * PAIR, 4 * PAIR)], axis=1),
+        fold(gains[2 * m]),
+        fold(gains[2 * m + 1]),
+        join(SPLIT, CHUNK).T,
+        gains[m : 2 * m].reshape(width),
+        jnp.stack([side(1), side(2)], axis=1),
+        side(0).T,
+    )
 
 
 def normalize(values):
@@ -261,4 +1233,6 @@
         P("dp", None, "tensor"),
         P("tensor", "dp"),
     )
-    return jax.shard_map(shards, mesh=mesh, in_specs=in_specs, out_specs=out_specs, check_vma=False)
+    paired_axes = mesh.shape["tensor"] == 2 and mesh.shape["dp"] == 16
+    body = functools.partial(paired, mesh.shape["dp"]) if paired_axes else shards
+    return jax.shard_map(body, mesh=mesh, in_specs=in_specs, out_specs=out_specs, check_vma=False)

time: 839 us -> 309 us (0.37)
  waiting for transfers between devices: 408 us -> 30.1 us
  Pallas kernels: 0 us -> 234 us
  matrix products: 203 us -> 0 us
  local copies, waits for them, and re-layouts: 89.2 us -> 20.3 us
  other arithmetic: 65.1 us -> 12.8 us
  blocking collectives: 39.8 us -> 0 us
  between operations: 15.9 us -> 1.02 us
    pallas_call x0 -> x8, Pallas kernels: none -> 234 us  [the longest x1 152 us: back(): pl.pallas_call(functools.partial(back_kernel, n_dp, tuple(scratch)), in_s...]
    dot_general x29 -> x0, matrix products: 203 us -> none  [the longest x4 30.9 us: scores_of(): jnp.einsum('qhgd,thd->hgqt', q_block, keys, preferred_element_type=f32)]
    unnamed x13 -> x0, waiting for transfers between devices: 195 us -> none
    reduce_scatter x7 -> x0, waiting for transfers between devices: 116 us -> none  [the longest x1 54.4 us: shards(): lax.psum_scatter(jnp.dot(attended_low, w_o, preferred_element_type=f32),...]
    all_gather x4 -> x0, waiting for transfers between devices: 96.7 us -> none  [the longest x1 33.9 us: shards(): attn_all = lax.all_gather(attn_in, 'tensor', axis=0, tiled=True)]
    dynamic_update_slice x4 -> x0, local copies, waits for them, and re-layouts: 41.2 us -> none  [shards(): attended, log_sums = lax.map(attend, starts)]
    psum x1 -> x0, blocking collectives: 39.8 us -> none  [shards(): lax.psum((gain_attn_part, gain_ffn_part, q_gain_part, k_gain_part), ('dp'...]
    ppermute x0 -> x5, waiting for transfers between devices: none -> 30.1 us  [swap(): return lax.ppermute(value, axis, [(i, i ^ bit) for i in range(size)])]
  transfers between devices with their start and end apart: 12 -> 5, of which waited for: 8 -> 3; matrix products, arithmetic and copies ran while one was open for 31% -> 7% of each run, Pallas kernels for 0% -> 18%
where the time goes in v2:
time: 309 us; the launch traced here: 306 us
  Pallas kernels  234 us (76%)
  waiting for transfers between devices  30.1 us (10%)
  local copies, waits for them, and re-layouts  20.3 us (7%)
  other arithmetic  12.8 us (4%)
  starting transfers between devices  7.09 us (2%)
    pallas_call x1, Pallas kernels, back(): pl.pallas_call(functools.partial(back_kernel, n_dp, tuple(scratch)), in_s...  152 us
    pallas_call x2, Pallas kernels, ffn(): pl.pallas_call(ffn_kernel, grid=(nf,), in_specs=[whole, whole, pl.BlockSp...  45.5 us
    ppermute x5, waiting for transfers between devices, swap(): return lax.ppermute(value, axis, [(i, i ^ bit) for i in range(size)])  30.1 us
    pallas_call x2, Pallas kernels, attn_fwd(): pl.pallas_call(attn_fwd_kernel, grid_spec=pltpu.PrefetchScalarGridSpec(nu...  19.6 us
    unnamed x29, local copies, waits for them, and re-layouts  17.1 us
    pallas_call x2, Pallas kernels, qkv(): pl.pallas_call(qkv_kernel, grid=(nb,), in_specs=[row(width), whole((1, wi...  12.1 us
    ppermute x5, starting transfers between devices, swap(): return lax.ppermute(value, axis, [(i, i ^ bit) for i in range(size)])  7.09 us
  transfers between devices with their start and end apart: 5, of which 3 were waited for; matrix products, arithmetic and copies ran while one was open for 7% of the time, Pallas kernels for 18%

profile of v2, /device:TPU:0, one launch (start us, length us, event | category | flops | bytes accessed | tf_op | source)
XLA Modules:
  0.0 305.8 jit_solution(9796081147022940454)
XLA Ops:
  0.6 3.0 collective-permute-start
  3.7 0.5 broadcast.63
  4.2 1.3 reduce.3
  5.5 0.1 fusion.14
  5.6 0.1 copy.37
  5.7 0.1 copy.36
  5.8 1.3 maximum_bitcast_fusion.6
  7.1 0.2 convert_reduce_fusion
  7.3 0.6 add_add_fusion.1
  7.9 0.0 copy-start.9
  7.9 0.0 copy-start
  8.0 0.0 copy-start.6
  8.0 1.9 fusion.2
  9.9 1.8 pad_maximum_fusion.1
  11.7 15.3 %collective-permute-done.x_ref.refs_9_ = bf16[512,1024]{1,0:T(8,128)(2,1)S(1)} collective-permute-done((bf16[512,1024]{1,0:T(8,128)(2,1)}, bf16[512,1024]{1,0:T(8,128)(2,1)S(1)}, u32[]{:S(2)}, u32[]{:S(2)}) %collective-permute-start) | collective-permute-done | bytes 1048608 | tf_op jit(solution)/shard_map/ppermute | solution.py:883
  27.1 1.7 collective-permute-start.2
  28.8 1.2 copy.38
  30.0 6.1 %qkv.2 = (bf16[512,1024]{1,0:T(8,128)(2,1)}, bf16[512,512]{1,0:T(8,128)(2,1)}, bf16[512,512]{1,0:T(8,128)(2,1)}, bf16[512,512]{1,0:T(8,128)(2,1)}, bf16[512,512]{1,0:T(8,128)(2,1)}, /*index=5*/bf16[512,256]{1,0:T(8,128)(2,1)}) custom-call(bf16[512,1024]{1,0:T(8,128)(2,1)} %refs_8_.1, f32[1,1024]{1,0:T(1,128)} %bitcast.71, bf16[1024,512]{1,0:T(8,128)(2,1)} %refs_17_.1, ...), custom_call_target="tpu_custom_call" | custom-call | flops 50000000 | tf_op jit(solution)/shard_map/qkv/pallas_call | solution.py:100
  36.1 0.9 fusion.1.segk_ref.refs_34_
  37.0 0.9 subtract_convert_fusion.segq_ref.refs_33_
  37.9 6.0 %qkv.3 = (bf16[512,1024]{1,0:T(8,128)(2,1)}, bf16[512,512]{1,0:T(8,128)(2,1)}, bf16[512,512]{1,0:T(8,128)(2,1)}, bf16[512,512]{1,0:T(8,128)(2,1)}, bf16[512,512]{1,0:T(8,128)(2,1)}, /*index=5*/bf16[512,256]{1,0:T(8,128)(2,1)}) custom-call(bf16[512,1024]{1,0:T(8,128)(2,1)} %copy-done.2, f32[1,1024]{1,0:T(1,128)} %bitcast.72, bf16[1024,512]{1,0:T(8,128)(2,1)} %refs_17_.1, ...), custom_call_target="tpu_custom_call" | custom-call | flops 50000000 | tf_op jit(solution)/shard_map/qkv/pallas_call | solution.py:100
  43.9 9.8 %attn_fwd.3 = (bf16[512,512]{1,0:T(8,128)(2,1)}, f32[512,512]{1,0:T(8,128)}) custom-call(s32[6]{0:T(128)} %get-tuple-element.136.s_ref, bf16[512,512]{1,0:T(8,128)(2,1)} %get-tuple-element.48.q_ref.refs_20_, bf16[512,512]{1,0:T(8,128)(2,1)} %get-tuple-element.43.kown_ref.refs_21_, bf16[512,512]{1,0:T(8,128)(2,1)} %get-tuple-element.44.koth_ref.refs_22_, ...), custom_call_target="tpu_custom_call" | custom-call | flops 100000000 | tf_op jit(solution)/shard_map/attn_fwd/pallas_call | solution.py:178
  53.7 0.3 collective-permute-start.1
  54.0 9.9 %attn_fwd.2 = (bf16[512,512]{1,0:T(8,128)(2,1)}, f32[512,512]{1,0:T(8,128)}) custom-call(s32[6]{0:T(128)} %get-tuple-element.137.s_ref, bf16[512,512]{1,0:T(8,128)(2,1)} %get-tuple-element.42.q_ref.refs_19_, bf16[512,512]{1,0:T(8,128)(2,1)} %get-tuple-element.43.kown_ref.refs_21_, bf16[512,512]{1,0:T(8,128)(2,1)} %get-tuple-element.44.koth_ref.refs_22_, ...), custom_call_target="tpu_custom_call" | custom-call | flops 100000000 | tf_op jit(solution)/shard_map/attn_fwd/pallas_call | solution.py:178
  63.8 3.0 collective-permute-done.1.theirs_ref
  66.8 0.0 collective-permute-done.2.wt_ref.refs_16_
  66.8 0.8 copy-done.8
  67.6 0.4 copy-done.3
  68.0 4.8 %resid.1 = (f32[512,1024]{1,0:T(8,128)}, bf16[512,1024]{1,0:T(8,128)(2,1)}) custom-call(bf16[512,512]{1,0:T(8,128)(2,1)} %get-tuple-element.47.mine_ref.refs_25_, bf16[512,512]{1,0:T(8,128)(2,1)} %copy-done.8, bf16[512,1024]{1,0:T(8,128)(2,1)} %refs_15_.1, bf16[512,1024]{1,0:T(8,128)(2,1)} %copy-done.3, bf16[512,1024]{1,0:T(8,128)(2,1)} %refs_8_.1, ...), custom_call_target="tpu_custom_call" | custom-call | flops 40000000 | tf_op jit(solution)/shard_map/resid/pallas_call | solution.py:217
  72.8 0.3 collective-permute-start.3
  73.1 1.7 collective-permute-start.4
  74.8 9.0 %copy.39 = bf16[128,8,2,2304]{3,1,2,0:T(8,128)(2,1)} copy(bf16[128,8,2,2304]{3,2,1,0:T(2,128)(2,1)} %bitcast.68) | data formatting | bytes 18874368
  83.8 23.3 %ffn.2 = (bf16[3,512,2304]{2,1,0:T(8,128)(2,1)}, f32[512,1024]{1,0:T(8,128)}, f32[512,1024]{1,0:T(8,128)}) custom-call(bf16[512,1024]{1,0:T(8,128)(2,1)} %get-tuple-element.51.x_ref.refs_4_, bf16[512,1024]{1,0:T(8,128)(2,1)} %refs_2_.1, bf16[1024,4608]{1,0:T(8,128)(2,1)} %bitcast.59, bf16[1024,4608]{1,0:T(8,128)(2,1)} %bitcast.60, bf16[2304,1024]{1,0:T(8,128)(2,1)} %wd_ref.3), custom_call_target="tpu_custom_call" | custom-call | flops 200000000 | tf_op jit(solution)/shard_map/ffn/pallas_call | solution.py:268
  107.1 0.0 collective-permute-done.3.x_ref.refs_5_
  107.1 11.8 %collective-permute-done.4.c_ref.refs_3_ = bf16[512,1024]{1,0:T(8,128)(2,1)} collective-permute-done((bf16[512,1024]{1,0:T(8,128)(2,1)S(1)}, bf16[512,1024]{1,0:T(8,128)(2,1)}, u32[]{:S(2)}, u32[]{:S(2)}) %collective-permute-start.4) | collective-permute-done | bytes 1048608 | tf_op jit(solution)/shard_map/ppermute | solution.py:883
  118.9 22.3 %ffn.3 = (bf16[3,512,2304]{2,1,0:T(8,128)(2,1)}, bf16[512,1024]{1,0:T(8,128)(2,1)}, bf16[512,1024]{1,0:T(8,128)(2,1)}) custom-call(bf16[512,1024]{1,0:T(8,128)(2,1)} %copy-done.4, bf16[512,1024]{1,0:T(8,128)(2,1)} %collective-permute-done.4.c_ref.refs_3_, bf16[1024,4608]{1,0:T(8,128)(2,1)} %bitcast.61, bf16[1024,4608]{1,0:T(8,128)(2,1)} %bitcast.62, ...), custom_call_target="tpu_custom_call" | custom-call | flops 200000000 | tf_op jit(solution)/shard_map/ffn/pallas_call | solution.py:268
  141.2 152.4 %back.1 = (bf16[512,1024]{1,0:T(8,128)(2,1)}, f32[512,1024]{1,0:T(8,128)}, f32[11,64,768]{2,1,0:T(8,128)}, f32[24,128]{1,0:T(8,128)}, bf16[512,1024]{1,0:T(8,128)(2,1)}) custom-call(bf16[3,512,2304]{2,1,0:T(8,128)(2,1)} %get-tuple-element.52.refs_0_, bf16[3,512,2304]{2,1,0:T(8,128)(2,1)} %get-tuple-element.56.refs_1_, bf16[512,1024]{1,0:T(8,128)(2,1)} %refs_2_.1, ...), custom_call_target="tpu_custom_call" | custom-call | flops 1000000000 | tf_op jit(solution)/shard_map/back/pallas_call | solution.py:864
  293.6 1.4 add_bitcast_fusion
  295.0 1.3 slice_bitcast_fusion.11
  296.3 1.8 slice_bitcast_fusion.2
  298.2 0.8 copy.34
  299.1 0.1 pad_maximum_fusion
  299.2 1.9 copy.35
  301.1 0.7 maximum_bitcast_fusion.3
  301.8 0.7 pad_maximum_fusion.3
  302.4 0.9 maximum_bitcast_fusion.2
  303.3 1.0 copy.42
  304.2 1.3 copy.43
  (31 shorter events, 0.2 us)
Async XLA Ops:
  0.6 26.4 %collective-permute-start = (bf16[512,1024]{1,0:T(8,128)(2,1)}, bf16[512,1024]{1,0:T(8,128)(2,1)S(1)}, u32[]{:S(2)}, u32[]{:S(2)}) collective-permute-start(bf16[512,1024]{1,0:T(8,128)(2,1)} %refs_8_.1), channel_id=1, source_target_pairs={{0,1},{1,0},{2,3},{3,2},{4,5},{5,4},{6,7},{7,6},{8,9},{9,8},{10,11... | collective-permute-start | bytes 3145736 | tf_op jit(solution)/shard_map/ppermute | solution.py:883
  7.9 3.8 %copy-start.9 = (s32[1,1024]{1,0:T(1,128)S(1)}, s32[1,1024]{1,0:T(1,128)}, u32[]{:S(2)}) copy-start(s32[1,1024]{1,0:T(1,128)} %param.13) | copy-start | bytes 12292
  7.9 19.1 %copy-start = (bf16[512,1024]{1,0:T(8,128)(2,1)S(1)}, bf16[512,1024]{1,0:T(8,128)(2,1)}, u32[]{:S(2)}) copy-start(bf16[512,1024]{1,0:T(8,128)(2,1)} %refs_15_.1) | copy-start | bytes 3145732
  8.0 20.8 %copy-start.6 = (bf16[1024,2,256]{2,1,0:T(2,128)(2,1)S(1)}, bf16[1024,2,256]{2,1,0:T(2,128)(2,1)}, u32[]{:S(2)}) copy-start(bf16[1024,2,256]{2,1,0:T(2,128)(2,1)} %param.16) | copy-start | bytes 3145732
  27.0 9.1 %copy-start.2 = (bf16[512,1024]{1,0:T(8,128)(2,1)}, bf16[512,1024]{1,0:T(8,128)(2,1)S(1)}, u32[]{:S(2)}) copy-start(bf16[512,1024]{1,0:T(8,128)(2,1)S(1)} %collective-permute-done.x_ref.refs_9_) | copy-start | bytes 3145732
  27.1 39.8 %collective-permute-start.2 = (bf16[512,1024]{1,0:T(8,128)(2,1)S(1)}, bf16[512,1024]{1,0:T(8,128)(2,1)S(1)}, u32[]{:S(2)}, u32[]{:S(2)}) collective-permute-start(bf16[512,1024]{1,0:T(8,128)(2,1)S(1)} %copy-done), channel_id=1, source_target_pairs={{0,1},{1,0},{2,3},{3,2},{4,5},{5,4},{6,7},{7,6},{8,9},{9,8},{10,11... | collective-permute-start | bytes 3145736 | tf_op jit(solution)/shard_map/ppermute | solution.py:883
  53.7 13.1 %collective-permute-start.1 = (bf16[512,512]{1,0:T(8,128)(2,1)}, bf16[512,512]{1,0:T(8,128)(2,1)S(1)}, u32[]{:S(2)}, u32[]{:S(2)}) collective-permute-start(bf16[512,512]{1,0:T(8,128)(2,1)} %get-tuple-element.49.refs_26_), channel_id=1, source_target_pairs={{0,1},{1,0},{2,3},{3,2},{4,5},{5,4},{6,7},{7,6},{8,9},{9,8},{10,11... | collective-permute-start | bytes 1572872 | tf_op jit(solution)/shard_map/ppermute | solution.py:883
  66.8 0.8 copy-start.8
  66.8 1.2 copy-start.3
  68.0 5.1 %copy-start.1 = (bf16[512,1024]{1,0:T(8,128)(2,1)S(1)}, bf16[512,1024]{1,0:T(8,128)(2,1)}, u32[]{:S(2)}) copy-start(bf16[512,1024]{1,0:T(8,128)(2,1)} %refs_2_.1) | copy-start | bytes 3145732
  72.8 34.3 %collective-permute-start.3 = (bf16[512,1024]{1,0:T(8,128)(2,1)}, bf16[512,1024]{1,0:T(8,128)(2,1)S(1)}, u32[]{:S(2)}, u32[]{:S(2)}) collective-permute-start(bf16[512,1024]{1,0:T(8,128)(2,1)} %get-tuple-element.51.x_ref.refs_4_), channel_id=1, source_target_pairs={{0,1},{1,0},{2,3},{3,2},{4,5},{5,4},{6,7},{7,6},{8,9},{9,8},{10,11... | collective-permute-start | bytes 3145736 | tf_op jit(solution)/shard_map/ppermute | solution.py:883
  73.1 45.8 %collective-permute-start.4 = (bf16[512,1024]{1,0:T(8,128)(2,1)S(1)}, bf16[512,1024]{1,0:T(8,128)(2,1)}, u32[]{:S(2)}, u32[]{:S(2)}) collective-permute-start(bf16[512,1024]{1,0:T(8,128)(2,1)S(1)} %copy-done.1), channel_id=1, source_target_pairs={{0,1},{1,0},{2,3},{3,2},{4,5},{5,4},{6,7},{7,6},{8,9},{9,8},{10,11... | collective-permute-start | bytes 3145736 | tf_op jit(solution)/shard_map/ppermute | solution.py:883
  107.1 11.8 %copy-start.4 = (bf16[512,1024]{1,0:T(8,128)(2,1)}, bf16[512,1024]{1,0:T(8,128)(2,1)S(1)}, u32[]{:S(2)}) copy-start(bf16[512,1024]{1,0:T(8,128)(2,1)S(1)} %collective-permute-done.3.x_ref.refs_5_) | copy-start | bytes 3145732
  299.2 4.1 %copy-start.7 = (bf16[512,1024]{1,0:T(8,128)(2,1)S(1)}, bf16[512,1024]{1,0:T(8,128)(2,1)}, u32[]{:S(2)}) copy-start(bf16[512,1024]{1,0:T(8,128)(2,1)} %get-tuple-element.153) | copy-start | bytes 3145732
  301.1 3.2 %copy-start.5 = (f32[512,1024]{1,0:T(8,128)S(1)}, f32[512,1024]{1,0:T(8,128)}, u32[]{:S(2)}) copy-start(f32[512,1024]{1,0:T(8,128)} %get-tuple-element.154) | copy-start | bytes 6291460

commit v3 on v2

--- a/solution.py
+++ b/solution.py
@@ -115,193 +115,34 @@
     )(x, gain, w_q, w_kv, w_kv, qg, kg, cosine, sine)
 
 
-def attn_fwd_kernel(
-    s_ref, q_ref, kown_ref, koth_ref, vown_ref, voth_ref, segq_ref, segk_ref,
-    o_ref, linv_ref, kx0, kx1, vx0, vx1, acc,
-):
-    rows = q_ref.shape[0]
-    own = s_ref[0]
-    first = s_ref[1]
-    nb = rows // BLOCK
-    low = lane_of((rows, PAIR)) < 64
-    zero = jnp.zeros((rows, PAIR), BF16)
-
-    @pl.when(pl.program_id(0) == 0)
-    def _():
-        one = jnp.ones((2 * rows, PAIR), F32)
-        both = lane_of((2 * rows, PAIR)) < 64
-        kx0[:, PAIR:] = segk_ref[...]
-        kx1[:, PAIR:] = segk_ref[...]
-        vx0[:, PAIR:] = jnp.where(both, one, 0.0).astype(BF16)
-        vx1[:, PAIR:] = jnp.where(both, 0.0, one).astype(BF16)
-
-    for part, (k_ref, v_ref) in enumerate(((kown_ref, vown_ref), (koth_ref, voth_ref))):
-        at = slice(part * rows, (part + 1) * rows)
-        kx0[at, :PAIR] = jnp.where(low, k_ref[...], zero)
-        kx1[at, :PAIR] = jnp.where(low, zero, k_ref[...])
-        vx0[at, :PAIR] = jnp.where(low, v_ref[...], zero)
-        vx1[at, :PAIR] = jnp.where(low, zero, v_ref[...])
-
-    for i in range(nb):
-        at = slice(i * BLOCK, (i + 1) * BLOCK)
-        q = jnp.concatenate([q_ref[at, :], segq_ref[at, :]], axis=1)
-        block = first + i
-
-        def step(kb, diagonal):
-            here = pl.ds(pl.multiple_of(lax.rem(kb + own, 2 * nb) * BLOCK, BLOCK), BLOCK)
-            total = None
-            for kx, vx in ((kx0, vx0), (kx1, vx1)):
-                s = dot_nt(q, kx[here, :])
-                if diagonal:
-                    r = lax.broadcasted_iota(jnp.int32, s.shape, 0)
-                    s = jnp.where(lane_of(s.shape) <= r, s, -1e30)
-                term = dot_nn(jnp.exp2(s).astype(BF16), vx[here, :])
-                total = term if total is None else total + term
-            return total
-
-        acc[...] = step(block, True)
-
-        def body(kb, carry):
-            acc[...] += step(kb, False)
-            return carry
-
-        lax.fori_loop(s_ref[2 + block], block, body, 0)
-        inverse = 1.0 / acc[:, PAIR:]
-        o_ref[at, :] = (acc[:, :PAIR] * inverse).astype(BF16)
-        linv_ref[at, :] = inverse
-
-
-def attn_fwd(scalars, q, k_own, k_oth, v_own, v_oth, segq, segk, half):
-    rows, qc = q.shape
-    groups = qc // PAIR
-    col = pl.BlockSpec((rows, PAIR), lambda g, s: (0, g))
-    return pl.pallas_call(
-        attn_fwd_kernel,
-        grid_spec=pltpu.PrefetchScalarGridSpec(
-            num_scalar_prefetch=1,
-            grid=(groups,),
-            in_specs=[col] * 5
-            + [
-                pl.BlockSpec((rows, PAIR), lambda g, s: (half, 0)),
-                pl.BlockSpec((2 * rows, PAIR), lambda g, s: (0, 0)),
-            ],
-            out_specs=[col, col],
-            scratch_shapes=[pltpu.VMEM((2 * rows, 2 * PAIR), BF16)] * 4
-            + [pltpu.VMEM((BLOCK, 2 * PAIR), F32)],
-        ),
-        out_shape=[
-            jax.ShapeDtypeStruct((rows, qc), BF16),
-            jax.ShapeDtypeStruct((rows, qc), F32),
-        ],
-        compiler_params=pltpu.CompilerParams(vmem_limit_bytes=VMEM_LIMIT),
-        cost_estimate=cost(10e-6),
-        name="attn_fwd",
-    )(scalars, q, k_own, k_oth, v_own, v_oth, segq, segk)
-
-
-def resid_kernel(mine_ref, theirs_ref, wm_ref, wt_ref, x_ref, gain_ref, resid_ref, ffn_ref):
-    resid = (
-        x_ref[...].astype(F32)
-        + dot_nn(mine_ref[...], wm_ref[...])
-        + dot_nn(theirs_ref[...], wt_ref[...])
-    )
-    resid_ref[...] = resid
-    ffn_ref[...] = (resid * row_norm(resid) * gain_ref[...]).astype(BF16)
-
-
-def resid_norm(mine, theirs, w_mine, w_theirs, x, gain):
-    rows, width = x.shape
-    cols = mine.shape[1]
-    row = lambda c: pl.BlockSpec((BLOCK, c), lambda i: (i, 0))
-    whole = lambda r, c: pl.BlockSpec((r, c), lambda i: (0, 0))
-    return pl.pallas_call(
-        resid_kernel,
-        grid=(rows // BLOCK,),
-        in_specs=[row(cols), row(cols), whole(cols, width), whole(cols, width), row(width), whole(1, width)],
-        out_specs=[row(width), row(width)],
-        out_shape=[jax.ShapeDtypeStruct((rows, width), F32), jax.ShapeDtypeStruct((rows, width), BF16)],
-        compiler_params=pltpu.CompilerParams(vmem_limit_bytes=VMEM_LIMIT),
-        cost_estimate=cost(4e-6),
-        name="resid",
-    )(mine, theirs, w_mine, w_theirs, x, gain)
-
-
-def ffn_kernel(x_ref, c_ref, wg_ref, wu_ref, wd_ref, h_ref, y_ref, gf_ref, yacc, gacc):
-    x, c = x_ref[...], c_ref[...]
-    gate = dot_nn(x, wg_ref[...])
-    up = dot_nn(x, wu_ref[...])
-    grad = dot_nt(c, wd_ref[...])
-    sig = 0.5 * jnp.tanh(0.5 * gate) + 0.5
-    silu = gate * sig
-    mixed = (silu * up).astype(BF16)
-    gg = (grad * up * (sig + silu * (1.0 - sig))).astype(BF16)
-    gu = (grad * silu).astype(BF16)
-    for i, value in enumerate((mixed, gg, gu)):
-        h_ref[i] = value
-    y = dot_nn(mixed, wd_ref[...])
-    gf = dot_nt(gg, wg_ref[...]) + dot_nt(gu, wu_ref[...])
-    step = pl.program_id(0)
-
-    @pl.when(step == 0)
-    def _():
-        yacc[...] = y
-        gacc[...] = gf
-
-    @pl.when(step > 0)
-    def _():
-        yacc[...] += y
-        gacc[...] += gf
-
-    @pl.when(step == pl.num_programs(0) - 1)
-    def _():
-        y_ref[...] = yacc[...].astype(y_ref.dtype)
-        gf_ref[...] = gacc[...].astype(gf_ref.dtype)
-
-
-def ffn(x, c, w_gu, w_down, dtype):
-    rows, width = x.shape
-    hidden = w_down.shape[0]
-    tile = CHUNK
-    nf = hidden // tile
-    whole = pl.BlockSpec((rows, width), lambda f: (0, 0))
-    mid = pl.BlockSpec((3, rows, tile), lambda f: (0, 0, f))
-    return pl.pallas_call(
-        ffn_kernel,
-        grid=(nf,),
-        in_specs=[
-            whole, whole,
-            pl.BlockSpec((width, tile), lambda f: (0, f)),
-            pl.BlockSpec((width, tile), lambda f: (0, f + nf)),
-            pl.BlockSpec((tile, width), lambda f: (f, 0)),
-        ],
-        out_specs=[mid, whole, whole],
-        out_shape=[jax.ShapeDtypeStruct((3, rows, hidden), BF16)]
-        + [jax.ShapeDtypeStruct((rows, width), dtype)] * 2,
-        scratch_shapes=[pltpu.VMEM((rows, width), F32)] * 2,
-        compiler_params=pltpu.CompilerParams(vmem_limit_bytes=VMEM_LIMIT),
-        cost_estimate=cost(20e-6),
-        name="ffn",
-    )(x, c, w_gu, w_gu, w_down)
-
-
 MESH = pl.DeviceIdType.MESH
 CHUNK = 768
 SPLIT = 512
-BITS = 3
+DEPTH = 3
 
 
 def dot_tn(a, b):
     return lax.dot_general(a, b, (((0,), (0,)), ((), ())), preferred_element_type=F32)
 
 
+def pack_columns(dst, first, ref):
+    rows, width = ref.shape
+    low = lane_of((rows, PAIR)) < 64
+    for k in range(width // (2 * PAIR)):
+        a = ref[:, 2 * k * PAIR : (2 * k + 1) * PAIR].astype(F32)
+        b = ref[:, (2 * k + 1) * PAIR : (2 * k + 2) * PAIR].astype(F32)
+        lanes = slice(k * PAIR, (k + 1) * PAIR)
+        dst[0, first : first + rows, lanes] = jnp.where(low, a, pltpu.roll(b, 64, 1)).astype(BF16)
+        dst[1, first : first + rows, lanes] = jnp.where(low, pltpu.roll(a, 64, 1), b).astype(BF16)
+
+
 BACK_INPUTS = (
-    "h_own", "h_oth", "cot_own", "cot_oth", "ffn_own", "ffn_oth", "attn_own", "attn_oth", "tok_own", "tok_oth",
-    "gf_own", "gf_send", "y_own", "y_send", "resid", "wo_mine", "wo_oth", "w_q", "w_kv",
-    "q_own", "q_oth", "kd_own", "kd_oth", "vd_own", "vd_oth", "o_own", "o_oth", "linv_own", "linv_oth",
+    "h_own", "h_oth", "cot_pack", "ffn_pack", "attn_pack", "tok_own", "tok_oth", "y_send", "branch", "do_own", "do_send",
+    "w_q", "w_kv", "q_own", "q_oth", "kd_own", "kd_oth", "vd_own", "vd_oth", "o_own", "o_oth", "linv_own", "linv_oth",
     "qraw_own", "qraw_oth", "kraw_own", "kraw_oth",
 )
-BACK_TABLES = ("segq", "segk", "cos", "sin", "gain1", "gain2", "qg", "kg")
-BACK_OUTPUTS = ("output", "grad_tokens", "shards", "gains", "y_recv")
+BACK_TABLES = ("segq", "segk", "cos", "sin", "gain_ffn", "qg", "kg")
+BACK_OUTPUTS = ("ga_out", "ga_recv", "shards", "gains", "y_recv")
 
 
 class Names:
@@ -311,7 +152,7 @@
 
 def back_kernel(n_dp, scratch_names, *refs):
     m = Names(BACK_INPUTS + BACK_TABLES + BACK_OUTPUTS + scratch_names, refs)
-    rows, width = m.resid.shape
+    rows, width = m.tok_own.shape
     hidden = m.h_own.shape[2]
     per_x = hidden // CHUNK
     n_wide = 3 * per_x
@@ -343,11 +184,10 @@
             device_id=over_t, device_id_type=MESH,
         )
 
-    gf_copy = tensor_copy(0, m.gf_send, m.gf_recv)
     do_copy = tensor_copy(1, m.do_send, m.do_recv)
-    branch_copy = tensor_copy(2, m.branch, m.branch_recv)
+    branch_copy = tensor_copy(2, m.branch_v, m.branch_recv)
     y_copy = tensor_copy(3, m.y_send, m.y_recv)
-    ga_copy = tensor_copy(4, m.branch, m.gf_recv)
+    ga_copy = tensor_copy(4, m.branch_v, m.ga_recv)
 
     def rs_copy(stage, c, src, dst, device):
         return pltpu.make_async_remote_copy(
@@ -421,9 +261,9 @@
                     ).astype(BF16)
             start(second_copies(i))
 
-        @pl.when(i + 2 < n_chunks)
+        @pl.when(i + DEPTH < n_chunks - 1)
         def _():
-            start(first_copies(i + 2))
+            start(first_copies(i + DEPTH))
 
         @pl.when((i >= 1) & (i < n_chunks + 1))
         def _():
@@ -452,16 +292,6 @@
             m.totals[lax.rem(c, 2)] = m.sums[c, zh, zl, x].astype(F32) + m.r3[c].astype(F32)
             total_copy(c).start()
 
-    def pack(dst, own_ref, oth_ref):
-        for part, ref in enumerate((own_ref, oth_ref)):
-            at = pl.ds(part * rows, rows)
-            for k in range(width // (2 * PAIR)):
-                a = ref[:, 2 * k * PAIR : (2 * k + 1) * PAIR].astype(F32)
-                b = ref[:, (2 * k + 1) * PAIR : (2 * k + 2) * PAIR].astype(F32)
-                lanes = slice(k * PAIR, (k + 1) * PAIR)
-                m.packed[dst, 0, at, lanes] = jnp.where(low, a, pltpu.roll(b, 64, 1)).astype(BF16)
-                m.packed[dst, 1, at, lanes] = jnp.where(low, pltpu.roll(a, 64, 1), b).astype(BF16)
-
     def put(ref, slot, lanes, value):
         for a in range(2):
             for b in range(2):
@@ -469,14 +299,12 @@
                     k = ((a * 2 + b) * 2 + e) * block_rows
                     ref[slot, a, b, e, :, lanes] = value[k : k + block_rows].astype(BF16)
 
-    gf_copy.start()
-    stage_cot = both(0, m.cot_own, m.cot_oth, m.stage)
-    stage_ffn = both(0, m.ffn_own, m.ffn_oth, m.stage)
-    stage_attn = both(0, m.attn_own, m.attn_oth, m.stage)
-    start(stage_cot)
+    do_copy.start()
+    packs = [local(i, src, m.packed.at[i]) for i, src in enumerate((m.cot_pack, m.ffn_pack))]
+    attn_load = local(0, m.attn_pack, m.packed.at[0])
+    start(packs)
     loads = [
-        local(2, m.gf_own, m.gres), local(3, m.resid, m.resid_v), local(4, m.wo_mine, m.wom_v),
-        local(5, m.wo_oth, m.wot_v), local(6, m.cot_own, m.cot_v), local(7, m.w_q, m.wq_v), local(8, m.w_kv, m.wkv_v),
+        local(2, m.branch, m.branch_v), local(3, m.do_own, m.do_v), local(7, m.w_q, m.wq_v), local(8, m.w_kv, m.wkv_v),
         *both(9, m.o_own, m.o_oth, m.o_v), *both(11, m.kraw_own, m.kraw_oth, m.kraw_v),
     ]
 
@@ -504,10 +332,8 @@
             ]
 
         start(fetch(0))
-        wait(stage_cot)
-        pack(0, m.stage.at[own_rows], m.stage.at[oth_rows])
-        start(stage_ffn)
         start(loads)
+        packs[0].wait()
 
         def chunk(c, which):
             slot = lax.rem(c, 2)
@@ -529,22 +355,21 @@
             def _():
                 add_core(c - 1)
 
-            @pl.when((c >= 1) & (c <= 2))
+            @pl.when((c >= 1) & (c <= DEPTH))
             def _():
                 start(first_copies(c - 1))
 
-            @pl.when(c == n_wide - 3)
+            @pl.when((c == n_wide - 4) | (c == n_wide - 2))
             def _():
-                tick(0)
+                tick((c - n_wide + 4) // 2)
 
         def first(c, carry):
             chunk(c, 0)
             return carry
 
         lax.fori_loop(0, per_x, first, 0)
-        wait(stage_ffn)
-        pack(1, m.stage.at[own_rows], m.stage.at[oth_rows])
-        start(stage_attn)
+        packs[1].wait()
+        attn_load.start()
 
         def second(c, carry):
             chunk(c, 1)
@@ -552,39 +377,15 @@
 
         lax.fori_loop(per_x, n_wide, second, 0)
         add_core(n_wide - 1)
-        tick(1)
+        tick(2)
 
     pl.run_scoped(wide_phase, pltpu.VMEM((2, 2 * rows, CHUNK), BF16))
     start(tiles(0))
 
     wait(loads)
-    gf_copy.wait_recv()
-    gain_sum = jnp.zeros((1, width), F32)
-    for i in range(rows // BLOCK):
-        at = slice(i * BLOCK, (i + 1) * BLOCK)
-        grad = m.gres[at, :] + m.gf_recv[at, :].astype(F32)
-        resid = m.resid_v[at, :]
-        inverse = row_norm(resid)
-        normed = resid * inverse
-        gain_sum += jnp.sum(grad * normed, axis=0, keepdims=True)
-        w = grad * m.gain2[...]
-        gres = m.cot_v[at, :].astype(F32) + inverse * (
-            w - normed * jnp.mean(w * normed, axis=-1, keepdims=True)
-        )
-        m.gres[at, :] = gres
-        branch = gres.astype(BF16)
-        m.branch[at, :] = branch
-        m.do_send[at, :] = dot_nt(branch, m.wot_v[...]).astype(BF16)
-    do_copy.start()
-    m.do_own[...] = dot_nt(m.branch[...], m.wom_v[...]).astype(BF16)
-    for r in range(width // PAIR):
-        m.mine[width // PAIR + r : width // PAIR + r + 1, :] = gain_sum[:, r * PAIR : (r + 1) * PAIR]
-    wait(stage_attn)
-    pack(0, m.stage.at[own_rows], m.stage.at[oth_rows])
-    tick(2)
+    attn_load.wait()
+    branch_copy.start()
     do_copy.wait_recv()
-    branch_copy.start()
-    tick(3)
 
     def narrow_chunk(p):
         c = n_wide + p
@@ -644,7 +445,7 @@
             vx0[:, :PAIR] = jnp.where(all_low, v, zero)
             vx1[:, :PAIR] = jnp.where(all_low, zero, v)
             kt[...] = jnp.transpose(k.astype(F32))[:64, :].astype(BF16)
-            for at, do_ref in ((own_rows, m.do_own), (oth_rows, m.do_recv)):
+            for at, do_ref in ((own_rows, m.do_v), (oth_rows, m.do_recv)):
                 scaled = do_ref[:, lanes].astype(F32) * m.linv_v[slot, at, :]
                 dox[at, :PAIR] = scaled.astype(BF16)
                 dox[at, PAIR:] = (scaled * m.o_v[at, lanes].astype(F32)).astype(BF16)
@@ -662,6 +463,10 @@
                 return c
 
             lax.fori_loop(0, nb, q_body, 0)
+
+            @pl.when(g == 1)
+            def _():
+                tick(4)
 
             g_lanes = pl.ds(pl.multiple_of(p * SPLIT + slot * PAIR, PAIR), PAIR)
             for at in (own_rows, oth_rows):
@@ -705,7 +510,8 @@
                 def _():
                     branch_copy.wait_recv()
                     y_copy.start()
-                    pack(1, m.branch, m.branch_recv)
+                    pack_columns(m.packed.at[1], 0, m.branch_v)
+                    pack_columns(m.packed.at[1], rows, m.branch_recv)
 
                 narrow_chunk(p)
 
@@ -713,7 +519,7 @@
             def _():
                 add_core(n_wide)
 
-            tick(4 + g)
+            tick(3 + g + jnp.minimum(g, 1))
             return carry
 
         lax.fori_loop(0, 4, group, 0)
@@ -739,11 +545,8 @@
                 out = term if out is None else out + term
         return out
 
-    def end_phase(ga_own, y_v, y_other):
-        tok_v, out_v = m.stage, m.cot_v
+    def end_phase(ga_own, tok_v):
         start(both(0, m.tok_own, m.tok_oth, tok_v))
-        load_y = local(2, m.y_own, y_v)
-        load_y.start()
         wait(both(0, m.tok_own, m.tok_oth, tok_v))
 
         def grad_and_gain(at):
@@ -755,17 +558,22 @@
         total = jnp.zeros((1, width), F32)
         for i in range(rows // BLOCK):
             grad, part = grad_and_gain(pl.ds(rows + i * BLOCK, BLOCK))
-            m.branch[i * BLOCK : (i + 1) * BLOCK, :] = grad.astype(BF16)
+            m.branch_v[i * BLOCK : (i + 1) * BLOCK, :] = grad.astype(BF16)
             total += part
         ga_copy.start()
         add_core(n_chunks - 1)
+        start(first_copies(n_chunks - 1))
         tick(n_chunks - 3)
         for i in range(rows // BLOCK):
             grad, part = grad_and_gain(pl.ds(i * BLOCK, BLOCK))
             ga_own[i * BLOCK : (i + 1) * BLOCK, :] = grad
             total += part
+        ga_out_copy = local(3, ga_own, m.ga_out)
+        ga_out_copy.start()
         for r in range(width // PAIR):
             m.mine[r : r + 1, :] = total[:, r * PAIR : (r + 1) * PAIR]
+            at = slice(width // PAIR + r, width // PAIR + r + 1)
+            m.mine[at, :] = m.gain_ffn[:, r * PAIR : (r + 1) * PAIR]
         last = 2 * width // PAIR
         m.mine[last : last + 1, :] = m.qgain[...]
         m.mine[last + 1 : last + 2, :] = m.kgain[...]
@@ -780,31 +588,14 @@
         for i, device in enumerate(partners):
             m.gain_out[i] = m.mine[...]
             gain_copy(i, device).start()
-            if i == 2:
-                y_copy.wait_recv()
-                load_y.wait()
-                arrived = local(4, m.y_recv, y_other)
-                arrived.start()
-                arrived.wait()
-                out_v[...] = (m.resid_v[...] + y_v[...] + y_other[...].astype(F32)).astype(BF16)
-                local(3, out_v, m.output).start()
             if i >= 1:
                 tick(n_chunks - 3 + i)
             gain_copy(i, device).wait_recv()
             m.mine[...] += m.gain_in[i]
         m.gains[...] = m.mine[...]
+        y_copy.wait_recv()
         ga_copy.wait_recv()
-        for i in range(rows // PAIR):
-            at = slice(i * PAIR, (i + 1) * PAIR)
-            tokens = tok_v[at, :].astype(F32)
-            inverse = row_norm(tokens)
-            normed = tokens * inverse
-            w = (ga_own[at, :] + m.gf_recv[at, :].astype(F32)) * m.gain1[...]
-            ga_own[at, :] = m.gres[at, :] + inverse * (
-                w - normed * jnp.mean(w * normed, axis=-1, keepdims=True)
-            )
-            local(4 + i, ga_own.at[pl.ds(i * PAIR, PAIR)], m.grad_tokens.at[pl.ds(i * PAIR, PAIR)]).start()
-        for copy in (gf_copy, do_copy, y_copy, ga_copy):
+        for copy in (do_copy, y_copy, ga_copy):
             copy.wait_send()
         for i, device in enumerate(partners):
             gain_copy(i, device).wait_send()
@@ -817,20 +608,15 @@
             return carry
 
         lax.fori_loop(0, n_chunks, drain, 0)
-        local(3, out_v, m.output).wait()
-        for i in range(rows // PAIR):
-            local(4 + i, ga_own.at[pl.ds(i * PAIR, PAIR)], m.grad_tokens.at[pl.ds(i * PAIR, PAIR)]).wait()
         for c in (n_chunks - 2, n_chunks - 1):
             total_copy(c).wait()
-
-    pl.run_scoped(
-        end_phase,
-        pltpu.VMEM((rows, width), F32), pltpu.VMEM((rows, width), F32), pltpu.VMEM((rows, width), BF16),
-    )
+        ga_out_copy.wait()
+
+    pl.run_scoped(end_phase, pltpu.VMEM((rows, width), F32), pltpu.VMEM((2 * rows, width), BF16))
 
 
 def back(n_dp, values, tables):
-    rows, width = values["resid"].shape
+    rows, width = values["tok_own"].shape
     hidden = values["h_own"].shape[2]
     seq = 2 * rows
     qc = values["w_q"].shape[1]
@@ -839,25 +625,23 @@
     vm = pltpu.VMEM
     dma = pltpu.SemaphoreType.DMA
     scratch = dict(
-        stage=vm((seq, width), BF16), packed=vm((2, 2, seq, width // 2), BF16),
+        packed=vm((2, 2, seq, width // 2), BF16),
         core_send=vm((2, 2, 2, 2, block, CHUNK), BF16), kept=vm((2, 2, 2, 2, block, CHUNK), BF16),
         sums=vm((n_chunks, 2, 2, 2, block, CHUNK), BF16),
         r1a=vm((n_chunks, 2, 2, block, SPLIT), BF16), r1b=vm((n_chunks, 2, 2, block, CHUNK - SPLIT), BF16),
         r2a=vm((n_chunks, 2, block, SPLIT), BF16), r2b=vm((n_chunks, 2, block, CHUNK - SPLIT), BF16),
         r3=vm((n_chunks, block, CHUNK), BF16), totals=vm((2, block, CHUNK), F32),
-        gres=vm((rows, width), F32), resid_v=vm((rows, width), F32), cot_v=vm((rows, width), BF16),
-        wom_v=vm((qc, width), BF16), wot_v=vm((qc, width), BF16),
         wq_v=vm((width, qc), BF16), wkv_v=vm((width, qc), BF16),
         o_v=vm((seq, qc), BF16), kraw_v=vm((seq, qc // 2), BF16),
         q_v=vm((2, seq, PAIR), BF16), kd_v=vm((2, seq, PAIR), BF16), vd_v=vm((2, seq, PAIR), BF16),
         qraw_v=vm((2, seq, PAIR), BF16), linv_v=vm((2, seq, PAIR), F32),
-        g_v=vm((seq, 2 * SPLIT), BF16), do_own=vm((rows, qc), BF16),
-        gf_recv=vm((rows, width), BF16), do_send=vm((rows, qc), BF16), do_recv=vm((rows, qc), BF16),
-        branch=vm((rows, width), BF16), branch_recv=vm((rows, width), BF16),
+        g_v=vm((seq, 2 * SPLIT), BF16), do_v=vm((rows, qc), BF16),
+        do_recv=vm((rows, qc), BF16),
+        branch_v=vm((rows, width), BF16), branch_recv=vm((rows, width), BF16),
         qgain=vm((1, PAIR), F32), kgain=vm((1, PAIR), F32), mine=vm((24, PAIR), F32),
         gain_out=vm((5, 24, PAIR), F32), gain_in=vm((5, 24, PAIR), F32),
         t_send=dma((5,)), t_recv=dma((5,)), rs_send=dma((6, n_chunks)), rs_recv=dma((6, n_chunks)),
-        l_sem=dma((13,)), g_sem=dma((2, 10)), h_sem=dma((2, 2)), s_sem=dma((2,)), gain_sem=dma((2, 5)),
+        l_sem=dma((14,)), g_sem=dma((2, 10)), h_sem=dma((2, 2)), s_sem=dma((2,)), gain_sem=dma((2, 5)),
     )
     anywhere = pl.BlockSpec(memory_space=pl.ANY)
     vmem = pl.BlockSpec(memory_space=pltpu.VMEM)
@@ -866,7 +650,8 @@
         in_specs=[anywhere] * len(BACK_INPUTS) + [vmem] * len(BACK_TABLES),
         out_specs=[anywhere, anywhere, anywhere, vmem, anywhere],
         out_shape=[
-            jax.ShapeDtypeStruct((rows, width), BF16), jax.ShapeDtypeStruct((rows, width), F32),
+            jax.ShapeDtypeStruct((rows, width), F32),
+            jax.ShapeDtypeStruct((rows, width), BF16),
             jax.ShapeDtypeStruct((n_chunks, block, CHUNK), F32), jax.ShapeDtypeStruct((24, PAIR), F32),
             jax.ShapeDtypeStruct((rows, width), BF16),
         ],
@@ -879,6 +664,400 @@
     )(*[values[k] for k in BACK_INPUTS], *[tables[k] for k in BACK_TABLES])
 
 
+FRONT_INPUTS = (
+    "tok_own", "tok_oth", "cot_own", "w_q", "w_kv", "w_o", "w_gu", "w_down",
+    "q_own", "kd_own", "vd_own", "attn_own",
+)
+FRONT_TABLES = ("segq", "segk", "cos", "sin", "gain1", "gain2", "qg", "kg")
+FRONT_OUTPUTS = (
+    "q_oth", "kd_oth", "vd_oth", "qraw_oth", "kraw_oth", "o_own", "o_oth", "linv_own", "linv_oth",
+    "cot_pack", "ffn_pack", "attn_pack", "h_own", "h_oth", "base", "y_send", "gres", "branch", "do_own", "do_send",
+    "gain_ffn",
+)
+PIECES = 4
+
+
+def front_kernel(scratch_names, *refs):
+    m = Names(FRONT_INPUTS + FRONT_TABLES + FRONT_OUTPUTS + scratch_names, refs)
+    rows, width = m.tok_own.shape
+    hidden = m.w_down.shape[0]
+    qc = m.w_q.shape[1]
+    kc = m.w_kv.shape[1] // 2
+    nb = 2 * rows // BLOCK
+    t = lax.axis_index("tensor")
+    d = lax.axis_index("dp")
+    core = lax.rem(d, 2)
+    over_t = {"tensor": 1 - t}
+    over_core = {"dp": d + 1 - 2 * core}
+
+    barrier = pltpu.get_barrier_semaphore()
+    for p in (over_t, over_core):
+        pl.semaphore_signal(barrier, inc=1, device_id=p, device_id_type=MESH)
+    pl.semaphore_wait(barrier, 2)
+
+    def remote(i, src, dst, device):
+        return pltpu.make_async_remote_copy(
+            src_ref=src, dst_ref=dst, send_sem=m.r_send.at[i], recv_sem=m.r_recv.at[i],
+            device_id=device, device_id_type=MESH,
+        )
+
+    pieces = [pl.ds(i * (rows // PIECES), rows // PIECES) for i in range(PIECES)]
+    halves = [pl.ds(i * BLOCK, BLOCK) for i in range(rows // BLOCK)]
+    cot_copies = [remote(i, m.cot_own.at[at], m.cot_v.at[1, at], over_t) for i, at in enumerate(pieces)]
+    half_o = qc // 2
+    mine_o = pl.ds(pl.multiple_of(core * half_o, half_o), half_o)
+    wo_copy = remote(4, m.w_o.at[mine_o], m.wot_v.at[mine_o], over_t)
+    wo_core = remote(5, m.wot_v.at[mine_o], m.wot_v.at[mine_o], over_core)
+    o_copy = remote(6, m.o_v.at[1], m.theirs, over_t)
+    ffn_copies = [remote(7 + i, m.ffn_v.at[0, at], m.ffn_v.at[1, at], over_t) for i, at in enumerate(halves)]
+    gf_copies = [remote(9 + i, m.gf_send.at[at], m.gf_in.at[at], over_t) for i, at in enumerate(halves)]
+
+    def local(i, src, dst):
+        return pltpu.make_async_copy(src, dst, m.l_sem.at[i])
+
+    loads = [
+        local(i, src, dst)
+        for i, (src, dst) in enumerate((
+            (m.tok_oth, m.tok_v.at[1]), (m.w_q, m.wq_v), (m.w_kv, m.wkv_v), (m.q_own, m.q_v.at[0]),
+            (m.kd_own, m.kd_v.at[0]), (m.vd_own, m.vd_v.at[0]), (m.w_o, m.wom_v), (m.tok_own, m.tok_v.at[0]),
+            (m.attn_own, m.attn_v.at[0]), (m.cot_own, m.cot_v.at[0]), (m.w_gu, m.wgu_v), (m.w_down, m.wd_v),
+        ))
+    ]
+    out_sem = [0]
+    stores = []
+
+    def store(src, dst):
+        copy = pltpu.make_async_copy(src, dst, m.o_sem.at[out_sem[0]])
+        out_sem[0] += 1
+        copy.start()
+        stores.append(copy)
+
+    wo_copy.start()
+    for copy in cot_copies[:3]:
+        copy.start()
+    for copy in loads:
+        copy.start()
+    for copy in loads[:6]:
+        copy.wait()
+
+    for at in halves:
+        table = pl.ds(rows + at.start, BLOCK)
+        qkv_kernel(
+            m.tok_v.at[1, at], m.gain1, m.wq_v, m.wkv_v.at[:, pl.ds(0, kc)], m.wkv_v.at[:, pl.ds(kc, kc)],
+            m.qg, m.kg, m.cos.at[table], m.sin.at[table],
+            m.attn_v.at[1, at], m.q_v.at[1, at], m.kd_v.at[1, at], m.vd_v.at[1, at], m.qraw_v.at[at], m.kraw_v.at[at],
+        )
+    for src, dst in (
+        (m.q_v.at[1], m.q_oth), (m.kd_v.at[1], m.kd_oth), (m.vd_v.at[1], m.vd_oth),
+        (m.qraw_v, m.qraw_oth), (m.kraw_v, m.kraw_oth),
+    ):
+        store(src, dst)
+    wo_copy.wait_recv()
+    wo_core.start()
+
+    def place(block):
+        return pl.ds(pl.multiple_of(lax.rem(block + t * (nb // 2), nb) * BLOCK, BLOCK), BLOCK)
+
+    def attention_phase(kx0, kx1, vx0, vx1, acc):
+        both = lane_of((2 * rows, PAIR)) < 64
+        one = jnp.ones((2 * rows, PAIR), F32)
+        low = lane_of((rows, PAIR)) < 64
+        zero = jnp.zeros((rows, PAIR), BF16)
+        kx0[:, PAIR:] = m.segk[...]
+        kx1[:, PAIR:] = m.segk[...]
+        vx0[:, PAIR:] = jnp.where(both, one, 0.0).astype(BF16)
+        vx1[:, PAIR:] = jnp.where(both, 0.0, one).astype(BF16)
+
+        def half(part, first):
+            def group(g, carry):
+                lanes = pl.ds(pl.multiple_of(g * PAIR, PAIR), PAIR)
+                for i in range(2):
+                    at = pl.ds(i * rows, rows)
+                    k, v = m.kd_v[i, :, lanes], m.vd_v[i, :, lanes]
+                    kx0[at, :PAIR] = jnp.where(low, k, zero)
+                    kx1[at, :PAIR] = jnp.where(low, zero, k)
+                    vx0[at, :PAIR] = jnp.where(low, v, zero)
+                    vx1[at, :PAIR] = jnp.where(low, zero, v)
+                for i in range(rows // BLOCK):
+                    at = pl.ds(i * BLOCK, BLOCK)
+                    q = jnp.concatenate(
+                        [m.q_v[part, at, lanes], m.segq[pl.ds(part * rows + i * BLOCK, BLOCK), :]], axis=1
+                    )
+                    block = first + i
+
+                    def step(kb, diagonal):
+                        here = place(kb)
+                        total = None
+                        for kx, vx in ((kx0, vx0), (kx1, vx1)):
+                            s = dot_nt(q, kx[here, :])
+                            if diagonal:
+                                r = lax.broadcasted_iota(jnp.int32, s.shape, 0)
+                                s = jnp.where(lane_of(s.shape) <= r, s, -1e30)
+                            term = dot_nn(jnp.exp2(s).astype(BF16), vx[here, :])
+                            total = term if total is None else total + term
+                        return total
+
+                    acc[...] = step(block, True)
+
+                    def body(kb, c):
+                        acc[...] += step(kb, False)
+                        return c
+
+                    lax.fori_loop(jnp.maximum(block - 2, 0), block, body, 0)
+                    inverse = 1.0 / acc[:, PAIR:]
+                    m.o_v[part, at, lanes] = (acc[:, :PAIR] * inverse).astype(BF16)
+                    m.linv_v[part, at, lanes] = inverse
+                return carry
+
+            lax.fori_loop(0, qc // PAIR, group, 0)
+
+        half(1, (1 - t) * (nb // 2))
+        o_copy.start()
+        half(0, t * (nb // 2))
+
+    pl.run_scoped(
+        attention_phase, *[pltpu.VMEM((2 * rows, 2 * PAIR), BF16)] * 4, pltpu.VMEM((BLOCK, 2 * PAIR), F32)
+    )
+    for src, dst in (
+        (m.o_v.at[0], m.o_own), (m.o_v.at[1], m.o_oth), (m.linv_v.at[0], m.linv_own), (m.linv_v.at[1], m.linv_oth)
+    ):
+        store(src, dst)
+
+    for copy in loads[6:9]:
+        copy.wait()
+    pack_columns(m.ffn_pack_v, 0, m.attn_v.at[0])
+    pack_columns(m.ffn_pack_v, rows, m.attn_v.at[1])
+    attn_store = local(12, m.ffn_pack_v, m.attn_pack)
+    attn_store.start()
+    wo_core.wait_recv()
+    o_copy.wait_recv()
+    for i, at in enumerate(halves):
+        resid = (
+            m.tok_v[0, at, :].astype(F32) + dot_nn(m.o_v[0, at, :], m.wom_v[...]) + dot_nn(m.theirs[at, :], m.wot_v[...])
+        )
+        m.resid_v[at, :] = resid
+        m.ffn_v[0, at, :] = (resid * row_norm(resid) * m.gain2[...]).astype(BF16)
+        ffn_copies[i].start()
+        if i == 0:
+            for copy in cot_copies[3:]:
+                copy.start()
+
+    for copy in loads[9:]:
+        copy.wait()
+    n_tiles = hidden // CHUNK
+    h_dst = (m.h_own, m.h_oth)
+    h_count = [0]
+
+    def feed_forward(part, at):
+        x, c = m.ffn_v.at[part, at], m.cot_v.at[part, at]
+
+        def h_copy(slot, f, rows_at, dst):
+            cols = pl.ds(pl.multiple_of(f * CHUNK, CHUNK), CHUNK)
+            return pltpu.make_async_copy(m.h_v.at[slot], dst.at[:, rows_at, cols], m.h_sem.at[slot])
+
+        base = h_count[0]
+        h_count[0] += n_tiles
+
+        def tile(f, carry):
+            slot = lax.rem(base + f, 2)
+            cols = pl.ds(pl.multiple_of(f * CHUNK, CHUNK), CHUNK)
+            up_cols = pl.ds(pl.multiple_of(hidden + f * CHUNK, CHUNK), CHUNK)
+            gate = dot_nn(x[...], m.wgu_v[:, cols])
+            up = dot_nn(x[...], m.wgu_v[:, up_cols])
+            grad = dot_nt(c[...], m.wd_v[cols, :])
+
+            if base == 0:
+                @pl.when(f >= 2)
+                def _():
+                    h_copy(slot, f, at, h_dst[part]).wait()
+            else:
+                h_copy(slot, f, at, h_dst[part]).wait()
+
+            sig = 0.5 * jnp.tanh(0.5 * gate) + 0.5
+            silu = gate * sig
+            mixed = (silu * up).astype(BF16)
+            gg = (grad * up * (sig + silu * (1.0 - sig))).astype(BF16)
+            gu = (grad * silu).astype(BF16)
+            for i, value in enumerate((mixed, gg, gu)):
+                m.h_v[slot, i] = value
+            h_copy(slot, f, at, h_dst[part]).start()
+            y = dot_nn(mixed, m.wd_v[cols, :])
+            gf = dot_nt(gg, m.wgu_v[:, cols]) + dot_nt(gu, m.wgu_v[:, up_cols])
+
+            y_to, gf_to = (m.y_oth, m.gf_oth) if part else (m.y_v.at[at], m.gf_v.at[at])
+
+            @pl.when(f == 0)
+            def _():
+                y_to[...] = y
+                gf_to[...] = gf
+
+            @pl.when(f > 0)
+            def _():
+                y_to[...] += y
+                gf_to[...] += gf
+
+            return carry
+
+        lax.fori_loop(0, n_tiles, tile, 0)
+
+    feed_forward(0, halves[0])
+    pack_columns(m.cot_pack_v, 0, m.cot_v.at[0])
+    attn_store.wait()
+    pack_columns(m.ffn_pack_v, 0, m.ffn_v.at[0])
+    for i, at in enumerate(halves):
+        ffn_copies[i].wait_recv()
+        for copy in cot_copies[2 * i : 2 * i + 2]:
+            copy.wait_recv()
+        feed_forward(1, at)
+        m.gf_send[at, :] = m.gf_oth[...].astype(BF16)
+        gf_copies[i].start()
+        m.y_low[at, :] = m.y_oth[...].astype(BF16)
+    store(m.y_low, m.y_send)
+    feed_forward(0, halves[1])
+    pack_columns(m.cot_pack_v, rows, m.cot_v.at[1])
+    pack_columns(m.ffn_pack_v, rows, m.ffn_v.at[1])
+    store(m.cot_pack_v, m.cot_pack)
+    store(m.ffn_pack_v, m.ffn_pack)
+
+    total = jnp.zeros((1, width), F32)
+    for i, at in enumerate(halves):
+        gf_copies[i].wait_recv()
+        grad = m.gf_v[at, :] + m.gf_in[at, :].astype(F32)
+        resid = m.resid_v[at, :]
+        inverse = row_norm(resid)
+        normed = resid * inverse
+        total += jnp.sum(grad * normed, axis=0, keepdims=True)
+        w = grad * m.gain2[...]
+        gres = m.cot_v[0, at, :].astype(F32) + inverse * (
+            w - normed * jnp.mean(w * normed, axis=-1, keepdims=True)
+        )
+        m.gf_v[at, :] = gres
+        branch = gres.astype(BF16)
+        m.branch_v[at, :] = branch
+        m.do_v[0, at, :] = dot_nt(branch, m.wom_v[...]).astype(BF16)
+        m.do_v[1, at, :] = dot_nt(branch, m.wot_v[...]).astype(BF16)
+        m.y_v[at, :] += resid
+    for src, dst in (
+        (m.do_v.at[1], m.do_send), (m.do_v.at[0], m.do_own), (m.branch_v, m.branch), (m.gf_v, m.gres),
+        (m.y_v, m.base),
+    ):
+        store(src, dst)
+    m.gain_ffn[...] = total
+    for copy in (*cot_copies, wo_copy, wo_core, o_copy, *ffn_copies, *gf_copies):
+        copy.wait_send()
+    for slot in range(2):
+        pltpu.make_async_copy(m.h_v.at[slot], m.h_own.at[:, halves[1], pl.ds(0, CHUNK)], m.h_sem.at[slot]).wait()
+    for copy in stores:
+        copy.wait()
+
+
+def front(values, tables):
+    rows, width = values["tok_own"].shape
+    hidden = values["w_down"].shape[0]
+    qc = values["w_q"].shape[1]
+    seq = 2 * rows
+    vm = pltpu.VMEM
+    dma = pltpu.SemaphoreType.DMA
+    scratch = dict(
+        tok_v=vm((2, rows, width), BF16), cot_v=vm((2, rows, width), BF16),
+        wq_v=vm((width, qc), BF16), wkv_v=vm((width, qc), BF16), wom_v=vm((qc, width), BF16), wot_v=vm((qc, width), BF16),
+        wgu_v=vm((width, 2 * hidden), BF16), wd_v=vm((hidden, width), BF16),
+        q_v=vm((2, rows, qc), BF16), kd_v=vm((2, rows, qc), BF16), vd_v=vm((2, rows, qc), BF16),
+        attn_v=vm((2, rows, width), BF16), qraw_v=vm((rows, qc), BF16), kraw_v=vm((rows, qc // 2), BF16),
+        o_v=vm((2, rows, qc), BF16), linv_v=vm((2, rows, qc), F32), theirs=vm((rows, qc), BF16),
+        resid_v=vm((rows, width), F32), ffn_v=vm((2, rows, width), BF16),
+        h_v=vm((2, 3, BLOCK, CHUNK), BF16), y_v=vm((rows, width), F32), gf_v=vm((rows, width), F32),
+        y_oth=vm((BLOCK, width), F32), gf_oth=vm((BLOCK, width), F32),
+        y_low=vm((rows, width), BF16), gf_send=vm((rows, width), BF16), gf_in=vm((rows, width), BF16),
+        cot_pack_v=vm((2, seq, width // 2), BF16),
+        ffn_pack_v=vm((2, seq, width // 2), BF16), branch_v=vm((rows, width), BF16), do_v=vm((2, rows, qc), BF16),
+        r_send=dma((11,)), r_recv=dma((11,)), l_sem=dma((13,)), o_sem=dma((20,)), h_sem=dma((2,)),
+    )
+    anywhere = pl.BlockSpec(memory_space=pl.ANY)
+    vmem = pl.BlockSpec(memory_space=pltpu.VMEM)
+    low, full = (lambda *shape: jax.ShapeDtypeStruct(shape, BF16)), (lambda *shape: jax.ShapeDtypeStruct(shape, F32))
+    shapes = dict(
+        q_oth=low(rows, qc), kd_oth=low(rows, qc), vd_oth=low(rows, qc),
+        qraw_oth=low(rows, qc), kraw_oth=low(rows, qc // 2), o_own=low(rows, qc), o_oth=low(rows, qc),
+        linv_own=full(rows, qc), linv_oth=full(rows, qc),
+        cot_pack=low(2, seq, width // 2), ffn_pack=low(2, seq, width // 2), attn_pack=low(2, seq, width // 2),
+        h_own=low(3, rows, hidden), h_oth=low(3, rows, hidden), base=full(rows, width), y_send=low(rows, width),
+        gres=full(rows, width), branch=low(rows, width), do_own=low(rows, qc), do_send=low(rows, qc),
+        gain_ffn=full(1, width),
+    )
+    outs = pl.pallas_call(
+        functools.partial(front_kernel, tuple(scratch)),
+        in_specs=[anywhere] * len(FRONT_INPUTS) + [vmem] * len(FRONT_TABLES),
+        out_specs=[anywhere] * (len(FRONT_OUTPUTS) - 1) + [vmem],
+        out_shape=[shapes[k] for k in FRONT_OUTPUTS],
+        scratch_shapes=list(scratch.values()),
+        compiler_params=pltpu.CompilerParams(
+            vmem_limit_bytes=BACK_VMEM, collective_id=1, has_side_effects=True
+        ),
+        cost_estimate=cost(100e-6),
+        name="front",
+    )(*[values[k] for k in FRONT_INPUTS], *[tables[k] for k in FRONT_TABLES])
+    return dict(zip(FRONT_OUTPUTS, outs))
+
+
+def finish_kernel(
+    base_ref, yr_ref, ga_ref, gr_ref, x_ref, gres_ref, gain_ref, shards_ref,
+    out_ref, gt_ref, q_ref, kv_ref, o_ref, gu_ref, down_ref,
+):
+    out_ref[...] = (base_ref[...] + yr_ref[...].astype(F32)).astype(BF16)
+    x = x_ref[...].astype(F32)
+    inverse = row_norm(x)
+    normed = x * inverse
+    w = (ga_ref[...] + gr_ref[...].astype(F32)) * gain_ref[...]
+    gt_ref[...] = gres_ref[...] + inverse * (w - normed * jnp.mean(w * normed, axis=-1, keepdims=True))
+    n_chunks = shards_ref.shape[0]
+    per_x = (n_chunks - 2) // 3
+    two = 2 * PAIR
+    step = pl.program_id(0)
+
+    @pl.when(step < per_x)
+    def _():
+        down_ref[...] = shards_ref[step]
+        gu_ref[:, 0, :] = shards_ref[per_x + step]
+        gu_ref[:, 1, :] = shards_ref[2 * per_x + step]
+
+    @pl.when(step == per_x)
+    def _():
+        for p in range(2):
+            shard = shards_ref[3 * per_x + p]
+            q_ref[:, p * two : (p + 1) * two] = shard[:, :two]
+            kv_ref[:, 0, p * PAIR : (p + 1) * PAIR] = shard[:, two : two + PAIR]
+            kv_ref[:, 1, p * PAIR : (p + 1) * PAIR] = shard[:, two + PAIR : 2 * two]
+            o_ref[:, p * two : (p + 1) * two] = shard[:, 2 * two :]
+
+
+def finish(base, y_recv, ga_own, ga_recv, x, gres, gain, shards):
+    rows, width = x.shape
+    n_chunks, block, _ = shards.shape
+    hidden = (n_chunks - 2) // 3 * CHUNK
+    per_x = hidden // CHUNK
+    row = pl.BlockSpec((rows // (per_x + 1), width), lambda i: (i, 0))
+    fixed = lambda shape: pl.BlockSpec(shape, lambda i: (0,) * len(shape))
+    shapes = [(block, SPLIT), (block, 2, SPLIT // 2), (block, SPLIT), (block, 2, hidden), (block, hidden)]
+    piece = lambda i: jnp.minimum(i, per_x - 1)
+    return pl.pallas_call(
+        finish_kernel,
+        grid=(per_x + 1,),
+        in_specs=[row] * 6 + [fixed((1, width)), fixed(shards.shape)],
+        out_specs=[row, row]
+        + [fixed(shape) for shape in shapes[:3]]
+        + [
+            pl.BlockSpec((block, 2, CHUNK), lambda i: (0, 0, piece(i))),
+            pl.BlockSpec((block, CHUNK), lambda i: (0, piece(i))),
+        ],
+        out_shape=[jax.ShapeDtypeStruct((rows, width), BF16), jax.ShapeDtypeStruct((rows, width), F32)]
+        + [jax.ShapeDtypeStruct(shape, F32) for shape in shapes],
+        compiler_params=pltpu.CompilerParams(vmem_limit_bytes=VMEM_LIMIT),
+        cost_estimate=cost(6e-6),
+        name="finish",
+    )(base, y_recv, ga_own, ga_recv, x, gres, gain, shards)
+
+
 def swap(value, axis, size, bit):
     return lax.ppermute(value, axis, [(i, i ^ bit) for i in range(size)])
 
@@ -895,23 +1074,11 @@
     hidden = w_down.shape[0]
     seq = doc_ids.shape[1]
     t = lax.axis_index("tensor")
-    d = lax.axis_index("dp")
     over = functools.partial(swap, axis="tensor", size=2, bit=1)
 
     tokens_oth = over(tokens)
-    w_o_oth = over(after(w_o, tokens_oth))
-    cot_oth = over(after(cotangent, tokens_oth))
 
     segment = doc_ids[0]
-    nb = seq // BLOCK
-    heads_of_blocks = segment.reshape(nb, BLOCK)
-    first_doc, last_doc = heads_of_blocks[:, 0], heads_of_blocks[:, -1]
-    below = jnp.arange(nb)[None, :] < jnp.arange(nb)[:, None]
-    lowest = jnp.sum((below & (last_doc[None, :] < first_doc[:, None])).astype(jnp.int32), axis=1)
-    shift = t * (nb // 2)
-    table = lambda first: jnp.concatenate([jnp.stack([shift, first]).astype(jnp.int32), lowest])
-    scalars_own = table(shift)
-    scalars_oth = table(nb // 2 - shift)
     segment = jnp.where(t == 0, segment, jnp.roll(segment, rows))
     lanes = jnp.arange(PAIR, dtype=jnp.int32)[None, :]
     match = lanes == segment[:, None]
@@ -930,54 +1097,35 @@
     kg = jnp.concatenate([k_gain, k_gain]).reshape(1, PAIR)
     w_kv = w_kv.reshape(width, -1)
     w_gu = w_gu.reshape(width, 2 * hidden)
-    core = (d & 1).astype(jnp.int32).reshape(1)
+    tables = dict(segq=segq, segk=segk, cos=cosine, sin=sine, gain1=gain1, gain2=gain2, qg=qg, kg=kg)
 
     attn_own, q_own, kd_own, vd_own, qraw_own, kraw_own = qkv(
         tokens, gain1, w_q, w_kv, qg, kg, cosine, sine, 0
     )
-    attn_oth, q_oth, kd_oth, vd_oth, qraw_oth, kraw_oth = qkv(
-        tokens_oth, gain1, w_q, w_kv, qg, kg, cosine, sine, 1
-    )
-    o_oth, linv_oth = attn_fwd(scalars_oth, q_oth, kd_own, kd_oth, vd_own, vd_oth, segq, segk, 1)
-    theirs = over(o_oth)
-    o_own, linv_own = attn_fwd(scalars_own, q_own, kd_own, kd_oth, vd_own, vd_oth, segq, segk, 0)
-    resid, ffn_own = resid_norm(o_own, theirs, w_o, w_o_oth, tokens, gain2)
-
-    ffn_oth = over(ffn_own)
-    h_own, y_own, gf_own = ffn(ffn_own, cotangent, w_gu, w_down, F32)
-    h_oth, y_oth, gf_oth = ffn(after(ffn_oth, gf_own), cot_oth, w_gu, w_down, BF16)
-
-    output, grad_tokens, shards, gains, _ = back(
-        n_dp,
-        dict(
-            h_own=h_own, h_oth=h_oth, cot_own=cotangent, cot_oth=cot_oth, ffn_own=ffn_own, ffn_oth=ffn_oth,
-            attn_own=attn_own, attn_oth=attn_oth, tok_own=tokens, tok_oth=tokens_oth,
-            gf_own=gf_own, gf_send=gf_oth, y_own=y_own, y_send=y_oth, resid=resid,
-            wo_mine=w_o, wo_oth=w_o_oth, w_q=w_q, w_kv=w_kv,
-            q_own=q_own, q_oth=q_oth, kd_own=kd_own, kd_oth=kd_oth, vd_own=vd_own, vd_oth=vd_oth,
-            o_own=o_own, o_oth=o_oth, linv_own=linv_own, linv_oth=linv_oth,
-            qraw_own=qraw_own, qraw_oth=qraw_oth, kraw_own=kraw_own, kraw_oth=kraw_oth,
-        ),
-        dict(segq=segq, segk=segk, cos=cosine, sin=sine, gain1=gain1, gain2=gain2, qg=qg, kg=kg),
-    )
+    values = dict(
+        tok_own=tokens, tok_oth=tokens_oth, cot_own=cotangent, w_q=w_q, w_kv=w_kv, w_o=w_o, w_gu=w_gu, w_down=w_down,
+        attn_own=attn_own, q_own=q_own, kd_own=kd_own, vd_own=vd_own, qraw_own=qraw_own, kraw_own=kraw_own,
+    )
+    values.update(front(values, tables))
+    tables.update(gain_ffn=values["gain_ffn"])
+    ga_own, ga_recv, shards, gains, y_recv = back(n_dp, values, tables)
     m = width // PAIR
-    per_x = hidden // CHUNK
     fold = lambda row: row[:head_dim] + row[head_dim:]
-    side = lambda i: jnp.concatenate([shards[i * per_x + j] for j in range(per_x)], axis=1)
-    pairs = [shards[3 * per_x + p] for p in range(2)]
-    join = lambda a, b: jnp.concatenate([pair[:, a:b] for pair in pairs], axis=1)
+    output, grad_tokens, grad_q, grad_kv, grad_o, grad_gu, grad_down = finish(
+        values["base"], y_recv, ga_own, ga_recv, tokens, values["gres"], gain1, shards
+    )
     return (
         output,
         grad_tokens,
         gains[:m].reshape(width),
-        join(0, 2 * PAIR),
-        jnp.stack([join(2 * PAIR, 3 * PAIR), join(3 * PAIR, 4 * PAIR)], axis=1),
+        grad_q,
+        grad_kv,
         fold(gains[2 * m]),
         fold(gains[2 * m + 1]),
-        join(SPLIT, CHUNK).T,
+        grad_o.T,
         gains[m : 2 * m].reshape(width),
-        jnp.stack([side(1), side(2)], axis=1),
-        side(0).T,
+        grad_gu,
+        grad_down.T,
     )
 
 

time: 309 us -> 279 us (0.903)
  waiting for transfers between devices: 30.1 us -> 0.01 us
  Pallas kernels: 234 us -> 248 us
  local copies, waits for them, and re-layouts: 20.3 us -> 12.5 us
  other arithmetic: 12.8 us -> 8.36 us
  starting transfers between devices: 7.09 us -> 3.03 us
    pallas_call x5 -> x2, Pallas kernels: 69.9 us -> 114 us  [the longest x1 106 us: front(): pl.pallas_call(functools.partial(front_kernel, tuple(scratch)), in_specs=...]
    ppermute x5 -> x1, waiting for transfers between devices: 30.1 us -> 0.01 us  [swap(): return lax.ppermute(value, axis, [(i, i ^ bit) for i in range(size)])]
    pallas_call x1, Pallas kernels: 152 us -> 128 us  [back(): pl.pallas_call(functools.partial(back_kernel, n_dp, tuple(scratch)), in_s...]
    unnamed x29 -> x8, local copies, waits for them, and re-layouts: 17.1 us -> 11.2 us
    pallas_call x2 -> x1, Pallas kernels: 12.1 us -> 6.36 us  [qkv(): pl.pallas_call(qkv_kernel, grid=(nb,), in_specs=[row(width), whole((1, wi...]
    ppermute x5 -> x1, starting transfers between devices: 7.09 us -> 3.03 us  [swap(): return lax.ppermute(value, axis, [(i, i ^ bit) for i in range(size)])]
  transfers between devices with their start and end apart: 5 -> 1, of which waited for: 3 -> 0; matrix products, arithmetic and copies ran while one was open for 7% -> 6% of each run, Pallas kernels for 18% -> 2%
where the time goes in v3:
time: 279 us; the launch traced here: 273 us
  Pallas kernels  248 us (89%)
  local copies, waits for them, and re-layouts  12.5 us (4%)
  other arithmetic  8.36 us (3%)
  starting transfers between devices  3.03 us (1%)
    pallas_call x1, Pallas kernels, back(): pl.pallas_call(functools.partial(back_kernel, n_dp, tuple(scratch)), in_s...  128 us
    pallas_call x1, Pallas kernels, front(): pl.pallas_call(functools.partial(front_kernel, tuple(scratch)), in_specs=...  106 us
    unnamed x8, local copies, waits for them, and re-layouts  11.2 us
    pallas_call x1, Pallas kernels, finish(): pl.pallas_call(finish_kernel, grid=(per_x + 1,), in_specs=[row] * 6 + [fi...  7.94 us
    pallas_call x1, Pallas kernels, qkv(): pl.pallas_call(qkv_kernel, grid=(nb,), in_specs=[row(width), whole((1, wi...  6.36 us
  transfers between devices with their start and end apart: 1, of which 0 were waited for; matrix products, arithmetic and copies ran while one was open for 6% of the time, Pallas kernels for 2%

profile of v3, /device:TPU:0, one launch (start us, length us, event | category | flops | bytes accessed | tf_op | source)
XLA Modules:
  0.0 273.4 jit_solution(4007324474045774806)
XLA Ops:
  0.6 3.0 %collective-permute-start = (bf16[512,1024]{1,0:T(8,128)(2,1)}, bf16[512,1024]{1,0:T(8,128)(2,1)S(1)}, u32[]{:S(2)}, u32[]{:S(2)}) collective-permute-start(bf16[512,1024]{1,0:T(8,128)(2,1)} %x_ref.3), channel_id=1, source_target_pairs={{0,1},{1,0},{2,3},{3,2},{4,5},{5,4},{6,7},{7,6},{8,9},{9,8},{10,11... | collective-permute-start | bytes 3145736 | tf_op jit(solution)/shard_map/ppermute | solution.py:1062
  3.7 1.3 maximum_bitcast_fusion
  5.0 0.0 copy-start.1
  5.0 1.9 fusion.2
  6.9 1.9 pad_maximum_fusion
  8.8 0.0 copy-done.1
  8.8 1.2 copy.24
  10.0 9.0 %copy.25 = bf16[128,8,2,2304]{3,1,2,0:T(8,128)(2,1)} copy(bf16[128,8,2,2304]{3,2,1,0:T(2,128)(2,1)} %bitcast.28) | data formatting | bytes 18874368
  19.0 0.0 copy-start.2
  19.0 6.4 %qkv.1 = (bf16[512,1024]{1,0:T(8,128)(2,1)}, bf16[512,512]{1,0:T(8,128)(2,1)}, bf16[512,512]{1,0:T(8,128)(2,1)}, bf16[512,512]{1,0:T(8,128)(2,1)}, bf16[512,512]{1,0:T(8,128)(2,1)}, /*index=5*/bf16[512,256]{1,0:T(8,128)(2,1)}) custom-call(bf16[512,1024]{1,0:T(8,128)(2,1)} %x_ref.3, f32[1,1024]{1,0:T(1,128)} %bitcast.30, bf16[1024,512]{1,0:T(8,128)(2,1)} %refs_11_.1, ...), custom_call_target="tpu_custom_call" | custom-call | flops 50000000 | tf_op jit(solution)/shard_map/qkv/pallas_call | solution.py:100
  25.4 0.0 copy-done.2
  25.4 0.9 fusion.1.refs_13_.refs_28_
  26.3 0.9 subtract_convert_fusion.refs_12_.refs_27_
  27.2 0.0 collective-permute-done.refs_1_.refs_6_
  27.3 0.0 copy-start
  27.3 1.0 copy-done
  28.2 105.9 %front.1 = (bf16[512,512]{1,0:T(8,128)(2,1)}, bf16[512,512]{1,0:T(8,128)(2,1)}, bf16[512,512]{1,0:T(8,128)(2,1)}, bf16[512,512]{1,0:T(8,128)(2,1)}, bf16[512,256...) custom-call(bf16[512,1024]{1,0:T(8,128)(2,1)} %x_ref.3, ...), custom_call_target="tpu_custom_call" | custom-call | flops 1000000000 | tf_op jit(solution)/shard_map/front/pallas_call | solution.py:988
  134.1 128.2 %back.1 = (f32[512,1024]{1,0:T(8,128)}, bf16[512,1024]{1,0:T(8,128)(2,1)}, f32[11,64,768]{2,1,0:T(8,128)}, f32[24,128]{1,0:T(8,128)}, bf16[512,1024]{1,0:T(8,128)(2,1)}) custom-call(bf16[3,512,2304]{2,1,0:T(8,128)(2,1)} %get-tuple-element.55.refs_0_, bf16[3,512,2304]{2,1,0:T(8,128)(2,1)} %get-tuple-element.56.refs_1_, ...), custom_call_target="tpu_custom_call" | custom-call | flops 1000000000 | tf_op jit(solution)/shard_map/back/pallas_call | solution.py:648
  262.3 1.4 add_bitcast_fusion
  263.7 1.3 slice_bitcast_fusion
  265.0 7.9 %finish.1 = (bf16[512,1024]{1,0:T(8,128)(2,1)}, f32[512,1024]{1,0:T(8,128)}, f32[64,512]{1,0:T(8,128)}, f32[64,2,256]{2,1,0:T(2,128)}, f32[64,512]{1,0:T(8,128)}...) custom-call(f32[512,1024]{1,0:T(8,128)} %get-tuple-element.54.base_ref, bf16[512,1024]{1,0:T(8,128)(2,1)} %get-tuple-element.76.yr_ref, ...), custom_call_target="tpu_custom_call" | custom-call | flops 60000000 | tf_op jit(solution)/shard_map/finish/pallas_call | solution.py:1043
  (6 shorter events, 0.0 us)
Async XLA Ops:
  0.6 26.6 %collective-permute-start = (bf16[512,1024]{1,0:T(8,128)(2,1)}, bf16[512,1024]{1,0:T(8,128)(2,1)S(1)}, u32[]{:S(2)}, u32[]{:S(2)}) collective-permute-start(bf16[512,1024]{1,0:T(8,128)(2,1)} %x_ref.3), channel_id=1, source_target_pairs={{0,1},{1,0},{2,3},{3,2},{4,5},{5,4},{6,7},{7,6},{8,9},{9,8},{10,11... | collective-permute-start | bytes 3145736 | tf_op jit(solution)/shard_map/ppermute | solution.py:1062
  5.0 3.8 %copy-start.1 = (bf16[1024,2,256]{2,1,0:T(2,128)(2,1)S(1)}, bf16[1024,2,256]{2,1,0:T(2,128)(2,1)}, u32[]{:S(2)}) copy-start(bf16[1024,2,256]{2,1,0:T(2,128)(2,1)} %param.16) | copy-start | bytes 3145732
  19.0 6.4 %copy-start.2 = (s32[1,1024]{1,0:T(1,128)S(1)}, s32[1,1024]{1,0:T(1,128)}, u32[]{:S(2)}) copy-start(s32[1,1024]{1,0:T(1,128)} %param.13) | copy-start | bytes 12292
  27.3 1.0 copy-start

commit v4 on v3

--- a/solution.py
+++ b/solution.py
@@ -118,7 +118,7 @@
 MESH = pl.DeviceIdType.MESH
 CHUNK = 768
 SPLIT = 512
-DEPTH = 3
+DEPTH = 2
 
 
 def dot_tn(a, b):
@@ -137,7 +137,7 @@
 
 
 BACK_INPUTS = (
-    "h_own", "h_oth", "cot_pack", "ffn_pack", "attn_pack", "tok_own", "tok_oth", "y_send", "branch", "do_own", "do_send",
+    "h", "cot_pack", "ffn_pack", "attn_pack", "tok_own", "tok_oth", "y_send", "branch", "do_own", "do_send",
     "w_q", "w_kv", "q_own", "q_oth", "kd_own", "kd_oth", "vd_own", "vd_oth", "o_own", "o_oth", "linv_own", "linv_oth",
     "qraw_own", "qraw_oth", "kraw_own", "kraw_oth",
 )
@@ -153,7 +153,7 @@
 def back_kernel(n_dp, scratch_names, *refs):
     m = Names(BACK_INPUTS + BACK_TABLES + BACK_OUTPUTS + scratch_names, refs)
     rows, width = m.tok_own.shape
-    hidden = m.h_own.shape[2]
+    hidden = m.h.shape[3]
     per_x = hidden // CHUNK
     n_wide = 3 * per_x
     n_chunks = n_wide + 2
@@ -326,18 +326,25 @@
             cols = pl.ds(pl.multiple_of(lax.rem(c, per_x) * CHUNK, CHUNK), CHUNK)
             return [
                 pltpu.make_async_copy(
-                    h.at[c // per_x, :, cols], y_v.at[slot, at], m.h_sem.at[slot, j]
+                    m.h.at[j, c // per_x, :, cols], y_v.at[slot, at], m.h_sem.at[slot, j]
                 )
-                for j, (h, at) in enumerate(((m.h_own, own_rows), (m.h_oth, oth_rows)))
+                for j, at in enumerate((own_rows, oth_rows))
             ]
 
         start(fetch(0))
         start(loads)
         packs[0].wait()
-
-        def chunk(c, which):
+        loads[0].wait()
+
+        def chunk(c, carry):
             slot = lax.rem(c, 2)
+            which = jnp.minimum(c // per_x, 1)
             wait(fetch(c))
+
+            @pl.when(c == per_x)
+            def _():
+                packs[1].wait()
+                attn_load.start()
 
             @pl.when(c + 1 < n_wide)
             def _():
@@ -359,33 +366,27 @@
             def _():
                 start(first_copies(c - 1))
 
+            @pl.when(c == n_wide - 4)
+            def _():
+                do_copy.wait_recv()
+                branch_copy.start()
+
             @pl.when((c == n_wide - 4) | (c == n_wide - 2))
             def _():
                 tick((c - n_wide + 4) // 2)
 
-        def first(c, carry):
-            chunk(c, 0)
             return carry
 
-        lax.fori_loop(0, per_x, first, 0)
-        packs[1].wait()
-        attn_load.start()
-
-        def second(c, carry):
-            chunk(c, 1)
-            return carry
-
-        lax.fori_loop(per_x, n_wide, second, 0)
+        lax.fori_loop(0, n_wide, chunk, 0)
         add_core(n_wide - 1)
         tick(2)
 
     pl.run_scoped(wide_phase, pltpu.VMEM((2, 2 * rows, CHUNK), BF16))
     start(tiles(0))
 
-    wait(loads)
+    wait(loads[1:])
     attn_load.wait()
-    branch_copy.start()
-    do_copy.wait_recv()
+    y_copy.start()
 
     def narrow_chunk(p):
         c = n_wide + p
@@ -509,7 +510,6 @@
                 @pl.when(p == 0)
                 def _():
                     branch_copy.wait_recv()
-                    y_copy.start()
                     pack_columns(m.packed.at[1], 0, m.branch_v)
                     pack_columns(m.packed.at[1], rows, m.branch_recv)
 
@@ -566,7 +566,7 @@
         tick(n_chunks - 3)
         for i in range(rows // BLOCK):
             grad, part = grad_and_gain(pl.ds(i * BLOCK, BLOCK))
-            ga_own[i * BLOCK : (i + 1) * BLOCK, :] = grad
+            ga_own[i * BLOCK : (i + 1) * BLOCK, :] = grad.astype(BF16)
             total += part
         ga_out_copy = local(3, ga_own, m.ga_out)
         ga_out_copy.start()
@@ -612,12 +612,12 @@
             total_copy(c).wait()
         ga_out_copy.wait()
 
-    pl.run_scoped(end_phase, pltpu.VMEM((rows, width), F32), pltpu.VMEM((2 * rows, width), BF16))
+    pl.run_scoped(end_phase, pltpu.VMEM((rows, width), BF16), pltpu.VMEM((2 * rows, width), BF16))
 
 
 def back(n_dp, values, tables):
     rows, width = values["tok_own"].shape
-    hidden = values["h_own"].shape[2]
+    hidden = values["h"].shape[3]
     seq = 2 * rows
     qc = values["w_q"].shape[1]
     n_chunks = 3 * hidden // CHUNK + 2
@@ -650,7 +650,7 @@
         in_specs=[anywhere] * len(BACK_INPUTS) + [vmem] * len(BACK_TABLES),
         out_specs=[anywhere, anywhere, anywhere, vmem, anywhere],
         out_shape=[
-            jax.ShapeDtypeStruct((rows, width), F32),
+            jax.ShapeDtypeStruct((rows, width), BF16),
             jax.ShapeDtypeStruct((rows, width), BF16),
             jax.ShapeDtypeStruct((n_chunks, block, CHUNK), F32), jax.ShapeDtypeStruct((24, PAIR), F32),
             jax.ShapeDtypeStruct((rows, width), BF16),
@@ -671,7 +671,7 @@
 FRONT_TABLES = ("segq", "segk", "cos", "sin", "gain1", "gain2", "qg", "kg")
 FRONT_OUTPUTS = (
     "q_oth", "kd_oth", "vd_oth", "qraw_oth", "kraw_oth", "o_own", "o_oth", "linv_own", "linv_oth",
-    "cot_pack", "ffn_pack", "attn_pack", "h_own", "h_oth", "base", "y_send", "gres", "branch", "do_own", "do_send",
+    "cot_pack", "ffn_pack", "attn_pack", "h", "base", "y_send", "branch", "do_own", "do_send",
     "gain_ffn",
 )
 PIECES = 4
@@ -768,7 +768,10 @@
         vx0[:, PAIR:] = jnp.where(both, one, 0.0).astype(BF16)
         vx1[:, PAIR:] = jnp.where(both, 0.0, one).astype(BF16)
 
-        def half(part, first):
+        def half(which, carry):
+            part = 1 - which
+            first = lax.rem(part + t, 2) * (nb // 2)
+
             def group(g, carry):
                 lanes = pl.ds(pl.multiple_of(g * PAIR, PAIR), PAIR)
                 for i in range(2):
@@ -778,11 +781,11 @@
                     kx1[at, :PAIR] = jnp.where(low, zero, k)
                     vx0[at, :PAIR] = jnp.where(low, v, zero)
                     vx1[at, :PAIR] = jnp.where(low, zero, v)
-                for i in range(rows // BLOCK):
-                    at = pl.ds(i * BLOCK, BLOCK)
-                    q = jnp.concatenate(
-                        [m.q_v[part, at, lanes], m.segq[pl.ds(part * rows + i * BLOCK, BLOCK), :]], axis=1
-                    )
+
+                def q_block(i, c):
+                    at = pl.ds(pl.multiple_of(i * BLOCK, BLOCK), BLOCK)
+                    seg_at = pl.ds(pl.multiple_of(part * rows + i * BLOCK, BLOCK), BLOCK)
+                    q = jnp.concatenate([m.q_v[part, at, lanes], m.segq[seg_at, :]], axis=1)
                     block = first + i
 
                     def step(kb, diagonal):
@@ -807,13 +810,21 @@
                     inverse = 1.0 / acc[:, PAIR:]
                     m.o_v[part, at, lanes] = (acc[:, :PAIR] * inverse).astype(BF16)
                     m.linv_v[part, at, lanes] = inverse
+                    return c
+
+                lax.fori_loop(0, rows // BLOCK, q_block, 0)
                 return carry
 
             lax.fori_loop(0, qc // PAIR, group, 0)
 
-        half(1, (1 - t) * (nb // 2))
-        o_copy.start()
-        half(0, t * (nb // 2))
+            @pl.when(which == 0)
+            def _():
+                o_copy.start()
+                cot_copies[3].start()
+
+            return carry
+
+        lax.fori_loop(0, 2, half, 0)
 
     pl.run_scoped(
         attention_phase, *[pltpu.VMEM((2 * rows, 2 * PAIR), BF16)] * 4, pltpu.VMEM((BLOCK, 2 * PAIR), F32)
@@ -838,40 +849,38 @@
         m.resid_v[at, :] = resid
         m.ffn_v[0, at, :] = (resid * row_norm(resid) * m.gain2[...]).astype(BF16)
         ffn_copies[i].start()
-        if i == 0:
-            for copy in cot_copies[3:]:
-                copy.start()
 
     for copy in loads[9:]:
         copy.wait()
     n_tiles = hidden // CHUNK
-    h_dst = (m.h_own, m.h_oth)
-    h_count = [0]
-
-    def feed_forward(part, at):
-        x, c = m.ffn_v.at[part, at], m.cot_v.at[part, at]
-
-        def h_copy(slot, f, rows_at, dst):
-            cols = pl.ds(pl.multiple_of(f * CHUNK, CHUNK), CHUNK)
-            return pltpu.make_async_copy(m.h_v.at[slot], dst.at[:, rows_at, cols], m.h_sem.at[slot])
-
-        base = h_count[0]
-        h_count[0] += n_tiles
-
-        def tile(f, carry):
-            slot = lax.rem(base + f, 2)
+
+    def h_copy(slot, part, at, f):
+        cols = pl.ds(pl.multiple_of(f * CHUNK, CHUNK), CHUNK)
+        return pltpu.make_async_copy(m.h_v.at[slot], m.h.at[part, :, at, cols], m.h_sem.at[slot])
+
+    def piece(n, carry):
+        part = lax.rem((n + 1) // 2, 2)
+        at = pl.ds(pl.multiple_of((n // 2) * BLOCK, BLOCK), BLOCK)
+        to = pl.ds(pl.multiple_of((2 * part + (1 - part) * (n // 3)) * BLOCK, BLOCK), BLOCK)
+        for i in range(2):
+            @pl.when(n == 1 + i)
+            def _():
+                ffn_copies[i].wait_recv()
+                for copy in cot_copies[2 * i : 2 * i + 2]:
+                    copy.wait_recv()
+
+        def tile(f, c):
+            slot = lax.rem(n * n_tiles + f, 2)
             cols = pl.ds(pl.multiple_of(f * CHUNK, CHUNK), CHUNK)
             up_cols = pl.ds(pl.multiple_of(hidden + f * CHUNK, CHUNK), CHUNK)
-            gate = dot_nn(x[...], m.wgu_v[:, cols])
-            up = dot_nn(x[...], m.wgu_v[:, up_cols])
-            grad = dot_nt(c[...], m.wd_v[cols, :])
-
-            if base == 0:
-                @pl.when(f >= 2)
-                def _():
-                    h_copy(slot, f, at, h_dst[part]).wait()
-            else:
-                h_copy(slot, f, at, h_dst[part]).wait()
+            x = m.ffn_v[part, at, :]
+            gate = dot_nn(x, m.wgu_v[:, cols])
+            up = dot_nn(x, m.wgu_v[:, up_cols])
+            grad = dot_nt(m.cot_v[part, at, :], m.wd_v[cols, :])
+
+            @pl.when(n * n_tiles + f >= 2)
+            def _():
+                h_copy(slot, part, at, f).wait()
 
             sig = 0.5 * jnp.tanh(0.5 * gate) + 0.5
             silu = gate * sig
@@ -880,40 +889,41 @@
             gu = (grad * silu).astype(BF16)
             for i, value in enumerate((mixed, gg, gu)):
                 m.h_v[slot, i] = value
-            h_copy(slot, f, at, h_dst[part]).start()
+            h_copy(slot, part, at, f).start()
             y = dot_nn(mixed, m.wd_v[cols, :])
             gf = dot_nt(gg, m.wgu_v[:, cols]) + dot_nt(gu, m.wgu_v[:, up_cols])
 
-            y_to, gf_to = (m.y_oth, m.gf_oth) if part else (m.y_v.at[at], m.gf_v.at[at])
-
             @pl.when(f == 0)
             def _():
-                y_to[...] = y
-                gf_to[...] = gf
+                m.y_v[to, :] = y
+                m.gf_v[to, :] = gf
 
             @pl.when(f > 0)
             def _():
-                y_to[...] += y
-                gf_to[...] += gf
-
-            return carry
+                m.y_v[to, :] += y
+                m.gf_v[to, :] += gf
+
+            return c
 
         lax.fori_loop(0, n_tiles, tile, 0)
 
-    feed_forward(0, halves[0])
-    pack_columns(m.cot_pack_v, 0, m.cot_v.at[0])
-    attn_store.wait()
-    pack_columns(m.ffn_pack_v, 0, m.ffn_v.at[0])
-    for i, at in enumerate(halves):
-        ffn_copies[i].wait_recv()
-        for copy in cot_copies[2 * i : 2 * i + 2]:
-            copy.wait_recv()
-        feed_forward(1, at)
-        m.gf_send[at, :] = m.gf_oth[...].astype(BF16)
-        gf_copies[i].start()
-        m.y_low[at, :] = m.y_oth[...].astype(BF16)
-    store(m.y_low, m.y_send)
-    feed_forward(0, halves[1])
+        @pl.when(n == 0)
+        def _():
+            pack_columns(m.cot_pack_v, 0, m.cot_v.at[0])
+            attn_store.wait()
+            pack_columns(m.ffn_pack_v, 0, m.ffn_v.at[0])
+
+        for i in range(2):
+            @pl.when(n == 1 + i)
+            def _():
+                m.gf_send[halves[i], :] = m.gf_v[2 * BLOCK :, :].astype(BF16)
+                gf_copies[i].start()
+                m.attn_v[1, halves[i], :] = m.y_v[2 * BLOCK :, :].astype(BF16)
+
+        return carry
+
+    lax.fori_loop(0, 4, piece, 0)
+    store(m.attn_v.at[1], m.y_send)
     pack_columns(m.cot_pack_v, rows, m.cot_v.at[1])
     pack_columns(m.ffn_pack_v, rows, m.ffn_v.at[1])
     store(m.cot_pack_v, m.cot_pack)
@@ -931,22 +941,21 @@
         gres = m.cot_v[0, at, :].astype(F32) + inverse * (
             w - normed * jnp.mean(w * normed, axis=-1, keepdims=True)
         )
-        m.gf_v[at, :] = gres
         branch = gres.astype(BF16)
-        m.branch_v[at, :] = branch
+        m.attn_v[0, at, :] = branch
         m.do_v[0, at, :] = dot_nt(branch, m.wom_v[...]).astype(BF16)
         m.do_v[1, at, :] = dot_nt(branch, m.wot_v[...]).astype(BF16)
-        m.y_v[at, :] += resid
+        m.tok_v[0, at, :] = (m.y_v[at, :] + resid).astype(BF16)
     for src, dst in (
-        (m.do_v.at[1], m.do_send), (m.do_v.at[0], m.do_own), (m.branch_v, m.branch), (m.gf_v, m.gres),
-        (m.y_v, m.base),
+        (m.do_v.at[1], m.do_send), (m.do_v.at[0], m.do_own), (m.attn_v.at[0], m.branch),
+        (m.tok_v.at[0], m.base),
     ):
         store(src, dst)
     m.gain_ffn[...] = total
     for copy in (*cot_copies, wo_copy, wo_core, o_copy, *ffn_copies, *gf_copies):
         copy.wait_send()
     for slot in range(2):
-        pltpu.make_async_copy(m.h_v.at[slot], m.h_own.at[:, halves[1], pl.ds(0, CHUNK)], m.h_sem.at[slot]).wait()
+        pltpu.make_async_copy(m.h_v.at[slot], m.h.at[0, :, halves[1], pl.ds(0, CHUNK)], m.h_sem.at[slot]).wait()
     for copy in stores:
         copy.wait()
 
@@ -966,11 +975,10 @@
         attn_v=vm((2, rows, width), BF16), qraw_v=vm((rows, qc), BF16), kraw_v=vm((rows, qc // 2), BF16),
         o_v=vm((2, rows, qc), BF16), linv_v=vm((2, rows, qc), F32), theirs=vm((rows, qc), BF16),
         resid_v=vm((rows, width), F32), ffn_v=vm((2, rows, width), BF16),
-        h_v=vm((2, 3, BLOCK, CHUNK), BF16), y_v=vm((rows, width), F32), gf_v=vm((rows, width), F32),
-        y_oth=vm((BLOCK, width), F32), gf_oth=vm((BLOCK, width), F32),
-        y_low=vm((rows, width), BF16), gf_send=vm((rows, width), BF16), gf_in=vm((rows, width), BF16),
+        h_v=vm((2, 3, BLOCK, CHUNK), BF16), y_v=vm((3 * BLOCK, width), F32), gf_v=vm((3 * BLOCK, width), F32),
+        gf_send=vm((rows, width), BF16), gf_in=vm((rows, width), BF16),
         cot_pack_v=vm((2, seq, width // 2), BF16),
-        ffn_pack_v=vm((2, seq, width // 2), BF16), branch_v=vm((rows, width), BF16), do_v=vm((2, rows, qc), BF16),
+        ffn_pack_v=vm((2, seq, width // 2), BF16), do_v=vm((2, rows, qc), BF16),
         r_send=dma((11,)), r_recv=dma((11,)), l_sem=dma((13,)), o_sem=dma((20,)), h_sem=dma((2,)),
     )
     anywhere = pl.BlockSpec(memory_space=pl.ANY)
@@ -981,8 +989,8 @@
         qraw_oth=low(rows, qc), kraw_oth=low(rows, qc // 2), o_own=low(rows, qc), o_oth=low(rows, qc),
         linv_own=full(rows, qc), linv_oth=full(rows, qc),
         cot_pack=low(2, seq, width // 2), ffn_pack=low(2, seq, width // 2), attn_pack=low(2, seq, width // 2),
-        h_own=low(3, rows, hidden), h_oth=low(3, rows, hidden), base=full(rows, width), y_send=low(rows, width),
-        gres=full(rows, width), branch=low(rows, width), do_own=low(rows, qc), do_send=low(rows, qc),
+        h=low(2, 3, rows, hidden), base=low(rows, width), y_send=low(rows, width),
+        branch=low(rows, width), do_own=low(rows, qc), do_send=low(rows, qc),
         gain_ffn=full(1, width),
     )
     outs = pl.pallas_call(
@@ -1001,15 +1009,15 @@
 
 
 def finish_kernel(
-    base_ref, yr_ref, ga_ref, gr_ref, x_ref, gres_ref, gain_ref, shards_ref,
-    out_ref, gt_ref, q_ref, kv_ref, o_ref, gu_ref, down_ref,
+    base_ref, yr_ref, ga_ref, gr_ref, x_ref, gres_ref, gain_ref, shards_ref, gains_ref,
+    out_ref, gt_ref, q_ref, kv_ref, o_ref, g1_ref, g2_ref, gq_ref, gk_ref, gu_ref, down_ref,
 ):
-    out_ref[...] = (base_ref[...] + yr_ref[...].astype(F32)).astype(BF16)
+    out_ref[...] = (base_ref[...].astype(F32) + yr_ref[...].astype(F32)).astype(BF16)
     x = x_ref[...].astype(F32)
     inverse = row_norm(x)
     normed = x * inverse
-    w = (ga_ref[...] + gr_ref[...].astype(F32)) * gain_ref[...]
-    gt_ref[...] = gres_ref[...] + inverse * (w - normed * jnp.mean(w * normed, axis=-1, keepdims=True))
+    w = (ga_ref[...].astype(F32) + gr_ref[...].astype(F32)) * gain_ref[...]
+    gt_ref[...] = gres_ref[...].astype(F32) + inverse * (w - normed * jnp.mean(w * normed, axis=-1, keepdims=True))
     n_chunks = shards_ref.shape[0]
     per_x = (n_chunks - 2) // 3
     two = 2 * PAIR
@@ -1023,6 +1031,12 @@
 
     @pl.when(step == per_x)
     def _():
+        n = g1_ref.shape[0]
+        g1_ref[...] = gains_ref[:n, :]
+        g2_ref[...] = gains_ref[n : 2 * n, :]
+        for i, ref in enumerate((gq_ref, gk_ref)):
+            row = gains_ref[2 * n + i : 2 * n + i + 1, :]
+            ref[...] = row[:, :64] + row[:, 64:]
         for p in range(2):
             shard = shards_ref[3 * per_x + p]
             q_ref[:, p * two : (p + 1) * two] = shard[:, :two]
@@ -1031,21 +1045,23 @@
             o_ref[:, p * two : (p + 1) * two] = shard[:, 2 * two :]
 
 
-def finish(base, y_recv, ga_own, ga_recv, x, gres, gain, shards):
+def finish(base, y_recv, ga_own, ga_recv, x, gres, gain, shards, gains):
     rows, width = x.shape
     n_chunks, block, _ = shards.shape
     hidden = (n_chunks - 2) // 3 * CHUNK
     per_x = hidden // CHUNK
     row = pl.BlockSpec((rows // (per_x + 1), width), lambda i: (i, 0))
     fixed = lambda shape: pl.BlockSpec(shape, lambda i: (0,) * len(shape))
-    shapes = [(block, SPLIT), (block, 2, SPLIT // 2), (block, SPLIT), (block, 2, hidden), (block, hidden)]
+    m = width // PAIR
+    shapes = [(block, SPLIT), (block, 2, SPLIT // 2), (block, SPLIT), (m, PAIR), (m, PAIR), (1, 64), (1, 64)]
+    shapes += [(block, 2, hidden), (block, hidden)]
     piece = lambda i: jnp.minimum(i, per_x - 1)
     return pl.pallas_call(
         finish_kernel,
         grid=(per_x + 1,),
-        in_specs=[row] * 6 + [fixed((1, width)), fixed(shards.shape)],
+        in_specs=[row] * 6 + [fixed((1, width)), fixed(shards.shape), fixed(gains.shape)],
         out_specs=[row, row]
-        + [fixed(shape) for shape in shapes[:3]]
+        + [fixed(shape) for shape in shapes[:7]]
         + [
             pl.BlockSpec((block, 2, CHUNK), lambda i: (0, 0, piece(i))),
             pl.BlockSpec((block, CHUNK), lambda i: (0, piece(i))),
@@ -1055,7 +1071,7 @@
         compiler_params=pltpu.CompilerParams(vmem_limit_bytes=VMEM_LIMIT),
         cost_estimate=cost(6e-6),
         name="finish",
-    )(base, y_recv, ga_own, ga_recv, x, gres, gain, shards)
+    )(base, y_recv, ga_own, ga_recv, x, gres, gain, shards, gains)
 
 
 def swap(value, axis, size, bit):
@@ -1109,21 +1125,19 @@
     values.update(front(values, tables))
     tables.update(gain_ffn=values["gain_ffn"])
     ga_own, ga_recv, shards, gains, y_recv = back(n_dp, values, tables)
-    m = width // PAIR
-    fold = lambda row: row[:head_dim] + row[head_dim:]
-    output, grad_tokens, grad_q, grad_kv, grad_o, grad_gu, grad_down = finish(
-        values["base"], y_recv, ga_own, ga_recv, tokens, values["gres"], gain1, shards
+    output, grad_tokens, grad_q, grad_kv, grad_o, sum_1, sum_2, sum_q, sum_k, grad_gu, grad_down = finish(
+        values["base"], y_recv, ga_own, ga_recv, tokens, values["branch"], gain1, shards, gains
     )
     return (
         output,
         grad_tokens,
-        gains[:m].reshape(width),
+        sum_1.reshape(width),
         grad_q,
         grad_kv,
-        fold(gains[2 * m]),
-        fold(gains[2 * m + 1]),
+        sum_q.reshape(head_dim),
+        sum_k.reshape(head_dim),
         grad_o.T,
-        gains[m : 2 * m].reshape(width),
+        sum_2.reshape(width),
         grad_gu,
         grad_down.T,
     )

time: 279 us -> 266 us (0.953); the launches traced: 273 us -> 266 us
  Pallas kernels: 248 us -> 243 us
    pallas_call x1, Pallas kernels: 128 us -> 125 us  [back(): pl.pallas_call(functools.partial(back_kernel, n_dp, tuple(scratch)), in_s...]
  transfers between devices with their start and end apart: 1 -> 1, of which waited for: 0 -> 1; matrix products, arithmetic and copies ran while one was open for 6% -> 6% of each run, Pallas kernels for 2% -> 2%
where the time goes in v4:
time: 266 us
  Pallas kernels  243 us (91%)
  local copies, waits for them, and re-layouts  11.1 us (4%)
  other arithmetic  6.91 us (3%)
  starting transfers between devices  3.03 us (1%)
    pallas_call x1, Pallas kernels, back(): pl.pallas_call(functools.partial(back_kernel, n_dp, tuple(scratch)), in_s...  125 us
    pallas_call x1, Pallas kernels, front(): pl.pallas_call(functools.partial(front_kernel, tuple(scratch)), in_specs=...  105 us
    unnamed x8, local copies, waits for them, and re-layouts  11.1 us
    pallas_call x1, Pallas kernels, finish(): pl.pallas_call(finish_kernel, grid=(per_x + 1,), in_specs=[row] * 6 + [fi...  7.25 us
    pallas_call x1, Pallas kernels, qkv(): pl.pallas_call(qkv_kernel, grid=(nb,), in_specs=[row(width), whole((1, wi...  6.09 us
  transfers between devices with their start and end apart: 1, of which 1 were waited for; matrix products, arithmetic and copies ran while one was open for 6% of the time, Pallas kernels for 2%

profile of v4, /device:TPU:0, one launch (start us, length us, event | category | flops | bytes accessed | tf_op | source)
XLA Modules:
  0.0 265.6 jit_solution(15192082639812742159)
XLA Ops:
  0.6 0.0 copy-start.1
  0.7 3.0 %collective-permute-start = (bf16[512,1024]{1,0:T(8,128)(2,1)}, bf16[512,1024]{1,0:T(8,128)(2,1)S(1)}, u32[]{:S(2)}, u32[]{:S(2)}) collective-permute-start(bf16[512,1024]{1,0:T(8,128)(2,1)} %x_ref.3), channel_id=1, source_target_pairs={{0,1},{1,0},{2,3},{3,2},{4,5},{5,4},{6,7},{7,6},{8,9},{9,8},{10,11... | collective-permute-start | bytes 3145736 | tf_op jit(solution)/shard_map/ppermute | solution.py:1078
  3.7 1.3 maximum_bitcast_fusion
  5.0 1.9 fusion.2
  6.9 1.8 pad_maximum_fusion
  8.8 0.0 copy-done.1
  8.8 1.2 copy.24
  10.0 8.9 %copy.25 = bf16[128,8,2,2304]{3,1,2,0:T(8,128)(2,1)} copy(bf16[128,8,2,2304]{3,2,1,0:T(2,128)(2,1)} %bitcast.24) | data formatting | bytes 18874368
  18.9 0.0 copy-start.2
  18.9 6.1 %qkv.1 = (bf16[512,1024]{1,0:T(8,128)(2,1)}, bf16[512,512]{1,0:T(8,128)(2,1)}, bf16[512,512]{1,0:T(8,128)(2,1)}, bf16[512,512]{1,0:T(8,128)(2,1)}, bf16[512,512]{1,0:T(8,128)(2,1)}, /*index=5*/bf16[512,256]{1,0:T(8,128)(2,1)}) custom-call(bf16[512,1024]{1,0:T(8,128)(2,1)} %x_ref.3, f32[1,1024]{1,0:T(1,128)} %bitcast.26, bf16[1024,512]{1,0:T(8,128)(2,1)} %refs_10_.1, ...), custom_call_target="tpu_custom_call" | custom-call | flops 50000000 | tf_op jit(solution)/shard_map/qkv/pallas_call | solution.py:100
  25.0 0.0 copy-done.2
  25.1 0.9 fusion.1.refs_13_.refs_27_
  26.0 0.9 subtract_convert_fusion.refs_12_.refs_26_
  26.9 0.2 collective-permute-done.refs_1_.refs_5_
  27.1 0.0 copy-start
  27.1 1.0 copy-done
  28.0 105.4 %front.1 = (bf16[512,512]{1,0:T(8,128)(2,1)}, bf16[512,512]{1,0:T(8,128)(2,1)}, bf16[512,512]{1,0:T(8,128)(2,1)}, bf16[512,512]{1,0:T(8,128)(2,1)}, bf16[512,256...) custom-call(bf16[512,1024]{1,0:T(8,128)(2,1)} %x_ref.3, ...), custom_call_target="tpu_custom_call" | custom-call | flops 1000000000 | tf_op jit(solution)/shard_map/front/pallas_call | solution.py:996
  133.4 124.8 %back.1 = (bf16[512,1024]{1,0:T(8,128)(2,1)}, bf16[512,1024]{1,0:T(8,128)(2,1)}, f32[11,64,768]{2,1,0:T(8,128)}, f32[24,128]{1,0:T(8,128)}, bf16[512,1024]{1,0:T(8,128)(2,1)}) custom-call(bf16[2,3,512,2304]{3,2,1,0:T(8,128)(2,1)} %get-tuple-element.57.refs_0_, bf16[2,1024,512]{2,1,0:T(8,128)(2,1)} %get-tuple-element.58.refs_1_, ...), custom_call_target="tpu_custom_call" | custom-call | flops 1000000000 | tf_op jit(solution)/shard_map/back/pallas_call | solution.py:648
  258.2 7.2 %finish.1 = (bf16[512,1024]{1,0:T(8,128)(2,1)}, f32[512,1024]{1,0:T(8,128)}, f32[64,512]{1,0:T(8,128)}, f32[64,2,256]{2,1,0:T(2,128)}, f32[64,512]{1,0:T(8,128)}...) custom-call(bf16[512,1024]{1,0:T(8,128)(2,1)} %get-tuple-element.56., ...), custom_call_target="tpu_custom_call" | custom-call | flops 60000000 | tf_op jit(solution)/shard_map/finish/pallas_call | solution.py:1059
  (6 shorter events, 0.0 us)
Async XLA Ops:
  0.6 8.1 %copy-start.1 = (bf16[1024,2,256]{2,1,0:T(2,128)(2,1)S(1)}, bf16[1024,2,256]{2,1,0:T(2,128)(2,1)}, u32[]{:S(2)}) copy-start(bf16[1024,2,256]{2,1,0:T(2,128)(2,1)} %param.16) | copy-start | bytes 3145732
  0.7 26.4 %collective-permute-start = (bf16[512,1024]{1,0:T(8,128)(2,1)}, bf16[512,1024]{1,0:T(8,128)(2,1)S(1)}, u32[]{:S(2)}, u32[]{:S(2)}) collective-permute-start(bf16[512,1024]{1,0:T(8,128)(2,1)} %x_ref.3), channel_id=1, source_target_pairs={{0,1},{1,0},{2,3},{3,2},{4,5},{5,4},{6,7},{7,6},{8,9},{9,8},{10,11... | collective-permute-start | bytes 3145736 | tf_op jit(solution)/shard_map/ppermute | solution.py:1078
  18.9 6.1 %copy-start.2 = (s32[1,1024]{1,0:T(1,128)S(1)}, s32[1,1024]{1,0:T(1,128)}, u32[]{:S(2)}) copy-start(s32[1,1024]{1,0:T(1,128)} %param.13) | copy-start | bytes 12292
  27.1 1.0 copy-start

commit v5 on v4

--- a/solution.py
+++ b/solution.py
@@ -687,13 +687,15 @@
     t = lax.axis_index("tensor")
     d = lax.axis_index("dp")
     core = lax.rem(d, 2)
+    x_at = lax.rem(d // 2, 2)
+    over_x = {"dp": d + 2 - 4 * x_at}
     over_t = {"tensor": 1 - t}
     over_core = {"dp": d + 1 - 2 * core}
 
     barrier = pltpu.get_barrier_semaphore()
-    for p in (over_t, over_core):
+    for p in (over_t, over_core, over_x):
         pl.semaphore_signal(barrier, inc=1, device_id=p, device_id_type=MESH)
-    pl.semaphore_wait(barrier, 2)
+    pl.semaphore_wait(barrier, 3)
 
     def remote(i, src, dst, device):
         return pltpu.make_async_remote_copy(
@@ -704,10 +706,18 @@
     pieces = [pl.ds(i * (rows // PIECES), rows // PIECES) for i in range(PIECES)]
     halves = [pl.ds(i * BLOCK, BLOCK) for i in range(rows // BLOCK)]
     cot_copies = [remote(i, m.cot_own.at[at], m.cot_v.at[1, at], over_t) for i, at in enumerate(pieces)]
-    half_o = qc // 2
-    mine_o = pl.ds(pl.multiple_of(core * half_o, half_o), half_o)
+    part_o = qc // 4
+
+    def wo_part(x_of, core_of):
+        return pl.ds(pl.multiple_of((2 * x_of + core_of) * part_o, part_o), part_o)
+
+    mine_o, core_o = wo_part(x_at, core), wo_part(x_at, 1 - core)
     wo_copy = remote(4, m.w_o.at[mine_o], m.wot_v.at[mine_o], over_t)
     wo_core = remote(5, m.wot_v.at[mine_o], m.wot_v.at[mine_o], over_core)
+    wo_x = (
+        remote(11, m.wot_v.at[mine_o], m.wot_v.at[mine_o], over_x),
+        remote(12, m.wot_v.at[core_o], m.wot_v.at[core_o], over_x),
+    )
     o_copy = remote(6, m.o_v.at[1], m.theirs, over_t)
     ffn_copies = [remote(7 + i, m.ffn_v.at[0, at], m.ffn_v.at[1, at], over_t) for i, at in enumerate(halves)]
     gf_copies = [remote(9 + i, m.gf_send.at[at], m.gf_in.at[at], over_t) for i, at in enumerate(halves)]
@@ -754,6 +764,7 @@
         store(src, dst)
     wo_copy.wait_recv()
     wo_core.start()
+    wo_x[0].start()
 
     def place(block):
         return pl.ds(pl.multiple_of(lax.rem(block + t * (nb // 2), nb) * BLOCK, BLOCK), BLOCK)
@@ -820,6 +831,8 @@
             @pl.when(which == 0)
             def _():
                 o_copy.start()
+                wo_core.wait_recv()
+                wo_x[1].start()
                 cot_copies[3].start()
 
             return carry
@@ -840,7 +853,8 @@
     pack_columns(m.ffn_pack_v, rows, m.attn_v.at[1])
     attn_store = local(12, m.ffn_pack_v, m.attn_pack)
     attn_store.start()
-    wo_core.wait_recv()
+    for copy in wo_x:
+        copy.wait_recv()
     o_copy.wait_recv()
     for i, at in enumerate(halves):
         resid = (
@@ -952,7 +966,7 @@
     ):
         store(src, dst)
     m.gain_ffn[...] = total
-    for copy in (*cot_copies, wo_copy, wo_core, o_copy, *ffn_copies, *gf_copies):
+    for copy in (*cot_copies, wo_copy, wo_core, *wo_x, o_copy, *ffn_copies, *gf_copies):
         copy.wait_send()
     for slot in range(2):
         pltpu.make_async_copy(m.h_v.at[slot], m.h.at[0, :, halves[1], pl.ds(0, CHUNK)], m.h_sem.at[slot]).wait()
@@ -979,7 +993,7 @@
         gf_send=vm((rows, width), BF16), gf_in=vm((rows, width), BF16),
         cot_pack_v=vm((2, seq, width // 2), BF16),
         ffn_pack_v=vm((2, seq, width // 2), BF16), do_v=vm((2, rows, qc), BF16),
-        r_send=dma((11,)), r_recv=dma((11,)), l_sem=dma((13,)), o_sem=dma((20,)), h_sem=dma((2,)),
+        r_send=dma((13,)), r_recv=dma((13,)), l_sem=dma((13,)), o_sem=dma((20,)), h_sem=dma((2,)),
     )
     anywhere = pl.BlockSpec(memory_space=pl.ANY)
     vmem = pl.BlockSpec(memory_space=pltpu.VMEM)

time: 266 us -> 261 us (0.981)
  Pallas kernels: 243 us -> 238 us
    pallas_call x1, Pallas kernels: 105 us -> 101 us  [front(): pl.pallas_call(functools.partial(front_kernel, tuple(scratch)), in_specs=...]
  transfers between devices with their start and end apart: 1 -> 1, of which waited for: 1 -> 1; matrix products, arithmetic and copies ran while one was open for 6% -> 7% of each run, Pallas kernels for 2% -> 2%
where the time goes in v5:
time: 261 us; the launch traced here: 260 us
  Pallas kernels  238 us (91%)
  local copies, waits for them, and re-layouts  11.1 us (4%)
  other arithmetic  6.91 us (3%)
  starting transfers between devices  3.03 us (1%)
    pallas_call x1, Pallas kernels, back(): pl.pallas_call(functools.partial(back_kernel, n_dp, tuple(scratch)), in_s...  123 us
    pallas_call x1, Pallas kernels, front(): pl.pallas_call(functools.partial(front_kernel, tuple(scratch)), in_specs=...  101 us
    unnamed x8, local copies, waits for them, and re-layouts  11.1 us
    pallas_call x1, Pallas kernels, finish(): pl.pallas_call(finish_kernel, grid=(per_x + 1,), in_specs=[row] * 6 + [fi...  7.25 us
    pallas_call x1, Pallas kernels, qkv(): pl.pallas_call(qkv_kernel, grid=(nb,), in_specs=[row(width), whole((1, wi...  6.09 us
  transfers between devices with their start and end apart: 1, of which 1 were waited for; matrix products, arithmetic and copies ran while one was open for 7% of the time, Pallas kernels for 2%

profile of v5, /device:TPU:0, one launch (start us, length us, event | category | flops | bytes accessed | tf_op | source)
XLA Modules:
  0.0 260.0 jit_solution(10187338684058672626)
XLA Ops:
  0.6 0.0 copy-start.1
  0.7 3.0 %collective-permute-start = (bf16[512,1024]{1,0:T(8,128)(2,1)}, bf16[512,1024]{1,0:T(8,128)(2,1)S(1)}, u32[]{:S(2)}, u32[]{:S(2)}) collective-permute-start(bf16[512,1024]{1,0:T(8,128)(2,1)} %x_ref.3), channel_id=1, source_target_pairs={{0,1},{1,0},{2,3},{3,2},{4,5},{5,4},{6,7},{7,6},{8,9},{9,8},{10,11... | collective-permute-start | bytes 3145736 | tf_op jit(solution)/shard_map/ppermute | solution.py:1092
  3.7 1.3 maximum_bitcast_fusion
  5.0 1.9 fusion.2
  6.9 1.8 pad_maximum_fusion
  8.8 0.0 copy-done.1
  8.8 1.2 copy.24
  10.0 8.9 %copy.25 = bf16[128,8,2,2304]{3,1,2,0:T(8,128)(2,1)} copy(bf16[128,8,2,2304]{3,2,1,0:T(2,128)(2,1)} %bitcast.24) | data formatting | bytes 18874368
  18.9 0.0 copy-start.2
  18.9 6.1 %qkv.1 = (bf16[512,1024]{1,0:T(8,128)(2,1)}, bf16[512,512]{1,0:T(8,128)(2,1)}, bf16[512,512]{1,0:T(8,128)(2,1)}, bf16[512,512]{1,0:T(8,128)(2,1)}, bf16[512,512]{1,0:T(8,128)(2,1)}, /*index=5*/bf16[512,256]{1,0:T(8,128)(2,1)}) custom-call(bf16[512,1024]{1,0:T(8,128)(2,1)} %x_ref.3, f32[1,1024]{1,0:T(1,128)} %bitcast.26, bf16[1024,512]{1,0:T(8,128)(2,1)} %refs_10_.1, ...), custom_call_target="tpu_custom_call" | custom-call | flops 50000000 | tf_op jit(solution)/shard_map/qkv/pallas_call | solution.py:100
  25.0 0.0 copy-done.2
  25.1 0.9 fusion.1.refs_13_.refs_27_
  26.0 0.9 subtract_convert_fusion.refs_12_.refs_26_
  26.9 0.2 collective-permute-done.refs_1_.refs_5_
  27.1 0.0 copy-start
  27.1 1.0 copy-done
  28.0 101.1 %front.1 = (bf16[512,512]{1,0:T(8,128)(2,1)}, bf16[512,512]{1,0:T(8,128)(2,1)}, bf16[512,512]{1,0:T(8,128)(2,1)}, bf16[512,512]{1,0:T(8,128)(2,1)}, bf16[512,256...) custom-call(bf16[512,1024]{1,0:T(8,128)(2,1)} %x_ref.3, ...), custom_call_target="tpu_custom_call" | custom-call | flops 1000000000 | tf_op jit(solution)/shard_map/front/pallas_call | solution.py:1010
  129.1 123.4 %back.1 = (bf16[512,1024]{1,0:T(8,128)(2,1)}, bf16[512,1024]{1,0:T(8,128)(2,1)}, f32[11,64,768]{2,1,0:T(8,128)}, f32[24,128]{1,0:T(8,128)}, bf16[512,1024]{1,0:T(8,128)(2,1)}) custom-call(bf16[2,3,512,2304]{3,2,1,0:T(8,128)(2,1)} %get-tuple-element.57.refs_0_, bf16[2,1024,512]{2,1,0:T(8,128)(2,1)} %get-tuple-element.58.refs_1_, ...), custom_call_target="tpu_custom_call" | custom-call | flops 1000000000 | tf_op jit(solution)/shard_map/back/pallas_call | solution.py:648
  252.6 7.2 %finish.1 = (bf16[512,1024]{1,0:T(8,128)(2,1)}, f32[512,1024]{1,0:T(8,128)}, f32[64,512]{1,0:T(8,128)}, f32[64,2,256]{2,1,0:T(2,128)}, f32[64,512]{1,0:T(8,128)}...) custom-call(bf16[512,1024]{1,0:T(8,128)(2,1)} %get-tuple-element.56., ...), custom_call_target="tpu_custom_call" | custom-call | flops 60000000 | tf_op jit(solution)/shard_map/finish/pallas_call | solution.py:1073
  (6 shorter events, 0.0 us)
Async XLA Ops:
  0.6 8.1 %copy-start.1 = (bf16[1024,2,256]{2,1,0:T(2,128)(2,1)S(1)}, bf16[1024,2,256]{2,1,0:T(2,128)(2,1)}, u32[]{:S(2)}) copy-start(bf16[1024,2,256]{2,1,0:T(2,128)(2,1)} %param.16) | copy-start | bytes 3145732
  0.7 26.4 %collective-permute-start = (bf16[512,1024]{1,0:T(8,128)(2,1)}, bf16[512,1024]{1,0:T(8,128)(2,1)S(1)}, u32[]{:S(2)}, u32[]{:S(2)}) collective-permute-start(bf16[512,1024]{1,0:T(8,128)(2,1)} %x_ref.3), channel_id=1, source_target_pairs={{0,1},{1,0},{2,3},{3,2},{4,5},{5,4},{6,7},{7,6},{8,9},{9,8},{10,11... | collective-permute-start | bytes 3145736 | tf_op jit(solution)/shard_map/ppermute | solution.py:1092
  18.9 6.1 %copy-start.2 = (s32[1,1024]{1,0:T(1,128)S(1)}, s32[1,1024]{1,0:T(1,128)}, u32[]{:S(2)}) copy-start(s32[1,1024]{1,0:T(1,128)} %param.13) | copy-start | bytes 12292
  27.1 1.0 copy-start

commit v6 on v5

--- a/solution.py
+++ b/solution.py
@@ -867,6 +867,7 @@
     for copy in loads[9:]:
         copy.wait()
     n_tiles = hidden // CHUNK
+    cot_store = local(13, m.cot_pack_v, m.cot_pack)
 
     def h_copy(slot, part, at, f):
         cols = pl.ds(pl.multiple_of(f * CHUNK, CHUNK), CHUNK)
@@ -880,8 +881,9 @@
             @pl.when(n == 1 + i)
             def _():
                 ffn_copies[i].wait_recv()
-                for copy in cot_copies[2 * i : 2 * i + 2]:
-                    copy.wait_recv()
+                if i == 0:
+                    for copy in cot_copies[:2]:
+                        copy.wait_recv()
 
         def tile(f, c):
             slot = lax.rem(n * n_tiles + f, 2)
@@ -933,14 +935,17 @@
                 m.gf_send[halves[i], :] = m.gf_v[2 * BLOCK :, :].astype(BF16)
                 gf_copies[i].start()
                 m.attn_v[1, halves[i], :] = m.y_v[2 * BLOCK :, :].astype(BF16)
+                if i == 0:
+                    for copy in cot_copies[2:]:
+                        copy.wait_recv()
+                    pack_columns(m.cot_pack_v, rows, m.cot_v.at[1])
+                    cot_store.start()
 
         return carry
 
     lax.fori_loop(0, 4, piece, 0)
     store(m.attn_v.at[1], m.y_send)
-    pack_columns(m.cot_pack_v, rows, m.cot_v.at[1])
     pack_columns(m.ffn_pack_v, rows, m.ffn_v.at[1])
-    store(m.cot_pack_v, m.cot_pack)
     store(m.ffn_pack_v, m.ffn_pack)
 
     total = jnp.zeros((1, width), F32)
@@ -970,6 +975,7 @@
         copy.wait_send()
     for slot in range(2):
         pltpu.make_async_copy(m.h_v.at[slot], m.h.at[0, :, halves[1], pl.ds(0, CHUNK)], m.h_sem.at[slot]).wait()
+    cot_store.wait()
     for copy in stores:
         copy.wait()
 
@@ -993,7 +999,7 @@
         gf_send=vm((rows, width), BF16), gf_in=vm((rows, width), BF16),
         cot_pack_v=vm((2, seq, width // 2), BF16),
         ffn_pack_v=vm((2, seq, width // 2), BF16), do_v=vm((2, rows, qc), BF16),
-        r_send=dma((13,)), r_recv=dma((13,)), l_sem=dma((13,)), o_sem=dma((20,)), h_sem=dma((2,)),
+        r_send=dma((13,)), r_recv=dma((13,)), l_sem=dma((14,)), o_sem=dma((20,)), h_sem=dma((2,)),
     )
     anywhere = pl.BlockSpec(memory_space=pl.ANY)
     vmem = pl.BlockSpec(memory_space=pltpu.VMEM)

time: 261 us -> 261 us (level)
  no operation moved by 1% of the time
where the time goes in v6:
time: 261 us; the launch traced here: 260 us
  Pallas kernels  238 us (91%)
  local copies, waits for them, and re-layouts  11.1 us (4%)
  other arithmetic  6.91 us (3%)
  starting transfers between devices  3.03 us (1%)
    pallas_call x1, Pallas kernels, back(): pl.pallas_call(functools.partial(back_kernel, n_dp, tuple(scratch)), in_s...  123 us
    pallas_call x1, Pallas kernels, front(): pl.pallas_call(functools.partial(front_kernel, tuple(scratch)), in_specs=...  101 us
    unnamed x8, local copies, waits for them, and re-layouts  11.1 us
    pallas_call x1, Pallas kernels, finish(): pl.pallas_call(finish_kernel, grid=(per_x + 1,), in_specs=[row] * 6 + [fi...  7.25 us
    pallas_call x1, Pallas kernels, qkv(): pl.pallas_call(qkv_kernel, grid=(nb,), in_specs=[row(width), whole((1, wi...  6.09 us
  transfers between devices with their start and end apart: 1, of which 1 were waited for; matrix products, arithmetic and copies ran while one was open for 7% of the time, Pallas kernels for 2%

profile of v6, /device:TPU:0, one launch (start us, length us, event | category | flops | bytes accessed | tf_op | source)
XLA Modules:
  0.0 259.9 jit_solution(11317742743295485232)
XLA Ops:
  0.6 0.0 copy-start.1
  0.7 3.0 %collective-permute-start = (bf16[512,1024]{1,0:T(8,128)(2,1)}, bf16[512,1024]{1,0:T(8,128)(2,1)S(1)}, u32[]{:S(2)}, u32[]{:S(2)}) collective-permute-start(bf16[512,1024]{1,0:T(8,128)(2,1)} %x_ref.3), channel_id=1, source_target_pairs={{0,1},{1,0},{2,3},{3,2},{4,5},{5,4},{6,7},{7,6},{8,9},{9,8},{10,11... | collective-permute-start | bytes 3145736 | tf_op jit(solution)/shard_map/ppermute | solution.py:1098
  3.7 1.3 maximum_bitcast_fusion
  5.0 1.9 fusion.2
  6.9 1.8 pad_maximum_fusion
  8.8 0.0 copy-done.1
  8.8 1.2 copy.24
  10.0 8.9 %copy.25 = bf16[128,8,2,2304]{3,1,2,0:T(8,128)(2,1)} copy(bf16[128,8,2,2304]{3,2,1,0:T(2,128)(2,1)} %bitcast.24) | data formatting | bytes 18874368
  18.9 0.0 copy-start.2
  18.9 6.1 %qkv.1 = (bf16[512,1024]{1,0:T(8,128)(2,1)}, bf16[512,512]{1,0:T(8,128)(2,1)}, bf16[512,512]{1,0:T(8,128)(2,1)}, bf16[512,512]{1,0:T(8,128)(2,1)}, bf16[512,512]{1,0:T(8,128)(2,1)}, /*index=5*/bf16[512,256]{1,0:T(8,128)(2,1)}) custom-call(bf16[512,1024]{1,0:T(8,128)(2,1)} %x_ref.3, f32[1,1024]{1,0:T(1,128)} %bitcast.26, bf16[1024,512]{1,0:T(8,128)(2,1)} %refs_10_.1, ...), custom_call_target="tpu_custom_call" | custom-call | flops 50000000 | tf_op jit(solution)/shard_map/qkv/pallas_call | solution.py:100
  25.0 0.0 copy-done.2
  25.1 0.9 fusion.1.refs_13_.refs_27_
  26.0 0.9 subtract_convert_fusion.refs_12_.refs_26_
  26.9 0.2 collective-permute-done.refs_1_.refs_5_
  27.1 0.0 copy-start
  27.1 1.0 copy-done
  28.0 101.0 %front.1 = (bf16[512,512]{1,0:T(8,128)(2,1)}, bf16[512,512]{1,0:T(8,128)(2,1)}, bf16[512,512]{1,0:T(8,128)(2,1)}, bf16[512,512]{1,0:T(8,128)(2,1)}, bf16[512,256...) custom-call(bf16[512,1024]{1,0:T(8,128)(2,1)} %x_ref.3, ...), custom_call_target="tpu_custom_call" | custom-call | flops 1000000000 | tf_op jit(solution)/shard_map/front/pallas_call | solution.py:1016
  129.0 123.4 %back.1 = (bf16[512,1024]{1,0:T(8,128)(2,1)}, bf16[512,1024]{1,0:T(8,128)(2,1)}, f32[11,64,768]{2,1,0:T(8,128)}, f32[24,128]{1,0:T(8,128)}, bf16[512,1024]{1,0:T(8,128)(2,1)}) custom-call(bf16[2,3,512,2304]{3,2,1,0:T(8,128)(2,1)} %get-tuple-element.57.refs_0_, bf16[2,1024,512]{2,1,0:T(8,128)(2,1)} %get-tuple-element.58.refs_1_, ...), custom_call_target="tpu_custom_call" | custom-call | flops 1000000000 | tf_op jit(solution)/shard_map/back/pallas_call | solution.py:648
  252.5 7.2 %finish.1 = (bf16[512,1024]{1,0:T(8,128)(2,1)}, f32[512,1024]{1,0:T(8,128)}, f32[64,512]{1,0:T(8,128)}, f32[64,2,256]{2,1,0:T(2,128)}, f32[64,512]{1,0:T(8,128)}...) custom-call(bf16[512,1024]{1,0:T(8,128)(2,1)} %get-tuple-element.56., ...), custom_call_target="tpu_custom_call" | custom-call | flops 60000000 | tf_op jit(solution)/shard_map/finish/pallas_call | solution.py:1079
  (6 shorter events, 0.0 us)
Async XLA Ops:
  0.6 8.1 %copy-start.1 = (bf16[1024,2,256]{2,1,0:T(2,128)(2,1)S(1)}, bf16[1024,2,256]{2,1,0:T(2,128)(2,1)}, u32[]{:S(2)}) copy-start(bf16[1024,2,256]{2,1,0:T(2,128)(2,1)} %param.16) | copy-start | bytes 3145732
  0.7 26.4 %collective-permute-start = (bf16[512,1024]{1,0:T(8,128)(2,1)}, bf16[512,1024]{1,0:T(8,128)(2,1)S(1)}, u32[]{:S(2)}, u32[]{:S(2)}) collective-permute-start(bf16[512,1024]{1,0:T(8,128)(2,1)} %x_ref.3), channel_id=1, source_target_pairs={{0,1},{1,0},{2,3},{3,2},{4,5},{5,4},{6,7},{7,6},{8,9},{9,8},{10,11... | collective-permute-start | bytes 3145736 | tf_op jit(solution)/shard_map/ppermute | solution.py:1098
  18.9 6.1 %copy-start.2 = (s32[1,1024]{1,0:T(1,128)S(1)}, s32[1,1024]{1,0:T(1,128)}, u32[]{:S(2)}) copy-start(s32[1,1024]{1,0:T(1,128)} %param.13) | copy-start | bytes 12292
  27.1 1.0 copy-start
